TPU v7x, 32 devices: a whole 2x2x4 slice. The times are simulated.
32 devices in a mesh: ctx: 8 (over z, y), fsdp: 4 (over x, core).
Axes of the slice: x: 2, y: 2, z: 4, core: 2. Of those that a mesh axis runs over, the one named last changes fastest.
Arguments:
- tokens: bfloat16 [8192, 1024], P(('fsdp', 'ctx')), may hold values from -6 to 6
- cotangent: bfloat16 [8192, 1024], P(('fsdp', 'ctx')), may hold values from -6 to 6
- gain_attn: bfloat16 [1024], P('fsdp'), may hold values from 0.5 to 1.5
- w_qkv: bfloat16 [1024, 3072], P('fsdp'), may hold values from -0.25 to 0.25
- w_out: bfloat16 [1024, 1024], P('fsdp'), may hold values from -0.75 to 0.75
- gain_ffn: bfloat16 [1024], P('fsdp'), may hold values from 0.5 to 1.5
- w_gate_up: bfloat16 [1024, 5632], P('fsdp'), may hold values from -0.1875 to 0.1875
- w_down: bfloat16 [2816, 1024], P('fsdp'), may hold values from -0.109375 to 0.109375
- lengths: int32 [4, 4], P('fsdp'), may hold values from 1 to 1024, 2048 in all within a row
- block_order: int32 [4, 32], P('fsdp'), may hold values from 0 to 31, each once within a row
Outputs:
- output: bfloat16 [8192, 1024], P(('fsdp', 'ctx'))
- grad_tokens: bfloat16 [8192, 1024], P(('fsdp', 'ctx'))
- grad_gain_attn: float32 [1024], P('fsdp')
- grad_w_qkv: float32 [1024, 3072], P('fsdp')
- grad_w_out: float32 [1024, 1024], P('fsdp')
- grad_gain_ffn: float32 [1024], P('fsdp')
- grad_w_gate_up: float32 [1024, 5632], P('fsdp')
- grad_w_down: float32 [2816, 1024], P('fsdp')
Inputs may be any that keep to these rules, and one draw needn't show every extreme that they name: Each row gives the lengths of the 4 sequences that fill one group's 2048 tokens, in sequence order; the longest is exactly 1024. `block_order`: each row is a permutation of the 32 blocks of one group.
All inputs are finite; a program needn't handle non-finite values.
Results may differ from a plain program's by a relative error of at most 0.024.
Values may be sent and summed in bfloat16 or wider, within the bound.
No kernel may reach another device: no remote copies, remote signals or barrier semaphores. Data moves between devices by JAX's collectives and lax.ppermute only.
A program may use at most 256 MiB of HBM per device.

v0:
```python
import functools
import math

import jax
import jax.numpy as jnp
from jax import lax
from jax.experimental import pallas as pl
from jax.experimental.pallas import tpu as pltpu
from jax.sharding import PartitionSpec as P

HEADS = 16
TILE = 256
VMEM_FWD = 26 << 20
VMEM_BWD = 34 << 20


EPS = 1e-05
MASKED=-1e30
def nt(a,b): return lax.dot_general(a,b,(((1,),(1,)),((),())),preferred_element_type=jnp.float32)
def nn(a,b): return lax.dot_general(a,b,(((1,),(0,)),((),())),preferred_element_type=jnp.float32)

def ends_of(lengths_ref):
    ends = [lengths_ref[0, 0]]
    for i in range(1, lengths_ref.shape[1]):
        ends.append(ends[-1] + lengths_ref[0, i])
    return ends

def first_tile(ends, position, tile):
    start = jnp.int32(0)
    for end in ends[:-1]:
        start = jnp.where(end <= position, end, start)
    return start // tile

def last_tile(ends, position, tile):
    last = ends[-1]
    for end in reversed(ends[:-1]):
        last = jnp.where(end > position, end, last)
    return (last - 1) // tile

def seen(ends, query_start, key_start, queries, keys):
    pos_query = query_start + lax.broadcasted_iota(jnp.int32, (1, queries), 1)
    start = jnp.zeros((1, queries), jnp.int32)
    for end in ends[:-1]:
        start = jnp.where(pos_query >= end, end, start)
    pos_key = key_start + lax.broadcasted_iota(jnp.int32, (keys, queries), 0)
    return (pos_key <= pos_query) & (pos_key >= start)

def head_lanes(x, head, heads, depth):
    if heads == 1:
        return x
    lane = lax.broadcasted_iota(jnp.int32, x.shape, 1)
    return jnp.where((lane >= head * depth) & (lane < (head + 1) * depth), x, jnp.zeros_like(x))

def placed(slots, block, table, order_ref, per):
    number = 0
    for slot in slots:
        for row in range(0, slot.shape[0], block):
            position = order_ref[0, table[0, number // per] * per + number % per] * block
            yield slot, pl.ds(row, block), pl.ds(pl.multiple_of(position, block), block)
            number += 1

def stored(owners, block, order_ref, per):
    for owner in range(owners):
        for b in range(per):
            position = order_ref[0, owner * per + b] * block
            yield owner, pl.ds(b * block, block), pl.ds(pl.multiple_of(position, block), block)

def fwd_kernel(meta, table, lengths_ref, order_ref, *refs):
    given, n, heads, depth, tile, block = meta
    qkv_refs, out_refs = refs[:given], refs[given:given+n]
    out_t_ref, lse_ref = refs[given+n], refs[given+n+1]
    q_ref, k_ref, v_ref, o_ref = refs[given+n+2:]
    ends = ends_of(lengths_ref)
    width = heads*depth
    scale = depth ** (-0.5)
    per = out_refs[0].shape[0] // block
    for slot, src, dst in placed(qkv_refs, block, table, order_ref, per):
        q = slot[src, 0:width].astype(jnp.float32)*scale
        for h in range(heads):
            q_ref[h, dst, :] = head_lanes(q, h, heads, depth).astype(jnp.bfloat16)
        k_ref[dst, :] = slot[src, width:2*width]
        v_ref[dst, :] = slot[src, 2*width:]
    wide_tile = 2 * tile
    tiles = q_ref.shape[1] // wide_tile
    def one_query(t, _):
        rows = pl.ds(pl.multiple_of(t*wide_tile, wide_tile), wide_tile)
        qs = [q_ref[h, rows, :] for h in range(heads)]
        def one_key(j, carry):
            keys = pl.ds(pl.multiple_of(j*tile, tile), tile)
            k = k_ref[keys, :]
            v_t = jnp.transpose(v_ref[keys, :].astype(jnp.float32)).astype(jnp.bfloat16)
            mask = seen(ends, t*wide_tile, j*tile, wide_tile, tile)
            new = []
            for h in range(heads):
                m, l, acc = carry[h]
                s = jnp.where(mask, nt(k, qs[h]), MASKED)
                m_new = jnp.maximum(m, jnp.max(s, axis=0, keepdims=True))
                e = jnp.exp(s - m_new)
                alpha = jnp.exp(m - m_new)
                l = l*alpha + jnp.sum(e, axis=0, keepdims=True)
                acc = acc*alpha + nn(v_t[h*depth:(h+1)*depth], e.astype(jnp.bfloat16))
                new.append((m_new, l, acc))
            return tuple(new)
        init = tuple((jnp.full((1,wide_tile),MASKED,jnp.float32), jnp.zeros((1,wide_tile),jnp.float32), jnp.zeros((depth,wide_tile),jnp.float32)) for _ in range(heads))
        final = lax.fori_loop(first_tile(ends, t*wide_tile, tile), 2*t+2, one_key, init)
        outs = []
        for h in range(heads):
            m, l, acc = final[h]
            outs.append(acc / l)
            lse_ref[h:h+1, rows] = m + jnp.log(l)
        out_t = jnp.concatenate(outs, axis=0) if heads > 1 else outs[0]
        out_t_ref[:, rows] = out_t
        o_ref[rows, :] = jnp.transpose(out_t).astype(jnp.bfloat16)
        return 0
    lax.fori_loop(0, tiles, one_query, 0)
    for slot, dst, src in placed(out_refs, block, table, order_ref, per):
        slot[dst, :] = o_ref[src, :]

def bwd_kernel(meta, table, lengths_ref, order_ref, *refs):
    given, n, heads, depth, tile, block = meta
    qkv_refs, grad_refs = refs[:given], refs[given:given+n]
    refs = refs[n:]
    part_out_ref, out_t_ref, lse_ref, dqkv_ref = refs[given:given+4]
    ends = ends_of(lengths_ref)
    q_ref, k_ref, v_ref, g_ref, k_t_ref, delta_ref, dq_t_ref, dq_ref, dk_ref, dv_ref = refs[given+4:]
    width = heads*depth
    scale = depth ** (-0.5)
    per = dqkv_ref.shape[1] // block
    total = k_ref.shape[0]
    for slot, src, dst in placed(qkv_refs, block, table, order_ref, per):
        q = slot[src, 0:width].astype(jnp.float32)*scale
        for h in range(heads):
            q_ref[h, dst, :] = head_lanes(q, h, heads, depth).astype(jnp.bfloat16)
        k_ref[dst, :] = slot[src, width:2*width]
        v_ref[dst, :] = slot[src, 2*width:]
    for slot, src, dst in placed(grad_refs, block, table, order_ref, per):
        g = slot[src, :].astype(jnp.float32)
        for h in range(heads):
            g_ref[h, dst, :] = head_lanes(g, h, heads, depth).astype(jnp.bfloat16)
    tiles = total // tile
    def prepare(t, _):
        rows = pl.ds(pl.multiple_of(t*tile, tile), tile)
        k_t_ref[:, rows] = jnp.transpose(k_ref[rows, :].astype(jnp.float32)).astype(jnp.bfloat16)
        g = g_ref[0, rows, :].astype(jnp.float32)
        for h in range(1, heads):
            g = g + g_ref[h, rows, :].astype(jnp.float32)
        prod = jnp.transpose(g) * out_t_ref[:, rows]
        for h in range(heads):
            delta_ref[h:h+1, rows] = jnp.sum(prod[h*depth:(h+1)*depth], axis=0, keepdims=True)
        dq_t_ref[:, rows] = jnp.zeros((width, tile), jnp.float32)
        return 0
    lax.fori_loop(0, tiles, prepare, 0)
    wide_tile = 2 * tile
    def one_key(j, _):
        keys = pl.ds(pl.multiple_of(j*tile, tile), tile)
        k = k_ref[keys, :]
        v = v_ref[keys, :]
        k_t = k_t_ref[:, keys]
        dk_ref[keys, :] = jnp.zeros((tile, width), jnp.float32)
        dv_ref[keys, :] = jnp.zeros((tile, width), jnp.float32)
        def one_query(t, _):
            rows = pl.ds(pl.multiple_of(t*wide_tile, wide_tile), wide_tile)
            mask = seen(ends, t*wide_tile, j*tile, wide_tile, tile)
            dk = dk_ref[keys, :]
            dv = dv_ref[keys, :]
            for h in range(heads):
                q = q_ref[h, rows, :]
                g = g_ref[h, rows, :]
                s = nt(k, q)
                p = jnp.where(mask, jnp.exp(s - lse_ref[h:h+1, rows]), 0.0)
                dp = nt(v, g)
                ds = (p*(dp - delta_ref[h:h+1, rows])).astype(jnp.bfloat16)
                dv = dv + nn(p.astype(jnp.bfloat16), g)
                dk = dk + nn(ds, q)
                part = pl.ds(h*depth, depth)
                dq_t_ref[part, rows] = dq_t_ref[part, rows] + nn(k_t[h*depth:(h+1)*depth], ds)
            dk_ref[keys, :] = dk
            dv_ref[keys, :] = dv
            return 0
        lax.fori_loop(j//2, last_tile(ends, j*tile + tile - 1, wide_tile) + 1, one_query, 0)
        return 0
    lax.fori_loop(0, tiles, one_key, 0)
    def finish(t, _):
        rows = pl.ds(pl.multiple_of(t*tile, tile), tile)
        dq_ref[rows, :] = (jnp.transpose(dq_t_ref[:, rows])*scale).astype(jnp.bfloat16)
        return 0
    lax.fori_loop(0, tiles, finish, 0)
    for owner, dst, src in stored(n, block, order_ref, per):
        dqkv_ref[owner, dst, 0:width] = dq_ref[src, :]
        dqkv_ref[owner, dst, width:2*width] = dk_ref[src, :].astype(jnp.bfloat16)
        dqkv_ref[owner, dst, 2*width:3*width] = dv_ref[src, :].astype(jnp.bfloat16)
    shard = part_out_ref.shape[1]
    rows = dqkv_ref.shape[1]
    for owner in range(n):
        dqkv_ref[owner, 0:shard, 3*width:] = part_out_ref[owner]
        if shard < rows:
            dqkv_ref[owner, shard:, 3*width:] = jnp.zeros((rows-shard, width), jnp.bfloat16)

SM=pl.BlockSpec(memory_space=pltpu.SMEM)
VM=pl.BlockSpec(memory_space=pltpu.VMEM)
def attention_forward(table, lengths, order, qkv, n, heads, depth, tile):
    total=sum(x.shape[0] for x in qkv); rows=total//n; width=heads*depth
    block=total//order.shape[1]
    meta=(len(qkv),n,heads,depth,tile,block)
    res=pl.pallas_call(functools.partial(fwd_kernel,meta),
        out_shape=[jax.ShapeDtypeStruct((rows,width),jnp.bfloat16)]*n+[jax.ShapeDtypeStruct((width,total),jnp.float32),jax.ShapeDtypeStruct((heads,total),jnp.float32)],
        in_specs=[SM,SM,SM]+[VM]*len(qkv), out_specs=[VM]*(n+2),
        scratch_shapes=[pltpu.VMEM((heads,total,width),jnp.bfloat16)]+[pltpu.VMEM((total,width),jnp.bfloat16)]*3,
        cost_estimate=cost(17),
        compiler_params=pltpu.CompilerParams(vmem_limit_bytes=VMEM_FWD),
        name="attention_forward")(table,lengths,order,*qkv)
    return list(res[:n]),res[n],res[n+1]
def attention_backward(table, lengths, order, qkv, grads, part_out, out_t, lse, heads, depth, tile):
    n=len(grads); rows=grads[0].shape[0]; total=n*rows; width=heads*depth
    block=total//order.shape[1]
    meta=(len(qkv),n,heads,depth,tile,block)
    f32=jnp.float32; b16=jnp.bfloat16
    return pl.pallas_call(functools.partial(bwd_kernel,meta),
        out_shape=jax.ShapeDtypeStruct((n,rows,4*width),b16),
        in_specs=[SM,SM,SM]+[VM]*(len(qkv)+n+3), out_specs=VM,
        scratch_shapes=[pltpu.VMEM((heads,total,width),b16),pltpu.VMEM((total,width),b16),pltpu.VMEM((total,width),b16),pltpu.VMEM((heads,total,width),b16),
          pltpu.VMEM((width,total),b16),pltpu.VMEM((heads,total),f32),pltpu.VMEM((width,total),f32),pltpu.VMEM((total,width),b16),pltpu.VMEM((total,width),f32),pltpu.VMEM((total,width),f32)],
        cost_estimate=cost(18),
        compiler_params=pltpu.CompilerParams(vmem_limit_bytes=VMEM_BWD),
        name="attention_backward")(table,lengths,order,*qkv,*grads,part_out,out_t,lse)


def tn(left, right):
    return lax.dot_general(left, right, (((0,), (0,)), ((), ())), preferred_element_type=jnp.float32)


def low(value):
    return value.astype(jnp.bfloat16)


def wide(value):
    return value.astype(jnp.float32)


def at(start, size):
    return pl.ds(pl.multiple_of(start, size), size)


def cost(microseconds):
    return pl.CostEstimate(flops=0, bytes_accessed=int(microseconds * 3.4e6), transcendentals=0)


def room(arrays, extra):
    total = 0
    for array in arrays:
        dims = [1, 1] + list(array.shape)
        rows, lanes = -(-dims[-2] // 16) * 16, -(-dims[-1] // 128) * 128
        total += math.prod(dims[:-2]) * rows * lanes * jnp.dtype(array.dtype).itemsize
    return pltpu.CompilerParams(vmem_limit_bytes=min(60 << 20, total + (extra << 20)))


def call(name, kernel, out, inputs, scratch=(), time=2.0, extra=8):
    return list(
        pl.pallas_call(
            kernel,
            out_shape=list(out),
            in_specs=[SM] + [VM] * (len(inputs) - 1),
            out_specs=[VM] * len(out),
            scratch_shapes=list(scratch),
            cost_estimate=cost(time),
            compiler_params=room(list(inputs[1:]) + list(out) + list(scratch), extra),
            name=name,
        )(*inputs)
    )


def shape(dims, dtype=jnp.bfloat16):
    return jax.ShapeDtypeStruct(tuple(dims), dtype)


def slice_kernel(own_width, table, w_ref, one_ref, two_ref, out_ref):
    shard, total = w_ref.shape
    for part in range(3):
        out_ref[0:shard, part * own_width : (part + 1) * own_width] = w_ref[
            :, at(part * (total // 3) + table[0, 0] * own_width, own_width)
        ]
    out_ref[shard : shard + 8, :] = gain_rows(wide(one_ref[...]), wide(two_ref[...]), 3 * own_width)


def gain_rows(one, two, lanes):
    shard = one.shape[1]
    if lanes > shard:
        rest = jnp.zeros((1, lanes - shard), jnp.float32)
        one, two = jnp.concatenate([one, rest], axis=1), jnp.concatenate([two, rest], axis=1)
    number = lax.broadcasted_iota(jnp.int32, (8, lanes), 0)
    return low(jnp.where(number == 0, one, jnp.where(number == 1, two, 0.0)))


def full_gain(table, n, pieces, row, gain_ref):
    shard = gain_ref.shape[1] // len(pieces)
    for slot, piece in enumerate(pieces):
        lines = wide(piece[pl.ds(piece.shape[0] - 8, 8), 0:shard])
        gain_ref[0:1, at(table[0, n + slot] * shard, shard)] = lines[row : row + 1]


def split_kernel(n, table, w_ref, *refs):
    outs, parts_ref = refs[:-1], refs[-1]
    count = len(outs)
    hidden = w_ref.shape[1] // (2 * count)
    for part in range(count):
        parts_ref[part, :, 0:hidden] = w_ref[:, part * hidden : (part + 1) * hidden]
        parts_ref[part, :, hidden:] = w_ref[:, (count + part) * hidden : (count + part + 1) * hidden]
    for slot in range(count):
        outs[slot][...] = parts_ref[table[0, n + slot]]


def project_kernel(n, table, rows_ref, *refs):
    pieces, attn_ref, qkv_ref, gain_ref, weight_ref = refs[:-4], refs[-4], refs[-3], refs[-2], refs[-1]
    shard = rows_ref.shape[1] // len(pieces)
    full_gain(table, n, pieces, 0, gain_ref)
    for slot, piece in enumerate(pieces):
        weight_ref[at(table[0, n + slot] * shard, shard), :] = piece[pl.ds(0, shard), :]
    value = wide(rows_ref[...])
    inverse = lax.rsqrt(jnp.mean(value * value, axis=1, keepdims=True) + EPS)
    attn_in = low(value * inverse * gain_ref[0:1, :])
    attn_ref[...] = attn_in
    qkv_ref[...] = low(nn(attn_in, weight_ref[...]))


def stage_rows(table, n, pieces, weight_ref):
    shard = pieces[0].shape[0]
    for slot, piece in enumerate(pieces):
        weight_ref[at(table[0, n + slot] * shard, shard), :] = piece[...]


def leave_kernel(n, count, table, tokens_ref, *refs):
    parts, outs, slices = refs[:n], refs[n : n + count], refs[n + count : n + 2 * count]
    resid_ref, ffn_ref, gain_ref, weight_ref = refs[n + 2 * count :]
    own_width = parts[0].shape[1]
    full_gain(table, n, slices, 1, gain_ref)
    stage_rows(table, n, outs, weight_ref)
    rows = tokens_ref.shape[0]
    attn = jnp.concatenate([parts[k][...] for k in range(n)], axis=1)
    ordered = jnp.concatenate([weight_ref[at(table[0, k] * own_width, own_width), :] for k in range(n)], axis=0)
    resid = wide(tokens_ref[...]) + nn(attn, ordered)
    resid_ref[...] = resid
    inverse = lax.rsqrt(jnp.mean(resid * resid, axis=1, keepdims=True) + EPS)
    ffn_ref[...] = low(resid * inverse * gain_ref[0:1, :])


def ffn_kernel(n, count, slots, table, *refs):
    ffn, cot = refs[:slots], refs[slots : 2 * slots]
    pieces, down_ref = refs[2 * slots : 2 * slots + count], refs[2 * slots + count]
    rest = refs[2 * slots + count + 1 :]
    terms, outs, hidden_ref, grad_ref = rest[:slots], rest[slots : 2 * slots], rest[2 * slots], rest[2 * slots + 1]
    gate_ref, up_ref, values_ref, cots_ref = rest[2 * slots + 2 :]
    hidden = down_ref.shape[0]
    shard = pieces[0].shape[0]
    rows = ffn[0].shape[0]
    for slot, piece in enumerate(pieces):
        place = at(table[0, n + slot] * shard, shard)
        gate_ref[place, :] = piece[:, 0:hidden]
        up_ref[place, :] = piece[:, hidden:]
    for slot in range(slots):
        values_ref[slot] = ffn[slot][...]
        cots_ref[slot] = cot[slot][...]

    def one(number, unused):
        value = values_ref[number]
        gate = nn(value, gate_ref[...])
        upward = nn(value, up_ref[...])
        grad_hidden = nt(cots_ref[number], down_ref[...])
        sigma = jax.nn.sigmoid(gate)
        active = gate * sigma
        hidden_low = low(active * upward)
        grad_gate = low(grad_hidden * upward * (sigma + active * (1.0 - sigma)))
        grad_up = low(grad_hidden * active)
        place = at(number * rows, rows)
        hidden_ref[place, :] = hidden_low
        grad_ref[place, 0:hidden] = grad_gate
        grad_ref[place, hidden:] = grad_up
        values_ref[number] = low(nt(grad_gate, gate_ref[...]) + nt(grad_up, up_ref[...]))
        cots_ref[number] = low(nn(hidden_low, down_ref[...]))
        return 0

    lax.fori_loop(0, slots, one, 0)
    for slot in range(slots):
        terms[slot][...] = values_ref[slot]
        outs[slot][...] = cots_ref[slot]


def ffn_weight_kernel(n, count, table, *refs):
    ffn, cot, rest = refs[:count], refs[count : 2 * count], refs[2 * count :]
    hiddens, grads, rest = rest[: count // 2], rest[count // 2 : count], rest[count:]
    outs, (value_ref, turned_ref) = rest[:-2], rest[-2:]
    hidden = hiddens[0].shape[1]
    half = n // 2
    shard = ffn[0].shape[1] // count
    sub = shard // n
    lines = count * sub
    cut = outs[half].shape[0]
    hidden_all = jnp.concatenate([r[...] for r in hiddens], axis=0)
    grad_all = jnp.concatenate([r[...] for r in grads], axis=0)

    def one(f, unused):
        lanes = at(f * shard, shard)
        ffn_all = jnp.concatenate([r[:, lanes] for r in ffn], axis=0)
        value_ref[f] = low(tn(ffn_all, grad_all))
        cot_all = jnp.concatenate([r[:, lanes] for r in cot], axis=0)
        turned_ref[f] = low(tn(cot_all, hidden_all))
        return 0

    lax.fori_loop(0, count, one, 0)

    def store(slot, row, lanes, value):
        if slot != half:
            outs[slot if slot < half else slot + 1][row : row + sub, lanes] = value
        elif row < cut:
            outs[half][row : row + sub, lanes] = value
        else:
            outs[half + 1][row - cut : row - cut + sub, lanes] = value

    for f in range(count):
        side, line = f // (count // 2), lines + (f % (count // 2)) * sub
        for slot in range(n):
            mine = at(table[0, slot] * sub, sub)
            store(slot, f * sub, slice(0, 2 * hidden), value_ref[f, mine, :])
            store(slot, line, slice(side * hidden, (side + 1) * hidden), turned_ref[f, mine, :])


def branch_kernel(n, count, got, table, resid_ref, cot_ref, *refs):
    terms, outs, slices = refs[:got], refs[got : got + count], refs[got + count : got + 2 * count]
    rest = refs[got + 2 * count :]
    grad_ref, branch_ref, parts = rest[0], rest[1], rest[2 : 2 + n]
    gain_ref, weight_ref = rest[2 + n :]
    own_width = parts[0].shape[1]
    full_gain(table, n, slices, 1, gain_ref)
    stage_rows(table, n, outs, weight_ref)
    resid = resid_ref[...]
    inverse = lax.rsqrt(jnp.mean(resid * resid, axis=1, keepdims=True) + EPS)
    normed = resid * inverse
    grad = wide(terms[0][...])
    for term in terms[1:]:
        grad = grad + wide(term[...])
    scaled = grad * gain_ref[0:1, :]
    inner = jnp.mean(scaled * normed, axis=1, keepdims=True)
    grad_resid = wide(cot_ref[...]) + inverse * (scaled - normed * inner)
    grad_ref[...] = grad_resid
    branch = low(grad_resid)
    branch_ref[...] = branch
    for k in range(n):
        parts[k][...] = low(nt(branch, weight_ref[at(table[0, k] * own_width, own_width), :]))


def out_weight_kernel(n, count, table, branch_ref, *refs):
    parts, outs, whole_ref = refs[:n], refs[n : n + count], refs[-1]
    own_width = parts[0].shape[1]
    shard = outs[0].shape[1]
    branch = branch_ref[...]
    for k in range(n):
        whole_ref[at(table[0, k] * own_width, own_width), :] = low(tn(parts[k][...], branch))
    for slot in range(count):
        lines = whole_ref[at(table[0, n + slot] * shard, shard), :]
        for owner in range(n):
            outs[slot][owner] = lines[:, owner * own_width : (owner + 1) * own_width]


def qkv_weight_kernel(given, n, count, table, *refs):
    attn, grads_ref, outs, whole_ref = refs[:given], refs[given], refs[given + 1 : -1], refs[-1]
    shard = outs[0].shape[0]
    used = outs[0].shape[1]
    grad_all = jnp.concatenate([grads_ref[table[0, k], :, 0:used] for k in range(n)], axis=0)

    def one(f, unused):
        attn_all = jnp.concatenate([r[:, at(f * shard, shard)] for r in attn], axis=0)
        whole_ref[f] = low(tn(attn_all, grad_all))
        return 0

    lax.fori_loop(0, count, one, 0)
    for slot in range(count):
        outs[slot][...] = whole_ref[table[0, n + slot]]


def tail_kernel(n, count, table, tokens_ref, grad_ref, parts_ref, *refs):
    weights, slices = refs[:count], refs[count : 2 * count]
    out_ref, gain_ref, sum_ref, grads_ref = refs[2 * count :]
    own_width = parts_ref.shape[2] // 4
    width = tokens_ref.shape[1]
    shard = width // count
    full_gain(table, n, slices, 0, gain_ref)
    for owner in range(n):
        for part in range(3):
            start = part * width + owner * own_width
            grads_ref[:, start : start + own_width] = parts_ref[owner, :, part * own_width : (part + 1) * own_width]
    sum_ref[...] = jnp.zeros_like(sum_ref)

    def one(part, unused):
        lanes = at(part * width, width)
        for slot in range(count):
            place = at(table[0, n + slot] * shard, shard)
            sum_ref[:, place] += nt(grads_ref[:, lanes], weights[slot][:, lanes])
        return 0

    lax.fori_loop(0, 3, one, 0)
    value = wide(tokens_ref[...])
    inverse = lax.rsqrt(jnp.mean(value * value, axis=1, keepdims=True) + EPS)
    normed = value * inverse
    scaled = sum_ref[...] * gain_ref[0:1, :]
    inner = jnp.mean(scaled * normed, axis=1, keepdims=True)
    out_ref[...] = low(grad_ref[...] + inverse * (scaled - normed * inner))


def row_sums(product):
    rows, lanes = product.shape
    total = product[:, 0:128]
    for i in range(1, lanes // 128):
        total = total + product[:, i * 128 : (i + 1) * 128]
    return jnp.sum(jnp.transpose(total), axis=0, keepdims=True)


def final_kernel(n, count, factor, aligned, table, gate_up_ref, gain_two_ref, w_qkv_ref, gain_one_ref, *refs):
    pieces, others = refs[: n + 1], refs[n + 1 : 2 * n + 2]
    outs, gain_outs, whole, sem = refs[2 * n + 2 : 2 * n + 6], refs[2 * n + 6 : 2 * n + 8], refs[2 * n + 8 : -1], refs[-1]
    gu_ref, down_ref, qkv_ref, out_ref, turned_ref, pieces_ref, others_ref = whole
    hidden, width = down_ref.shape
    sub = gu_ref.shape[0] // n
    own_width = others[0].shape[1] // 4
    half = n // 2
    copies = []

    def leave(number):
        copy = pltpu.make_async_copy(whole[number], outs[number], sem.at[number])
        copy.start()
        copies.append(copy)

    def stack(parts, whole_ref):
        for number, part in enumerate(parts):
            k = number if number <= half else number - 1
            row = parts[half].shape[0] if number == half + 1 else 0
            whole_ref[k, row : row + part.shape[0], :] = part[...]

    stack(pieces, pieces_ref)
    stack(others, others_ref)

    def one(k, unused):
        start = table[0, k] * sub
        for part in range(count):
            lines = wide(pieces_ref[k, part * sub : (part + 1) * sub, :]) * factor
            gu_ref[at(start, sub), part * hidden : (part + 1) * hidden] = lines[:, 0:hidden]
            gu_ref[at(start, sub), (count + part) * hidden : (count + part + 1) * hidden] = lines[:, hidden:]
            side, line = part // (count // 2), (count + part % (count // 2)) * sub
            turned = wide(pieces_ref[k, line : line + sub, :])[:, side * hidden : (side + 1) * hidden] * factor
            turned_ref[at(part * (n * sub) + start, sub), :] = turned
        return 0

    lax.fori_loop(0, n, one, 0)
    leave(0)

    def other(k, owner):
        for part in range(4):
            value = wide(others_ref[k, :, part * own_width : (part + 1) * own_width]) * factor
            target = out_ref if part == 3 else qkv_ref
            base = 0 if part == 3 else part * width
            if aligned:
                target[:, at(base + owner * own_width, own_width)] = value
            else:
                target[:, base + k * own_width : base + (k + 1) * own_width] = value
        return 0

    if aligned:
        lax.fori_loop(0, n, lambda k, unused: other(k, table[0, k]), 0)
    else:
        for k in range(n):
            other(k, None)
    leave(2)
    leave(3)
    for i in range(width // 128):
        down_ref[:, i * 128 : (i + 1) * 128] = jnp.transpose(turned_ref[i * 128 : (i + 1) * 128, :])
    leave(1)
    gain_outs[0][...] = row_sums(wide(gate_up_ref[...]) * gu_ref[...]) / wide(gain_two_ref[...])
    gain_outs[1][...] = row_sums(wide(w_qkv_ref[...]) * qkv_ref[...]) / wide(gain_one_ref[...])
    for copy in copies:
        copy.wait()


def cut_kernel(n, table, own_ref, up_ref, down_ref, *refs):
    outs, rest_ref, sum_ref = refs[:-2], refs[-2], refs[-1]
    sum_ref[...] = low(wide(own_ref[...]) + wide(up_ref[...]) + wide(down_ref[...]))
    sub = outs[0].shape[0]
    for slot, out in enumerate(outs):
        out[...] = sum_ref[at(table[0, n + slot] * sub, sub), :]
    rest_ref[...] = sum_ref[len(outs) * sub :, :]


def pack_kernel(n, table, rest_ref, *refs):
    pieces, out_ref = refs[:-1], refs[-1]
    sub = pieces[0].shape[0]
    for slot, piece in enumerate(pieces):
        out_ref[at(table[0, n + slot] * sub, sub), :] = piece[...]
    out_ref[len(pieces) * sub :, :] = rest_ref[...]


def join_kernel(terms, table, *refs):
    qkv, back_ref, out_ref = refs[:terms], refs[terms], refs[-1]
    total = wide(qkv[0][...])
    for term in qkv[1:]:
        total = total + wide(term[...])
    start = total.shape[1]
    out_ref[:, 0:start] = low(total)
    shard = out_ref.shape[0]
    other = wide(back_ref[0, 0:shard, start:])
    for owner in range(1, back_ref.shape[0]):
        other = other + wide(back_ref[owner, 0:shard, start:])
    out_ref[:, start:] = low(other)


def ring_of(count):
    if count % 4 or count < 8:
        return list(range(count))
    across = count // 4
    order = []
    for along in range(4):
        columns = range(1, across) if along % 2 == 0 else range(across - 1, 0, -1)
        order += [along * across + column for column in columns]
    return order + [along * across for along in reversed(range(4))]


def ring_shift(value, ring, step):
    count = len(ring)
    return lax.ppermute(
        value, "ctx", [(ring[i], ring[(i + step) % count]) for i in range(count)]
    )


def tie(*values):
    return lax.optimization_barrier(values)


class Gather:
    def __init__(self, value, ring):
        self.ring, self.half, self.step = ring, len(ring) // 2, 1
        self.first, self.ahead, self.behind, self.far = value, [], [], None
        self.up, self.down = tie(ring_shift(value, ring, 1), ring_shift(value, ring, -1))

    def advance(self, *others):
        self.ahead.append(self.down)
        self.behind.append(self.up)
        self.up, self.down, *others = tie(self.up, self.down, *others)
        self.step += 1
        up, down = self.up, self.down
        if self.step == self.half:
            cut = up.shape[0] // 2
            up, down = up[:cut], down[cut:]
        self.up, self.down = tie(ring_shift(up, self.ring, 1), ring_shift(down, self.ring, -1))
        return others

    def slots(self):
        while self.step < self.half:
            self.advance()
        return [self.first] + self.ahead + [self.up, self.down] + self.behind[::-1]


class Scatter:
    def __init__(self, terms, ring):
        self.ring, self.half, self.terms = ring, len(ring) // 2, terms
        self.up, self.down = terms[self.half : self.half + 2]
        self.step = self.half
        self.send()

    def send(self):
        self.up, self.down = tie(ring_shift(self.up, self.ring, 1), ring_shift(self.down, self.ring, -1))

    def advance(self, *others):
        self.up, self.down, *others = tie(self.up, self.down, *others)
        up, down, cut = self.terms[self.step - 1], self.terms[len(self.ring) + 2 - self.step], self.up.shape[0]
        if self.step == self.half:
            rows = up.shape[0]
            self.up = low(wide(up) + jnp.pad(wide(self.up), ((0, rows - cut), (0, 0))))
            self.down = low(wide(down) + jnp.pad(wide(self.down), ((rows - cut, 0), (0, 0))))
        else:
            self.up, self.down = add_low(up, self.up), add_low(down, self.down)
        self.up, self.down, *others = tie(self.up, self.down, *others)
        self.step -= 1
        self.send()
        return others

    def sums(self):
        while self.step > 1:
            self.advance()
        return [self.terms[0], self.up, self.down]


def ring_exchange(slots, ring):
    count = len(ring)
    result = [slots[0]] + [None] * (count - 1)
    for k in range(1, count):
        result[count - k] = ring_shift(slots[k], ring, k)
    return result


def exchange(array):
    return lax.all_to_all(array, "ctx", 0, 0, tiled=True)


def partner(value, count):
    return lax.ppermute(value, "fsdp", [(i, i ^ 1) for i in range(count)])


def chip_shift(value, count, step):
    return lax.ppermute(value, "fsdp", [(i, (i + 2 * step) % count) for i in range(count)])


def far_gather(value, count):
    return [value] + [chip_shift(value, count, -step) for step in range(1, count // 2)]


def near_gather(nears, count):
    slots = []
    for near in nears:
        slots += [near, partner(near, count)]
    return slots


def near_scatter(terms, count):
    return [add_low(terms[i], partner(terms[i + 1], count)) for i in range(0, count, 2)]


def far_scatter(nears, count):
    return [nears[0]] + [chip_shift(nears[step], count, step) for step in range(1, count // 2)]


def side_exchange(pieces, count, slots=None):
    chips = count // 2
    received = []
    for slot in range(count) if slots is None else slots:
        step, flip = (chips - slot // 2) % chips, slot % 2
        piece = pieces[2 * step + flip]
        if step or flip:
            pairs = [(i, ((i + 2 * step) % count) ^ flip) for i in range(count)]
            piece = lax.ppermute(piece, "fsdp", pairs)
        received.append(piece)
    return received


def add_low(left, right):
    return low(wide(left) + wide(right))


def total_of(terms):
    total = wide(terms[0])
    for term in terms[1:]:
        total = total + wide(term)
    return total


def body(
    tokens, cotangent, gain_attn, w_qkv, w_out, gain_ffn, w_gate_up, w_down, lengths, block_order
):
    rows, width = tokens.shape
    heads = HEADS
    depth = width // heads
    ctx = lax.axis_size("ctx")
    fsdp = lax.axis_size("fsdp")
    factor = 1.0 / math.sqrt(rows * ctx * fsdp)
    shard = width // fsdp
    hidden = w_down.shape[0]
    own_heads = heads // ctx
    own_width = own_heads * depth
    aligned = own_width % 128 == 0
    half = ctx // 2
    sub = shard // ctx
    lines = fsdp * sub
    ring = ring_of(ctx)
    chips = fsdp // 2
    entries = []
    for c in range(ctx):
        me = ring.index(c)
        for f in range(fsdp):
            owners = [ring[(me + k) % ctx] for k in range(ctx)]
            sides = [((f // 2 + s) % chips) * 2 + ((f % 2) ^ k) for s in range(chips) for k in (0, 1)]
            entries.append(owners + sides)
    device = lax.axis_index("ctx") * fsdp + lax.axis_index("fsdp")
    table = lax.dynamic_slice_in_dim(jnp.asarray(entries, jnp.int32), device, 1, 0)
    gain_one, gain_two = gain_attn.reshape(1, shard), gain_ffn.reshape(1, shard)
    f32 = jnp.float32
    gain_scratch = pltpu.VMEM((8, width), f32)
    square_scratch = pltpu.VMEM((width, width), jnp.bfloat16)

    going = Gather(tokens, ring)
    if aligned:
        (piece,) = call(
            "slice", functools.partial(slice_kernel, own_width),
            [shape((shard + 8, 3 * own_width))], [table, w_qkv, gain_one, gain_two],
            time=2.2,
        )
    else:
        mine = [
            lax.dynamic_slice(w_qkv, (0, part * width + table[0, 0] * own_width), (shard, own_width))
            for part in range(3)
        ]
        piece = jnp.concatenate(
            [jnp.concatenate(mine, axis=1), gain_rows(wide(gain_one), wide(gain_two), 3 * own_width)], axis=0
        )
    slices = far_gather(piece, fsdp)
    gate_pieces = call(
        "split", functools.partial(split_kernel, ctx),
        [shape((shard, 2 * hidden))] * fsdp, [table, w_gate_up],
        scratch=[pltpu.VMEM((fsdp, shard, 2 * hidden), jnp.bfloat16)],
        time=4,
    )
    sent = gate_pieces
    gate_pieces = [sent[0]] + side_exchange(sent, fsdp, range(1, 3)) + [None] * (fsdp - 3)
    slices, sent = going.advance(slices, sent)
    slices = near_gather(slices, fsdp)

    def project(slot):
        return call(
            "project", functools.partial(project_kernel, ctx),
            [shape(slot.shape), shape((slot.shape[0], 3 * own_width))], [table, slot] + slices,
            scratch=[gain_scratch, pltpu.VMEM((width, 3 * own_width), jnp.bfloat16)],
            time=2.6,
        )

    first = project(tokens)
    ahead, behind = [project(going.ahead[0])], [project(going.behind[0])]
    first, ahead[0], behind[0], gate_pieces[1:3] = going.advance(first, ahead[0], behind[0], gate_pieces[1:3])
    for step in range(1, half - 1):
        ahead.append(project(going.ahead[step]))
        behind.append(project(going.behind[step]))
        if step == 1:
            sent, unused = tie(sent, gate_pieces[1:3])
            gate_pieces[3:] = side_exchange(sent, fsdp, range(3, fsdp))
        if going.step < half:
            ahead[step], behind[step] = going.advance(ahead[step], behind[step])
    *far, ahead, behind, gate_pieces[3:] = tie(going.up, going.down, ahead, behind, gate_pieces[3:])
    far = [project(value) for value in far]
    later_out, far = tie(w_out, far)
    outs = far_gather(later_out, fsdp)
    pairs = [first] + ahead + far + behind[::-1]
    attn_slots, qkv = [pair[0] for pair in pairs], [pair[1] for pair in pairs]

    out_slots, out_t, log_total = attention_forward(
        table, lengths, block_order, qkv, ctx, own_heads, depth, TILE
    )
    out_slots, outs, gate_pieces = tie(out_slots, outs, gate_pieces)
    later_cot, out_slots = tie(cotangent, out_slots)
    cots = far_gather(later_cot, fsdp)
    attn_parts = ring_exchange(out_slots, ring)
    outs = near_gather(outs, fsdp)
    attn_parts, outs, cots = tie(attn_parts, outs, cots)
    cots = near_gather(cots, fsdp)
    resid, ffn_in = call(
        "leave", functools.partial(leave_kernel, ctx, fsdp),
        [shape((rows, width), f32), shape((rows, width))],
        [table, tokens] + attn_parts + outs + slices,
        scratch=[gain_scratch, square_scratch],
        time=4.1,
    )

    nears = far_gather(ffn_in, fsdp)
    ffns, grad_terms, out_terms, hiddens, grads = [], [], [], [], []
    for chip in range(chips):
        ffn_pair = [nears[chip], partner(nears[chip], fsdp)]
        result = call(
            "feed_forward", functools.partial(ffn_kernel, ctx, fsdp, 2),
            [shape((rows, width))] * 4 + [shape((2 * rows, hidden)), shape((2 * rows, 2 * hidden))],
            [table] + ffn_pair + cots[2 * chip : 2 * chip + 2] + gate_pieces + [w_down],
            scratch=[pltpu.VMEM((width, hidden), jnp.bfloat16)] * 2 + [pltpu.VMEM((2, rows, width), jnp.bfloat16)] * 2,
            time=9.5,
        )
        if chip == 0:
            result, nears[1:] = tie(result, nears[1:])
        ffns += ffn_pair
        grad_terms += result[0:2]
        out_terms += result[2:4]
        hiddens.append(result[4])
        grads.append(result[5])
    grad_nears = near_scatter(grad_terms, fsdp)
    hiddens, grad_nears = tie(hiddens, grad_nears)
    grad_parts = far_scatter(grad_nears, fsdp)
    terms_ffn = call(
        "feed_forward_weights", functools.partial(ffn_weight_kernel, ctx, fsdp),
        [shape((lines + lines // 2, 2 * hidden))] * half
        + [shape(((lines + lines // 2) // 2, 2 * hidden))] * 2
        + [shape((lines + lines // 2, 2 * hidden))] * (half - 1),
        [table] + ffns + cots + hiddens + grads,
        scratch=[pltpu.VMEM((fsdp, shard, 2 * hidden), jnp.bfloat16), pltpu.VMEM((fsdp, shard, hidden), jnp.bfloat16)],
        time=12,
    )
    grad_parts, unused = tie(grad_parts, terms_ffn[0])
    ffn_sums = Scatter(terms_ffn, ring)
    grad_resid, branch, *grad_attn = call(
        "branch", functools.partial(branch_kernel, ctx, fsdp, len(grad_parts)),
        [shape((rows, width), f32), shape((rows, width))] + [shape((rows, own_width))] * ctx,
        [table, resid, cotangent] + grad_parts + outs + slices,
        scratch=[gain_scratch, square_scratch],
        time=5,
    )
    grad_attn, branch, ffn_sums.up, ffn_sums.down = tie(grad_attn, branch, ffn_sums.up, ffn_sums.down)
    grad_slots = ring_exchange(grad_attn, ring)
    out_sides = call(
        "out_weights", functools.partial(out_weight_kernel, ctx, fsdp),
        [shape((ctx, shard, own_width))] * fsdp, [table, branch] + attn_parts,
        scratch=[square_scratch],
        time=3.3,
    )
    out_nears = near_scatter(out_sides, fsdp)

    out_parts = far_scatter(out_nears, fsdp)
    part_out = low(total_of(out_parts))
    grad_slots, part_out = ffn_sums.advance(grad_slots, part_out)
    grad_qkv = attention_backward(
        table, lengths, block_order, qkv, grad_slots, part_out, out_t, log_total, own_heads, depth, TILE
    )
    (grad_qkv,) = ffn_sums.advance(grad_qkv)
    qkv_sides = call(
        "qkv_weights", functools.partial(qkv_weight_kernel, len(attn_slots), ctx, fsdp),
        [shape((shard, 3 * own_width))] * fsdp, [table] + attn_slots + [grad_qkv],
        scratch=[pltpu.VMEM((fsdp, shard, 3 * own_width), jnp.bfloat16)],
        time=6,
    )
    if ffn_sums.step > 1:
        grad_qkv, qkv_sides = ffn_sums.advance(grad_qkv, qkv_sides)
    grad_back = exchange(grad_qkv)
    later_qkv, unused = tie(w_qkv, qkv_sides[0])
    qkv_nears = far_gather(later_qkv, fsdp)
    qkv_sum = far_scatter(near_scatter(qkv_sides, fsdp), fsdp)

    qkv_sum = ffn_sums.advance(qkv_sum)[0] if ffn_sums.step > 1 else qkv_sum
    own_sum, ffn_up, ffn_down = ffn_sums.sums()
    *gate_sides, rest = call(
        "cut", functools.partial(cut_kernel, ctx),
        [shape((sub, 2 * hidden))] * fsdp + [shape((lines // 2, 2 * hidden))],
        [table, own_sum, ffn_up, ffn_down],
        scratch=[pltpu.VMEM((lines + lines // 2, 2 * hidden), jnp.bfloat16)],
        time=3,
    )
    (joined,) = call(
        "join", functools.partial(join_kernel, len(qkv_sum)),
        [shape((shard, 4 * own_width))], [table] + qkv_sum + [grad_back],
        time=2.5,
    )
    gate_sides = side_exchange(gate_sides, fsdp)
    gate_sides, joined = tie(gate_sides, joined)
    (packed,) = call(
        "pack", functools.partial(pack_kernel, ctx),
        [shape((lines + lines // 2, 2 * hidden))], [table, rest] + gate_sides,
        time=2,
    )
    ffn_going = Gather(packed, ring)
    attn_going = Gather(joined, ring)
    weights = near_gather(qkv_nears, fsdp)
    (grad_tokens,) = call(
        "tail", functools.partial(tail_kernel, ctx, fsdp),
        [shape((rows, width))], [table, tokens, grad_resid, grad_back] + weights + slices,
        scratch=[gain_scratch, pltpu.VMEM((rows, width), f32), pltpu.VMEM((rows, 3 * width), jnp.bfloat16)],
        time=8,
    )
    ffn_going.advance()
    (grad_tokens,) = ffn_going.advance(grad_tokens)
    results = [
        shape((shard, 2 * hidden * fsdp), f32), shape((hidden, width), f32),
        shape((shard, 3 * width), f32), shape((shard, width), f32),
    ]
    inputs = [table, w_gate_up, gain_two, w_qkv if aligned else unmixed(relative(w_qkv, table, ctx), ctx, own_width), gain_one]
    inputs += ffn_going.slots() + attn_going.slots()
    scratch = [pltpu.VMEM(x.shape, f32) for x in results] + [pltpu.VMEM((width, hidden), f32)]
    scratch += [pltpu.VMEM((ctx,) + packed.shape, jnp.bfloat16), pltpu.VMEM((ctx,) + joined.shape, jnp.bfloat16)]
    *results, grad_gain_ffn, grad_gain_attn = pl.pallas_call(
        functools.partial(final_kernel, ctx, fsdp, factor, aligned),
        out_shape=results + [shape((1, shard), f32)] * 2,
        in_specs=[SM] + [VM] * (len(inputs) - 1),
        out_specs=[pl.BlockSpec(memory_space=pltpu.HBM)] * 4 + [VM] * 2,
        scratch_shapes=scratch + [pltpu.SemaphoreType.DMA((4,))],
        compiler_params=room(inputs[1:] + scratch, 8),
        cost_estimate=cost(6),
        name="final",
    )(*inputs)
    grad_w_gate_up, grad_w_down, grad_w_qkv, grad_w_out = results
    if not aligned:
        grad_w_qkv, grad_w_out = ordered(grad_w_qkv, table, 3, ctx), ordered(grad_w_out, table, 1, ctx)
    output = low(resid + total_of(far_scatter(near_scatter(out_terms, fsdp), fsdp)))
    return (
        output,
        grad_tokens,
        grad_gain_attn.reshape(shard),
        grad_w_qkv,
        grad_w_out,
        grad_gain_ffn.reshape(shard),
        grad_w_gate_up,
        grad_w_down,
    )


def relative(weight, table, ctx):
    rows = weight.shape[0]
    parts = weight.reshape(rows, 3, ctx, -1)
    slots = [lax.dynamic_index_in_dim(parts, table[0, k], 2, keepdims=False) for k in range(ctx)]
    return jnp.concatenate([slot.reshape(rows, -1) for slot in slots], axis=1)


def unmixed(weight, ctx, own_width):
    rows = weight.shape[0]
    return weight.reshape(rows, ctx, 3, own_width).transpose(0, 2, 1, 3).reshape(rows, -1)


def ordered(array, table, parts, ctx):
    rows = array.shape[0]
    split = array.reshape(rows, parts, ctx, -1)
    result = jnp.zeros_like(split)
    for k in range(ctx):
        result = lax.dynamic_update_slice(result, split[:, :, k : k + 1], (0, 0, table[0, k], 0))
    return result.reshape(rows, -1)


def solution(mesh):
    in_specs = (
        P(("fsdp", "ctx"), None),
        P(("fsdp", "ctx"), None),
        P("fsdp"),
        P("fsdp", None),
        P("fsdp", None),
        P("fsdp"),
        P("fsdp", None),
        P("fsdp", None),
        P("fsdp", None),
        P("fsdp", None),
    )
    out_specs = (
        P(("fsdp", "ctx"), None),
        P(("fsdp", "ctx"), None),
        P("fsdp"),
        P("fsdp", None),
        P("fsdp", None),
        P("fsdp"),
        P("fsdp", None),
        P("fsdp", None),
    )
    return jax.shard_map(body, mesh=mesh, in_specs=in_specs, out_specs=out_specs, check_vma=False)
```

profile of v0, /device:TPU:0, one launch (start us, length us, event | category | flops | bytes accessed | tf_op | source)
XLA Modules:
  0.0 360.0 jit_solution(11440386447626995381)
XLA Ops:
  0.6 3.1 collective-permute-start.1
  7.7 2.0 collective-permute-start.2
  13.0 2.8 collective-permute-done.1.rows_ref
  25.7 4.1 %collective-permute-done.3.rows_ref = bf16[256,1024]{1,0:T(8,128)(2,1)S(1)} collective-permute-done((bf16[256,1024]{1,0:T(8,128)(2,1)S(1)}, bf16[256,1024]{1,0:T(8,128)(2,1)S(1)}, u32[]{:S(2)}, u32[]{:S(2)}) %collective-permute-start.3) | collective-permute-done | bytes 524320 | tf_op jit(solution)/shard_map/ppermute | solution.py:625
  35.8 9.2 %collective-permute-done.9.rows_ref = bf16[256,1024]{1,0:T(8,128)(2,1)S(1)} collective-permute-done((bf16[256,1024]{1,0:T(8,128)(2,1)S(1)}, bf16[256,1024]{1,0:T(8,128)(2,1)S(1)}, u32[]{:S(2)}, u32[]{:S(2)}) %collective-permute-start.9) | collective-permute-done | bytes 524320 | tf_op jit(solution)/shard_map/ppermute | solution.py:625
  50.6 2.3 collective-permute-done.12.rows_ref
  55.9 11.1 %attention_forward.1 = (bf16[256,128]{1,0:T(8,128)(2,1)S(1)}, bf16[256,128]{1,0:T(8,128)(2,1)S(1)}, bf16[256,128]{1,0:T(8,128)(2,1)S(1)}, bf16[256,128]{1,0:T(8,...) custom-call(s32[1,12]{1,0:T(1,128)S(1)} %constant_dynamic-slice_fusi, ...), custom_call_target="tpu_custom_call" | custom-call | bytes 57800000 | tf_op jit(solution)/shard_map/attention_forward/pallas_call | solution.py:205
  67.0 5.9 %collective-permute-start.24 = (bf16[256,1024]{1,0:T(8,128)(2,1)S(1)}, bf16[256,1024]{1,0:T(8,128)(2,1)S(1)}, u32[]{:S(2)}, u32[]{:S(2)}) collective-permute-start(bf16[256,1024]{1,0:T(8,128)(2,1)S(1)} %copy-done.6), channel_id=1, source_target_pairs={{0,2},{1,3},{2,0},{3,1},{4,6},{5,7},{6,4},{7,5},{8,10},{9,11},{10,... | collective-permute-start | bytes 1572872 | tf_op jit(solution)/shard_map/ppermute | solution.py:705
  75.0 2.5 collective-permute-start.16
  77.7 4.3 %collective-permute-start.17 = (bf16[256,128]{1,0:T(8,128)(2,1)S(1)}, bf16[256,128]{1,0:T(8,128)(2,1)S(1)}, u32[]{:S(2)}, u32[]{:S(2)}) collective-permute-start(bf16[256,128]{1,0:T(8,128)(2,1)S(1)} %get-tuple-element.370), channel_id=1, source_target_pairs={{4,16},{12,8},{20,0},{28,4},{24,12},{16,20},{8,28},{0,24},{5,17},{... | collective-permute-start | bytes 196616 | tf_op jit(solution)/shard_map/ppermute | solution.py:625
  82.0 2.1 collective-permute-start.18
  85.8 3.4 collective-permute-done.18.refs_4_
  91.2 3.2 collective-permute-start.21
  100.3 7.4 %feed_forward.2 = (bf16[256,1024]{1,0:T(8,128)(2,1)S(1)}, bf16[256,1024]{1,0:T(8,128)(2,1)S(1)}, bf16[256,1024]{1,0:T(8,128)(2,1)S(1)}, bf16[256,1024]{1,0:T(8,1...) custom-call(s32[1,12]{1,0:T(1,128)S(1)} %constant_dynamic-slice_fusion.table, ...), custom_call_target="tpu_custom_call" | custom-call | bytes 32300000 | tf_op jit(solution)/shard_map/feed_forward/pallas_call | solution.py:259
  109.3 3.3 collective-permute-done.27.refs_0_.refs_2_
  114.6 7.4 %feed_forward.3 = (bf16[256,1024]{1,0:T(8,128)(2,1)S(1)}, bf16[256,1024]{1,0:T(8,128)(2,1)S(1)}, bf16[256,1024]{1,0:T(8,128)(2,1)S(1)}, bf16[256,1024]{1,0:T(8,1...) custom-call(s32[1,12]{1,0:T(1,128)S(1)} %constant_dynamic-slice_fusion.table, ...), custom_call_target="tpu_custom_call" | custom-call | bytes 32300000 | tf_op jit(solution)/shard_map/feed_forward/pallas_call | solution.py:259
  124.5 7.1 %feed_forward_weights.1 = (bf16[192,1408]{1,0:T(8,128)(2,1)S(1)}, bf16[192,1408]{1,0:T(8,128)(2,1)S(1)}, bf16[192,1408]{1,0:T(8,128)(2,1)S(1)}, bf16[192,1408]{1...) custom-call(s32[1,12]{1,0:T(1,128)S(1)} %constant_dynamic-slice_fusi, ...), custom_call_target="tpu_custom_call" | custom-call | bytes 40800000 | tf_op jit(solution)/shard_map/feed_forward_weights/pallas_call | solution.py:259
  131.6 2.2 collective-permute-start.36
  134.0 6.2 %collective-permute-done.36 = bf16[96,1408]{1,0:T(8,128)(2,1)S(1)} collective-permute-done((bf16[96,1408]{1,0:T(8,128)(2,1)S(1)}, bf16[96,1408]{1,0:T(8,128)(2,1)S(1)}, u32[]{:S(2)}, u32[]{:S(2)}) %collective-permute-start.36) | collective-permute-done | bytes 270368 | tf_op jit(solution)/shard_map/ppermute | solution.py:625
  141.8 2.4 branch.1
  150.1 2.8 collective-permute-start.39
  152.9 2.6 collective-permute-start.40
  155.5 2.5 collective-permute-start.41
  158.0 3.9 %collective-permute-start.42 = (bf16[256,128]{1,0:T(8,128)(2,1)S(1)}, bf16[256,128]{1,0:T(8,128)(2,1)S(1)}, u32[]{:S(2)}, u32[]{:S(2)}) collective-permute-start(bf16[256,128]{1,0:T(8,128)(2,1)S(1)} %get-tuple-element.447), channel_id=1, source_target_pairs={{4,28},{12,24},{20,16},{28,8},{24,0},{16,4},{8,12},{0,20},{5,29},{... | collective-permute-start | bytes 196616 | tf_op jit(solution)/shard_map/ppermute | solution.py:625
  162.0 2.7 collective-permute-start.43
  166.1 2.8 collective-permute-done.43.refs_15_
  168.9 2.6 collective-permute-done.44.refs_16_
  171.8 2.0 collective-permute-start.49
  173.7 14.6 %attention_backward.1.refs_9_ = bf16[8,256,512]{2,1,0:T(8,128)(2,1)} custom-call(s32[1,12]{1,0:T(1,128)S(1)} %constant_dynamic-slice_fusion.table, s32[1,4]{1,0:T(1,128)S(1)} %copy-done.26, s32[1,32]{1,0:T(1,128)S(1)} %copy-done.27, bf16[256,384]{1,0:T(8,128)(2,1)S(1)} %get-tuple-element.306.refs_0_, bf16[256,384]{1,0:T(8,128)(2,1)S(1)} %get-tuple-element.335.refs_1_, ...), custom_call_target="tpu_custom_call" | custom-call | bytes 61200000 | tf_op jit(solution)/shard_map/attention_backward/pallas_call | solution.py:218
  190.7 4.8 %qkv_weights.1 = (bf16[256,384]{1,0:T(8,128)(2,1)S(1)}, bf16[256,384]{1,0:T(8,128)(2,1)S(1)}, bf16[256,384]{1,0:T(8,128)(2,1)S(1)}, bf16[256,384]{1,0:T(8,128)(2,1)S(1)}) custom-call(s32[1,12]{1,0:T(1,128)S(1)} %constant_dynamic-slice_fusion.table, bf16[256,1024]{1,0:T(8,128)(2,1)S(1)} %get-tuple-element.491.refs_0_, ...), custom_call_target="tpu_custom_call" | custom-call | bytes 20400000 | tf_op jit(solution)/shard_map/qkv_weights/pallas_call | solution.py:259
  195.6 5.0 %collective-permute-done.50 = bf16[192,1408]{1,0:T(8,128)(2,1)S(1)} collective-permute-done((bf16[192,1408]{1,0:T(8,128)(2,1)S(1)}, bf16[192,1408]{1,0:T(8,128)(2,1)S(1)}, u32[]{:S(2)}, u32[]{:S(2)}) %collective-permute-start.50) | collective-permute-done | bytes 540704 | tf_op jit(solution)/shard_map/ppermute | solution.py:625
  200.5 2.6 collective-permute-done.51
  204.5 3.7 %all-to-all-start = ((bf16[8,256,512]{2,1,0:T(8,128)(2,1)}), bf16[8,256,512]{2,1,0:T(8,128)(2,1)S(1)}, u32[]{:S(2)}, u32[]{:S(2)}) async-start(bf16[8,256,512]{2,1,0:T(8,128)(2,1)} %attention_backward.1.refs_9_), calls=%async_computation | async-start | bytes 4194304 | tf_op jit(solution)/shard_map/all_to_all | solution.py:697
  208.2 2.0 collective-permute-start.52
  212.0 32.6 %collective-permute-done.65.refs_2_ = bf16[256,3072]{1,0:T(8,128)(2,1)} collective-permute-done((bf16[256,3072]{1,0:T(8,128)(2,1)}, bf16[256,3072]{1,0:T(8,128)(2,1)}, u32[]{:S(2)}, u32[]{:S(2)}) %collective-permute-start.65) | collective-permute-done | bytes 1572896 | tf_op jit(solution)/shard_map/ppermute | solution.py:705
  246.4 8.8 %collective-permute-done.53.down_ref = bf16[192,1408]{1,0:T(8,128)(2,1)S(1)} collective-permute-done((bf16[192,1408]{1,0:T(8,128)(2,1)}, bf16[192,1408]{1,0:T(8,128)(2,1)S(1)}, u32[]{:S(2)}, u32[]{:S(2)}) %collective-permute-start.53) | collective-permute-done | bytes 540704 | tf_op jit(solution)/shard_map/ppermute | solution.py:625
  266.6 15.0 %collective-permute-start.61 = (bf16[192,1408]{1,0:T(8,128)(2,1)S(1)}, bf16[192,1408]{1,0:T(8,128)(2,1)S(1)}, u32[]{:S(2)}, u32[]{:S(2)}) collective-permute-start(bf16[192,1408]{1,0:T(8,128)(2,1)S(1)} %pack.1.refs_0_), channel_id=1, source_target_pairs={{4,0},{12,4},{20,12},{28,20},{24,28},{16,24},{8,16},{0,8},{5,1},{1... | collective-permute-start | bytes 1622024 | tf_op jit(solution)/shard_map/ppermute | solution.py:625
  281.6 2.0 collective-permute-start.72
  283.6 10.6 %collective-permute-done.61.refs_1_ = bf16[192,1408]{1,0:T(8,128)(2,1)S(1)} collective-permute-done((bf16[192,1408]{1,0:T(8,128)(2,1)S(1)}, bf16[192,1408]{1,0:T(8,128)(2,1)S(1)}, u32[]{:S(2)}, u32[]{:S(2)}) %collective-permute-start.61) | collective-permute-done | bytes 540704 | tf_op jit(solution)/shard_map/ppermute | solution.py:625
  299.0 2.5 collective-permute-start.63
  301.5 2.4 collective-permute-done.71.refs_17_
  306.1 6.6 %tail.1 = bf16[256,1024]{1,0:T(8,128)(2,1)} custom-call(s32[1,12]{1,0:T(1,128)S(1)} %constant_dynamic-slice_fusion.table, bf16[256,1024]{1,0:T(8,128)(2,1)S(1)} %copy-done.5, f32[256,1024]{1,0:T(8,128)S(1)} %copy-done.11, bf16[8,256,512]{2,1,0:T(8,128)(2,1)S(1)} %all-to-all-done.refs_2_.parts_ref, bf16[256,3072]{1,0:T(8,128)(2,1)S(1)} %copy-done.1, ...), custom_call_target="tpu_custom_call" | custom-call | bytes 27200000 | tf_op jit(solution)/shard_map/tail/pallas_call | solution.py:259
  312.7 6.1 %collective-permute-done.73.refs_16_ = bf16[256,512]{1,0:T(8,128)(2,1)S(1)} collective-permute-done((bf16[256,512]{1,0:T(8,128)(2,1)S(1)}, bf16[256,512]{1,0:T(8,128)(2,1)S(1)}, u32[]{:S(2)}, u32[]{:S(2)}) %collective-permute-start.73) | collective-permute-done | bytes 262176 | tf_op jit(solution)/shard_map/ppermute | solution.py:625
  321.5 2.2 collective-permute-start.32
  323.7 4.6 %collective-permute-done.75.refs_15_ = bf16[256,512]{1,0:T(8,128)(2,1)S(1)} collective-permute-done((bf16[256,512]{1,0:T(8,128)(2,1)S(1)}, bf16[256,512]{1,0:T(8,128)(2,1)S(1)}, u32[]{:S(2)}, u32[]{:S(2)}) %collective-permute-start.75) | collective-permute-done | bytes 262176 | tf_op jit(solution)/shard_map/ppermute | solution.py:625
  330.0 10.1 %collective-permute-done.76.refs_12_ = bf16[256,512]{1,0:T(8,128)(2,1)S(1)} collective-permute-done((bf16[256,512]{1,0:T(8,128)(2,1)S(1)}, bf16[256,512]{1,0:T(8,128)(2,1)S(1)}, u32[]{:S(2)}, u32[]{:S(2)}) %collective-permute-start.76) | collective-permute-done | bytes 262176 | tf_op jit(solution)/shard_map/ppermute | solution.py:625
  347.4 2.9 collective-permute-done.70.refs_5_
  351.3 8.5 %final.1 = (f32[256,5632]{1,0:T(8,128)}, f32[704,1024]{1,0:T(8,128)}, f32[256,3072]{1,0:T(8,128)}, f32[256,1024]{1,0:T(8,128)}, f32[1,256]{1,0:T(1,128)}, /*index=5*/f32[1,256]{1,0:T(1,128)}) custom-call(s32[1,12]{1,0:T(1,128)S(1)} %constant_dynamic-slice_fusion.table, bf16[256,5632]{1,0:T(8,128)(2,1)S(1)} %copy-done.3, ...), custom_call_target="tpu_custom_call" | custom-call | bytes 20400000 | tf_op jit(solution)/shard_map/final/pallas_call | solution.py:964
  (227 shorter events, 97.0 us)
Async XLA Ops:
  0.6 15.2 %collective-permute-start.1 = (bf16[256,1024]{1,0:T(8,128)(2,1)}, bf16[256,1024]{1,0:T(8,128)(2,1)S(1)}, u32[]{:S(2)}, u32[]{:S(2)}) collective-permute-start(bf16[256,1024]{1,0:T(8,128)(2,1)} %tokens_ref.3), channel_id=1, source_target_pairs={{4,0},{12,4},{20,12},{28,20},{24,28},{16,24},{8,16},{0,8},{5,1},{1... | collective-permute-start | bytes 1572872 | tf_op jit(solution)/shard_map/ppermute | solution.py:625
  3.7 13.6 %collective-permute-start = (bf16[256,1024]{1,0:T(8,128)(2,1)}, bf16[256,1024]{1,0:T(8,128)(2,1)S(1)}, u32[]{:S(2)}, u32[]{:S(2)}) collective-permute-start(bf16[256,1024]{1,0:T(8,128)(2,1)} %tokens_ref.3), channel_id=1, source_target_pairs={{4,12},{12,20},{20,28},{28,24},{24,16},{16,8},{8,0},{0,4},{5,13},{... | collective-permute-start | bytes 1572872 | tf_op jit(solution)/shard_map/ppermute | solution.py:625
  7.7 9.6 %collective-permute-start.2 = (bf16[264,384]{1,0:T(8,128)(2,1)S(1)}, bf16[264,384]{1,0:T(8,128)(2,1)S(1)}, u32[]{:S(2)}, u32[]{:S(2)}) collective-permute-start(bf16[264,384]{1,0:T(8,128)(2,1)S(1)} %slice.25.refs_0_.refs_12_.refs_6_.refs_4_), channel_id=1, source_target_pairs={{0,2},{1,3},{2,0},{3,1},{4,6},{5,7},{6,4},{7,5},{8,10},{9,11},{10,... | collective-permute-start | bytes 608264 | tf_op jit(solution)/shard_map/ppermute | solution.py:705
  12.8 17.4 %collective-permute-start.7 = (bf16[256,1408]{1,0:T(8,128)(2,1)S(1)}, bf16[256,1408]{1,0:T(8,128)(2,1)S(1)}, u32[]{:S(2)}, u32[]{:S(2)}) collective-permute-start(bf16[256,1408]{1,0:T(8,128)(2,1)S(1)} %get-tuple-element.291), channel_id=1, source_target_pairs={{0,1},{1,0},{2,3},{3,2},{4,5},{5,4},{6,7},{7,6},{8,9},{9,8},{10,11... | collective-permute-start | bytes 2162696 | tf_op jit(solution)/shard_map/ppermute | solution.py:735
  12.9 18.6 %collective-permute-start.8 = (bf16[256,1408]{1,0:T(8,128)(2,1)S(1)}, bf16[256,1408]{1,0:T(8,128)(2,1)S(1)}, u32[]{:S(2)}, u32[]{:S(2)}) collective-permute-start(bf16[256,1408]{1,0:T(8,128)(2,1)S(1)} %get-tuple-element.292), channel_id=1, source_target_pairs={{0,2},{1,3},{2,0},{3,1},{4,6},{5,7},{6,4},{7,5},{8,10},{9,11},{10,... | collective-permute-start | bytes 2162696 | tf_op jit(solution)/shard_map/ppermute | solution.py:735
  17.3 12.5 %collective-permute-start.3 = (bf16[256,1024]{1,0:T(8,128)(2,1)S(1)}, bf16[256,1024]{1,0:T(8,128)(2,1)S(1)}, u32[]{:S(2)}, u32[]{:S(2)}) collective-permute-start(bf16[256,1024]{1,0:T(8,128)(2,1)S(1)} %collective-permute-done.rows_ref), channel_id=1, source_target_pairs={{4,12},{12,20},{20,28},{28,24},{24,16},{16,8},{8,0},{0,4},{5,13},{... | collective-permute-start | bytes 1572872 | tf_op jit(solution)/shard_map/ppermute | solution.py:625
  17.6 12.5 %collective-permute-start.4 = (bf16[256,1024]{1,0:T(8,128)(2,1)S(1)}, bf16[256,1024]{1,0:T(8,128)(2,1)S(1)}, u32[]{:S(2)}, u32[]{:S(2)}) collective-permute-start(bf16[256,1024]{1,0:T(8,128)(2,1)S(1)} %collective-permute-done.1.rows_ref), channel_id=1, source_target_pairs={{4,0},{12,4},{20,12},{28,20},{24,28},{16,24},{8,16},{0,8},{5,1},{1... | collective-permute-start | bytes 1572872 | tf_op jit(solution)/shard_map/ppermute | solution.py:625
  31.4 13.5 %collective-permute-start.9 = (bf16[256,1024]{1,0:T(8,128)(2,1)S(1)}, bf16[256,1024]{1,0:T(8,128)(2,1)S(1)}, u32[]{:S(2)}, u32[]{:S(2)}) collective-permute-start(bf16[256,1024]{1,0:T(8,128)(2,1)S(1)} %collective-permute-done.3.rows_ref), channel_id=1, source_target_pairs={{4,12},{12,20},{20,28},{28,24},{24,16},{16,8},{8,0},{0,4},{5,13},{... | collective-permute-start | bytes 1572872 | tf_op jit(solution)/shard_map/ppermute | solution.py:625
  32.9 13.2 %collective-permute-start.10 = (bf16[256,1024]{1,0:T(8,128)(2,1)S(1)}, bf16[256,1024]{1,0:T(8,128)(2,1)S(1)}, u32[]{:S(2)}, u32[]{:S(2)}) collective-permute-start(bf16[256,1024]{1,0:T(8,128)(2,1)S(1)} %collective-permute-done.4.rows_ref), channel_id=1, source_target_pairs={{4,0},{12,4},{20,12},{28,20},{24,28},{16,24},{8,16},{0,8},{5,1},{1... | collective-permute-start | bytes 1572872 | tf_op jit(solution)/shard_map/ppermute | solution.py:625
  33.4 19.8 %collective-permute-start.13 = (bf16[256,1408]{1,0:T(8,128)(2,1)S(1)}, bf16[256,1408]{1,0:T(8,128)(2,1)S(1)}, u32[]{:S(2)}, u32[]{:S(2)}) collective-permute-start(bf16[256,1408]{1,0:T(8,128)(2,1)S(1)} %get-tuple-element.334), channel_id=1, source_target_pairs={{0,3},{1,2},{2,1},{3,0},{4,7},{5,6},{6,5},{7,4},{8,11},{9,10},{10,... | collective-permute-start | bytes 2162696 | tf_op jit(solution)/shard_map/ppermute | solution.py:735
  55.3 11.7 %collective-permute-start.14 = (bf16[256,1024]{1,0:T(8,128)(2,1)S(1)}, bf16[256,1024]{1,0:T(8,128)(2,1)S(1)}, u32[]{:S(2)}, u32[]{:S(2)}) collective-permute-start(bf16[256,1024]{1,0:T(8,128)(2,1)S(1)} %copy-done.9), channel_id=1, source_target_pairs={{0,2},{1,3},{2,0},{3,1},{4,6},{5,7},{6,4},{7,5},{8,10},{9,11},{10,... | collective-permute-start | bytes 1572872 | tf_op jit(solution)/shard_map/ppermute | solution.py:705
  67.0 29.6 %collective-permute-start.24 = (bf16[256,1024]{1,0:T(8,128)(2,1)S(1)}, bf16[256,1024]{1,0:T(8,128)(2,1)S(1)}, u32[]{:S(2)}, u32[]{:S(2)}) collective-permute-start(bf16[256,1024]{1,0:T(8,128)(2,1)S(1)} %copy-done.6), channel_id=1, source_target_pairs={{0,2},{1,3},{2,0},{3,1},{4,6},{5,7},{6,4},{7,5},{8,10},{9,11},{10,... | collective-permute-start | bytes 1572872 | tf_op jit(solution)/shard_map/ppermute | solution.py:705
  72.9 23.7 %collective-permute-start.22 = (bf16[256,1024]{1,0:T(8,128)(2,1)S(1)}, bf16[256,1024]{1,0:T(8,128)(2,1)S(1)}, u32[]{:S(2)}, u32[]{:S(2)}) collective-permute-start(bf16[256,1024]{1,0:T(8,128)(2,1)S(1)} %copy-done.9), channel_id=1, source_target_pairs={{0,1},{1,0},{2,3},{3,2},{4,5},{5,4},{6,7},{7,6},{8,9},{9,8},{10,11... | collective-permute-start | bytes 1572872 | tf_op jit(solution)/shard_map/ppermute | solution.py:701
  72.9 23.7 %collective-permute-start.23 = (bf16[256,1024]{1,0:T(8,128)(2,1)S(1)}, bf16[256,1024]{1,0:T(8,128)(2,1)S(1)}, u32[]{:S(2)}, u32[]{:S(2)}) collective-permute-start(bf16[256,1024]{1,0:T(8,128)(2,1)S(1)} %collective-permute-done.14.refs_10_.refs_4_), channel_id=1, source_target_pairs={{0,1},{1,0},{2,3},{3,2},{4,5},{5,4},{6,7},{7,6},{8,9},{9,8},{10,11... | collective-permute-start | bytes 1572872 | tf_op jit(solution)/shard_map/ppermute | solution.py:701
  98.8 13.9 %collective-permute-start.27 = (bf16[256,1024]{1,0:T(8,128)(2,1)S(1)}, bf16[256,1024]{1,0:T(8,128)(2,1)S(1)}, u32[]{:S(2)}, u32[]{:S(2)}) collective-permute-start(bf16[256,1024]{1,0:T(8,128)(2,1)S(1)} %get-tuple-element.391.refs_0_), channel_id=1, source_target_pairs={{0,2},{1,3},{2,0},{3,1},{4,6},{5,7},{6,4},{7,5},{8,10},{9,11},{10,... | collective-permute-start | bytes 1572872 | tf_op jit(solution)/shard_map/ppermute | solution.py:705
  98.9 14.3 %collective-permute-start.30 = (bf16[256,1024]{1,0:T(8,128)(2,1)S(1)}, bf16[256,1024]{1,0:T(8,128)(2,1)S(1)}, u32[]{:S(2)}, u32[]{:S(2)}) collective-permute-start(bf16[256,1024]{1,0:T(8,128)(2,1)S(1)} %collective-permute-done.24.refs_2_.refs_6_), channel_id=1, source_target_pairs={{0,1},{1,0},{2,3},{3,2},{4,5},{5,4},{6,7},{7,6},{8,9},{9,8},{10,11... | collective-permute-start | bytes 1572872 | tf_op jit(solution)/shard_map/ppermute | solution.py:701
  112.7 9.5 %collective-permute-start.33 = (bf16[256,1024]{1,0:T(8,128)(2,1)S(1)}, bf16[256,1024]{1,0:T(8,128)(2,1)S(1)}, u32[]{:S(2)}, u32[]{:S(2)}) collective-permute-start(bf16[256,1024]{1,0:T(8,128)(2,1)S(1)} %get-tuple-element.412), channel_id=1, source_target_pairs={{0,1},{1,0},{2,3},{3,2},{4,5},{5,4},{6,7},{7,6},{8,9},{9,8},{10,11... | collective-permute-start | bytes 1572872 | tf_op jit(solution)/shard_map/ppermute | solution.py:701
  124.2 17.6 %collective-permute-start.35 = (bf16[256,1024]{1,0:T(8,128)(2,1)S(1)}, bf16[256,1024]{1,0:T(8,128)(2,1)S(1)}, u32[]{:S(2)}, u32[]{:S(2)}) collective-permute-start(bf16[256,1024]{1,0:T(8,128)(2,1)S(1)} %add_convert_fusion.9), channel_id=1, source_target_pairs={{0,2},{1,3},{2,0},{3,1},{4,6},{5,7},{6,4},{7,5},{8,10},{9,11},{10,... | collective-permute-start | bytes 1572872 | tf_op jit(solution)/shard_map/ppermute | solution.py:705
  145.8 16.1 %collective-permute-start.45 = (bf16[8,256,128]{2,1,0:T(8,128)(2,1)S(1)}, bf16[8,256,128]{2,1,0:T(8,128)(2,1)S(1)}, u32[]{:S(2)}, u32[]{:S(2)}) collective-permute-start(bf16[8,256,128]{2,1,0:T(8,128)(2,1)S(1)} %get-tuple-element.452), channel_id=1, source_target_pairs={{0,1},{1,0},{2,3},{3,2},{4,5},{5,4},{6,7},{7,6},{8,9},{9,8},{10,11... | collective-permute-start | bytes 1572872 | tf_op jit(solution)/shard_map/ppermute | solution.py:701
  147.9 16.8 %collective-permute-start.47 = (bf16[8,256,128]{2,1,0:T(8,128)(2,1)S(1)}, bf16[8,256,128]{2,1,0:T(8,128)(2,1)S(1)}, u32[]{:S(2)}, u32[]{:S(2)}) collective-permute-start(bf16[8,256,128]{2,1,0:T(8,128)(2,1)S(1)} %add_convert_fusion.7), channel_id=1, source_target_pairs={{0,2},{1,3},{2,0},{3,1},{4,6},{5,7},{6,4},{7,5},{8,10},{9,11},{10,... | collective-permute-start | bytes 1572872 | tf_op jit(solution)/shard_map/ppermute | solution.py:705
  152.9 12.0 %collective-permute-start.40 = (bf16[256,128]{1,0:T(8,128)(2,1)S(1)}, bf16[256,128]{1,0:T(8,128)(2,1)S(1)}, u32[]{:S(2)}, u32[]{:S(2)}) collective-permute-start(bf16[256,128]{1,0:T(8,128)(2,1)S(1)} %get-tuple-element.445), channel_id=1, source_target_pairs={{4,16},{12,8},{20,0},{28,4},{24,12},{16,20},{8,28},{0,24},{5,17},{... | collective-permute-start | bytes 196616 | tf_op jit(solution)/shard_map/ppermute | solution.py:625
  171.6 16.7 %collective-permute-start.48 = (bf16[192,1408]{1,0:T(8,128)(2,1)S(1)}, bf16[192,1408]{1,0:T(8,128)(2,1)S(1)}, u32[]{:S(2)}, u32[]{:S(2)}) collective-permute-start(bf16[192,1408]{1,0:T(8,128)(2,1)S(1)} %add_convert_fusion.5), channel_id=1, source_target_pairs={{4,12},{12,20},{20,28},{28,24},{24,16},{16,8},{8,0},{0,4},{5,13},{... | collective-permute-start | bytes 1622024 | tf_op jit(solution)/shard_map/ppermute | solution.py:625
  171.8 16.6 %collective-permute-start.49 = (bf16[192,1408]{1,0:T(8,128)(2,1)S(1)}, bf16[192,1408]{1,0:T(8,128)(2,1)S(1)}, u32[]{:S(2)}, u32[]{:S(2)}) collective-permute-start(bf16[192,1408]{1,0:T(8,128)(2,1)S(1)} %add_convert_fusion.4), channel_id=1, source_target_pairs={{4,0},{12,4},{20,12},{28,20},{24,28},{16,24},{8,16},{0,8},{5,1},{1... | collective-permute-start | bytes 1622024 | tf_op jit(solution)/shard_map/ppermute | solution.py:625
  188.6 11.9 %collective-permute-start.50 = (bf16[192,1408]{1,0:T(8,128)(2,1)S(1)}, bf16[192,1408]{1,0:T(8,128)(2,1)S(1)}, u32[]{:S(2)}, u32[]{:S(2)}) collective-permute-start(bf16[192,1408]{1,0:T(8,128)(2,1)S(1)} %add_convert_fusion.3), channel_id=1, source_target_pairs={{4,12},{12,20},{20,28},{28,24},{24,16},{16,8},{8,0},{0,4},{5,13},{... | collective-permute-start | bytes 1622024 | tf_op jit(solution)/shard_map/ppermute | solution.py:625
  188.8 14.4 %collective-permute-start.51 = (bf16[192,1408]{1,0:T(8,128)(2,1)S(1)}, bf16[192,1408]{1,0:T(8,128)(2,1)S(1)}, u32[]{:S(2)}, u32[]{:S(2)}) collective-permute-start(bf16[192,1408]{1,0:T(8,128)(2,1)S(1)} %add_convert_fusion.2), channel_id=1, source_target_pairs={{4,0},{12,4},{20,12},{28,20},{24,28},{16,24},{8,16},{0,8},{5,1},{1... | collective-permute-start | bytes 1622024 | tf_op jit(solution)/shard_map/ppermute | solution.py:625
  204.5 57.4 %all-to-all-start = ((bf16[8,256,512]{2,1,0:T(8,128)(2,1)}), bf16[8,256,512]{2,1,0:T(8,128)(2,1)S(1)}, u32[]{:S(2)}, u32[]{:S(2)}) async-start(bf16[8,256,512]{2,1,0:T(8,128)(2,1)} %attention_backward.1.refs_9_), calls=%async_computation | async-start | bytes 4194304 | tf_op jit(solution)/shard_map/all_to_all | solution.py:697
  208.1 36.5 %collective-permute-start.65 = (bf16[256,3072]{1,0:T(8,128)(2,1)}, bf16[256,3072]{1,0:T(8,128)(2,1)}, u32[]{:S(2)}, u32[]{:S(2)}) collective-permute-start(bf16[256,3072]{1,0:T(8,128)(2,1)} %w_qkv_ref.1), channel_id=1, source_target_pairs={{0,2},{1,3},{2,0},{3,1},{4,6},{5,7},{6,4},{7,5},{8,10},{9,11},{10,... | collective-permute-start | bytes 4718600 | tf_op jit(solution)/shard_map/ppermute | solution.py:705
  208.2 38.2 %collective-permute-start.52 = (bf16[192,1408]{1,0:T(8,128)(2,1)}, bf16[192,1408]{1,0:T(8,128)(2,1)S(1)}, u32[]{:S(2)}, u32[]{:S(2)}) collective-permute-start(bf16[192,1408]{1,0:T(8,128)(2,1)} %get-tuple-element.512), channel_id=1, source_target_pairs={{4,12},{12,20},{20,28},{28,24},{24,16},{16,8},{8,0},{0,4},{5,13},{... | collective-permute-start | bytes 1622024 | tf_op jit(solution)/shard_map/ppermute | solution.py:625
  210.2 45.0 %collective-permute-start.53 = (bf16[192,1408]{1,0:T(8,128)(2,1)}, bf16[192,1408]{1,0:T(8,128)(2,1)S(1)}, u32[]{:S(2)}, u32[]{:S(2)}) collective-permute-start(bf16[192,1408]{1,0:T(8,128)(2,1)} %get-tuple-element.513), channel_id=1, source_target_pairs={{4,0},{12,4},{20,12},{28,20},{24,28},{16,24},{8,16},{0,8},{5,1},{1... | collective-permute-start | bytes 1622024 | tf_op jit(solution)/shard_map/ppermute | solution.py:625
  210.4 93.6 %collective-permute-start.64 = (bf16[256,3072]{1,0:T(8,128)(2,1)}, bf16[256,3072]{1,0:T(8,128)(2,1)}, u32[]{:S(2)}, u32[]{:S(2)}) collective-permute-start(bf16[256,3072]{1,0:T(8,128)(2,1)} %w_qkv_ref.1), channel_id=1, source_target_pairs={{0,1},{1,0},{2,3},{3,2},{4,5},{5,4},{6,7},{7,6},{8,9},{9,8},{10,11... | collective-permute-start | bytes 4718600 | tf_op jit(solution)/shard_map/ppermute | solution.py:701
  211.9 46.8 %collective-permute-start.57 = (bf16[256,384]{1,0:T(8,128)(2,1)}, bf16[256,384]{1,0:T(8,128)(2,1)S(1)}, u32[]{:S(2)}, u32[]{:S(2)}) collective-permute-start(bf16[256,384]{1,0:T(8,128)(2,1)} %copy-done.32), channel_id=1, source_target_pairs={{0,1},{1,0},{2,3},{3,2},{4,5},{5,4},{6,7},{7,6},{8,9},{9,8},{10,11... | collective-permute-start | bytes 589832 | tf_op jit(solution)/shard_map/ppermute | solution.py:701
  244.6 59.8 %collective-permute-start.66 = (bf16[256,3072]{1,0:T(8,128)(2,1)}, bf16[256,3072]{1,0:T(8,128)(2,1)}, u32[]{:S(2)}, u32[]{:S(2)}) collective-permute-start(bf16[256,3072]{1,0:T(8,128)(2,1)} %collective-permute-done.65.refs_2_), channel_id=1, source_target_pairs={{0,1},{1,0},{2,3},{3,2},{4,5},{5,4},{6,7},{7,6},{8,9},{9,8},{10,11... | collective-permute-start | bytes 4718600 | tf_op jit(solution)/shard_map/ppermute | solution.py:701
  246.4 12.2 %collective-permute-start.59 = (bf16[256,384]{1,0:T(8,128)(2,1)S(1)}, bf16[256,384]{1,0:T(8,128)(2,1)S(1)}, u32[]{:S(2)}, u32[]{:S(2)}) collective-permute-start(bf16[256,384]{1,0:T(8,128)(2,1)S(1)} %add_convert_fusion.14), channel_id=1, source_target_pairs={{0,2},{1,3},{2,0},{3,1},{4,6},{5,7},{6,4},{7,5},{8,10},{9,11},{10,... | collective-permute-start | bytes 589832 | tf_op jit(solution)/shard_map/ppermute | solution.py:705
  266.6 27.7 %collective-permute-start.61 = (bf16[192,1408]{1,0:T(8,128)(2,1)S(1)}, bf16[192,1408]{1,0:T(8,128)(2,1)S(1)}, u32[]{:S(2)}, u32[]{:S(2)}) collective-permute-start(bf16[192,1408]{1,0:T(8,128)(2,1)S(1)} %pack.1.refs_0_), channel_id=1, source_target_pairs={{4,0},{12,4},{20,12},{28,20},{24,28},{16,24},{8,16},{0,8},{5,1},{1... | collective-permute-start | bytes 1622024 | tf_op jit(solution)/shard_map/ppermute | solution.py:625
  281.6 14.0 %collective-permute-start.60 = (bf16[192,1408]{1,0:T(8,128)(2,1)S(1)}, bf16[192,1408]{1,0:T(8,128)(2,1)S(1)}, u32[]{:S(2)}, u32[]{:S(2)}) collective-permute-start(bf16[192,1408]{1,0:T(8,128)(2,1)S(1)} %pack.1.refs_0_), channel_id=1, source_target_pairs={{4,12},{12,20},{20,28},{28,24},{24,16},{16,8},{8,0},{0,4},{5,13},{... | collective-permute-start | bytes 1622024 | tf_op jit(solution)/shard_map/ppermute | solution.py:625
  281.6 17.4 %collective-permute-start.72 = (bf16[256,512]{1,0:T(8,128)(2,1)S(1)}, bf16[256,512]{1,0:T(8,128)(2,1)S(1)}, u32[]{:S(2)}, u32[]{:S(2)}) collective-permute-start(bf16[256,512]{1,0:T(8,128)(2,1)S(1)} %join.1.refs_9_), channel_id=1, source_target_pairs={{4,0},{12,4},{20,12},{28,20},{24,28},{16,24},{8,16},{0,8},{5,1},{1... | collective-permute-start | bytes 786440 | tf_op jit(solution)/shard_map/ppermute | solution.py:625
  294.2 9.7 %collective-permute-start.71 = (bf16[256,512]{1,0:T(8,128)(2,1)S(1)}, bf16[256,512]{1,0:T(8,128)(2,1)S(1)}, u32[]{:S(2)}, u32[]{:S(2)}) collective-permute-start(bf16[256,512]{1,0:T(8,128)(2,1)S(1)} %join.1.refs_9_), channel_id=1, source_target_pairs={{4,12},{12,20},{20,28},{28,24},{24,16},{16,8},{8,0},{0,4},{5,13},{... | collective-permute-start | bytes 786440 | tf_op jit(solution)/shard_map/ppermute | solution.py:625
  295.6 23.6 %collective-permute-start.62 = (bf16[192,1408]{1,0:T(8,128)(2,1)S(1)}, bf16[192,1408]{1,0:T(8,128)(2,1)S(1)}, u32[]{:S(2)}, u32[]{:S(2)}) collective-permute-start(bf16[192,1408]{1,0:T(8,128)(2,1)S(1)} %collective-permute-done.60.refs_8_), channel_id=1, source_target_pairs={{4,12},{12,20},{20,28},{28,24},{24,16},{16,8},{8,0},{0,4},{5,13},{... | collective-permute-start | bytes 1622024 | tf_op jit(solution)/shard_map/ppermute | solution.py:625
  299.0 20.2 %collective-permute-start.63 = (bf16[192,1408]{1,0:T(8,128)(2,1)S(1)}, bf16[192,1408]{1,0:T(8,128)(2,1)S(1)}, u32[]{:S(2)}, u32[]{:S(2)}) collective-permute-start(bf16[192,1408]{1,0:T(8,128)(2,1)S(1)} %collective-permute-done.61.refs_1_), channel_id=1, source_target_pairs={{4,0},{12,4},{20,12},{28,20},{24,28},{16,24},{8,16},{0,8},{5,1},{1... | collective-permute-start | bytes 1622024 | tf_op jit(solution)/shard_map/ppermute | solution.py:625
  303.9 17.3 %collective-permute-start.31 = (bf16[256,1024]{1,0:T(8,128)(2,1)S(1)}, bf16[256,1024]{1,0:T(8,128)(2,1)S(1)}, u32[]{:S(2)}, u32[]{:S(2)}) collective-permute-start(bf16[256,1024]{1,0:T(8,128)(2,1)S(1)} %copy-done.31), channel_id=1, source_target_pairs={{0,1},{1,0},{2,3},{3,2},{4,5},{5,4},{6,7},{7,6},{8,9},{9,8},{10,11... | collective-permute-start | bytes 1572872 | tf_op jit(solution)/shard_map/ppermute | solution.py:701
  303.9 14.9 %collective-permute-start.73 = (bf16[256,512]{1,0:T(8,128)(2,1)S(1)}, bf16[256,512]{1,0:T(8,128)(2,1)S(1)}, u32[]{:S(2)}, u32[]{:S(2)}) collective-permute-start(bf16[256,512]{1,0:T(8,128)(2,1)S(1)} %collective-permute-done.71.refs_17_), channel_id=1, source_target_pairs={{4,12},{12,20},{20,28},{28,24},{24,16},{16,8},{8,0},{0,4},{5,13},{... | collective-permute-start | bytes 786440 | tf_op jit(solution)/shard_map/ppermute | solution.py:625
  304.5 14.4 %collective-permute-start.74 = (bf16[256,512]{1,0:T(8,128)(2,1)S(1)}, bf16[256,512]{1,0:T(8,128)(2,1)S(1)}, u32[]{:S(2)}, u32[]{:S(2)}) collective-permute-start(bf16[256,512]{1,0:T(8,128)(2,1)S(1)} %collective-permute-done.72.refs_10_), channel_id=1, source_target_pairs={{4,0},{12,4},{20,12},{28,20},{24,28},{16,24},{8,16},{0,8},{5,1},{1... | collective-permute-start | bytes 786440 | tf_op jit(solution)/shard_map/ppermute | solution.py:625
  318.8 24.4 %collective-permute-start.28 = (bf16[256,1024]{1,0:T(8,128)(2,1)S(1)}, bf16[256,1024]{1,0:T(8,128)(2,1)S(1)}, u32[]{:S(2)}, u32[]{:S(2)}) collective-permute-start(bf16[256,1024]{1,0:T(8,128)(2,1)S(1)} %copy-done.29), channel_id=1, source_target_pairs={{0,1},{1,0},{2,3},{3,2},{4,5},{5,4},{6,7},{7,6},{8,9},{9,8},{10,11... | collective-permute-start | bytes 1572872 | tf_op jit(solution)/shard_map/ppermute | solution.py:701
  318.8 9.5 %collective-permute-start.75 = (bf16[256,512]{1,0:T(8,128)(2,1)S(1)}, bf16[256,512]{1,0:T(8,128)(2,1)S(1)}, u32[]{:S(2)}, u32[]{:S(2)}) collective-permute-start(bf16[256,512]{1,0:T(8,128)(2,1)S(1)} %collective-permute-done.73.refs_16_), channel_id=1, source_target_pairs={{4,12},{12,20},{20,28},{28,24},{24,16},{16,8},{8,0},{0,4},{5,13},{... | collective-permute-start | bytes 786440 | tf_op jit(solution)/shard_map/ppermute | solution.py:625
  319.2 21.9 %collective-permute-start.67 = (bf16[192,1408]{1,0:T(8,128)(2,1)S(1)}, bf16[192,1408]{1,0:T(8,128)(2,1)S(1)}, u32[]{:S(2)}, u32[]{:S(2)}) collective-permute-start(bf16[192,1408]{1,0:T(8,128)(2,1)S(1)} %collective-permute-done.62.refs_7_), channel_id=1, source_target_pairs={{4,12},{12,20},{20,28},{28,24},{24,16},{16,8},{8,0},{0,4},{5,13},{... | collective-permute-start | bytes 1622024 | tf_op jit(solution)/shard_map/ppermute | solution.py:625
  320.7 21.5 %collective-permute-start.68 = (bf16[192,1408]{1,0:T(8,128)(2,1)S(1)}, bf16[192,1408]{1,0:T(8,128)(2,1)S(1)}, u32[]{:S(2)}, u32[]{:S(2)}) collective-permute-start(bf16[192,1408]{1,0:T(8,128)(2,1)S(1)} %collective-permute-done.63.refs_2_), channel_id=1, source_target_pairs={{4,0},{12,4},{20,12},{28,20},{24,28},{16,24},{8,16},{0,8},{5,1},{1... | collective-permute-start | bytes 1622024 | tf_op jit(solution)/shard_map/ppermute | solution.py:625
  321.5 22.9 %collective-permute-start.32 = (bf16[256,1024]{1,0:T(8,128)(2,1)S(1)}, bf16[256,1024]{1,0:T(8,128)(2,1)S(1)}, u32[]{:S(2)}, u32[]{:S(2)}) collective-permute-start(bf16[256,1024]{1,0:T(8,128)(2,1)S(1)} %add_convert_fusion.12), channel_id=1, source_target_pairs={{0,2},{1,3},{2,0},{3,1},{4,6},{5,7},{6,4},{7,5},{8,10},{9,11},{10,... | collective-permute-start | bytes 1572872 | tf_op jit(solution)/shard_map/ppermute | solution.py:705
  328.3 11.8 %collective-permute-start.76 = (bf16[256,512]{1,0:T(8,128)(2,1)S(1)}, bf16[256,512]{1,0:T(8,128)(2,1)S(1)}, u32[]{:S(2)}, u32[]{:S(2)}) collective-permute-start(bf16[256,512]{1,0:T(8,128)(2,1)S(1)} %collective-permute-done.74.refs_11_), channel_id=1, source_target_pairs={{4,0},{12,4},{20,12},{28,20},{24,28},{16,24},{8,16},{0,8},{5,1},{1... | collective-permute-start | bytes 786440 | tf_op jit(solution)/shard_map/ppermute | solution.py:625
  (66 other events, 618.8 us)
where the time goes:
time: 359 us; the launch traced here: 360 us
  waiting for transfers between devices  150 us (42%)
  starting transfers between devices  103 us (29%)
  Pallas kernels  88 us (25%)
  local copies, waits for them, and re-layouts  11.4 us (3%)
  other arithmetic  5.43 us (2%)
    ppermute x46, waiting for transfers between devices, ring_shift(): lax.ppermute(value, 'ctx', [(ring[i], ring[(i + step) % count]) for i in...  102 us
    ppermute x46, starting transfers between devices, ring_shift(): lax.ppermute(value, 'ctx', [(ring[i], ring[(i + step) % count]) for i in...  81.5 us
    pallas_call x22, Pallas kernels, call(): pl.pallas_call(kernel, out_shape=list(out), in_specs=[SM] + [VM] * (len(i...  53.8 us
    ppermute x9, waiting for transfers between devices, chip_shift(): lax.ppermute(value, 'fsdp', [(i, (i + 2 * step) % count) for i in range(c...  36 us
    pallas_call x1, Pallas kernels, attention_backward(): pl.pallas_call(functools.partial(bwd_kernel, meta), out_shape=jax.ShapeDt...  14.6 us
    ppermute x9, starting transfers between devices, chip_shift(): lax.ppermute(value, 'fsdp', [(i, (i + 2 * step) % count) for i in range(c...  13.1 us
    pallas_call x1, Pallas kernels, attention_forward(): pl.pallas_call(functools.partial(fwd_kernel, meta), out_shape=[jax.ShapeD...  11.1 us
    ppermute x18, waiting for transfers between devices, partner(): return lax.ppermute(value, 'fsdp', [(i, i ^ 1) for i in range(count)])  9.66 us
  transfers between devices with their start and end apart: 80, of which 45 were waited for; matrix products, arithmetic and copies ran while one was open for 2% of the time, Pallas kernels for 20%

commit v1 on v0

--- a/solution.py
+++ b/solution.py
@@ -544,8 +544,7 @@
             gu_ref[at(start, sub), part * hidden : (part + 1) * hidden] = lines[:, 0:hidden]
             gu_ref[at(start, sub), (count + part) * hidden : (count + part + 1) * hidden] = lines[:, hidden:]
             side, line = part // (count // 2), (count + part % (count // 2)) * sub
-            turned = wide(pieces_ref[k, line : line + sub, :])[:, side * hidden : (side + 1) * hidden] * factor
-            turned_ref[at(part * (n * sub) + start, sub), :] = turned
+            turned_ref[at(part * (n * sub) + start, sub), :] = pieces_ref[k, line : line + sub, side * hidden : (side + 1) * hidden]
         return 0
 
     lax.fori_loop(0, n, one, 0)
@@ -570,7 +569,7 @@
     leave(2)
     leave(3)
     for i in range(width // 128):
-        down_ref[:, i * 128 : (i + 1) * 128] = jnp.transpose(turned_ref[i * 128 : (i + 1) * 128, :])
+        down_ref[:, i * 128 : (i + 1) * 128] = wide(jnp.transpose(turned_ref[i * 128 : (i + 1) * 128, :])) * factor
     leave(1)
     gain_outs[0][...] = row_sums(wide(gate_up_ref[...]) * gu_ref[...]) / wide(gain_two_ref[...])
     gain_outs[1][...] = row_sums(wide(w_qkv_ref[...]) * qkv_ref[...]) / wide(gain_one_ref[...])
@@ -837,13 +836,12 @@
     out_slots, out_t, log_total = attention_forward(
         table, lengths, block_order, qkv, ctx, own_heads, depth, TILE
     )
-    out_slots, outs, gate_pieces = tie(out_slots, outs, gate_pieces)
-    later_cot, out_slots = tie(cotangent, out_slots)
+    near_out = partner(w_out, fsdp)
+    out_slots, outs, near_out, gate_pieces = tie(out_slots, outs, near_out, gate_pieces)
+    attn_parts = ring_exchange(out_slots, ring)
+    later_cot, outs, unused = tie(cotangent, outs, attn_parts[-1])
     cots = far_gather(later_cot, fsdp)
-    attn_parts = ring_exchange(out_slots, ring)
-    outs = near_gather(outs, fsdp)
-    attn_parts, outs, cots = tie(attn_parts, outs, cots)
-    cots = near_gather(cots, fsdp)
+    outs = [outs[0], near_out] + near_gather(outs[1:], fsdp)
     resid, ffn_in = call(
         "leave", functools.partial(leave_kernel, ctx, fsdp),
         [shape((rows, width), f32), shape((rows, width))],
@@ -851,6 +849,9 @@
         scratch=[gain_scratch, square_scratch],
         time=4.1,
     )
+
+    ffn_in, cots = tie(ffn_in, cots)
+    cots = near_gather(cots, fsdp)
 
     nears = far_gather(ffn_in, fsdp)
     ffns, grad_terms, out_terms, hiddens, grads = [], [], [], [], []
@@ -891,7 +892,6 @@
         scratch=[gain_scratch, square_scratch],
         time=5,
     )
-    grad_attn, branch, ffn_sums.up, ffn_sums.down = tie(grad_attn, branch, ffn_sums.up, ffn_sums.down)
     grad_slots = ring_exchange(grad_attn, ring)
     out_sides = call(
         "out_weights", functools.partial(out_weight_kernel, ctx, fsdp),
@@ -959,7 +959,7 @@
     ]
     inputs = [table, w_gate_up, gain_two, w_qkv if aligned else unmixed(relative(w_qkv, table, ctx), ctx, own_width), gain_one]
     inputs += ffn_going.slots() + attn_going.slots()
-    scratch = [pltpu.VMEM(x.shape, f32) for x in results] + [pltpu.VMEM((width, hidden), f32)]
+    scratch = [pltpu.VMEM(x.shape, f32) for x in results] + [pltpu.VMEM((width, hidden), jnp.bfloat16)]
     scratch += [pltpu.VMEM((ctx,) + packed.shape, jnp.bfloat16), pltpu.VMEM((ctx,) + joined.shape, jnp.bfloat16)]
     *results, grad_gain_ffn, grad_gain_attn = pl.pallas_call(
         functools.partial(final_kernel, ctx, fsdp, factor, aligned),

time: 359 us -> 355 us (0.989)
  starting transfers between devices: 103 us -> 92.8 us
  Pallas kernels: 88 us -> 96.7 us
  waiting for transfers between devices: 150 us -> 145 us
    ppermute x46, starting transfers between devices: 81.5 us -> 74.8 us  [ring_shift(): lax.ppermute(value, 'ctx', [(ring[i], ring[(i + step) % count]) for i in...]
    pallas_call x1, Pallas kernels: 14.6 us -> 19.2 us  [attention_backward(): pl.pallas_call(functools.partial(bwd_kernel, meta), out_shape=jax.ShapeDt...]
    pallas_call x1, Pallas kernels: 11.1 us -> 15.4 us  [attention_forward(): pl.pallas_call(functools.partial(fwd_kernel, meta), out_shape=[jax.ShapeD...]
  transfers between devices with their start and end apart: 80 -> 80, of which waited for: 45 -> 44; matrix products, arithmetic and copies ran while one was open for 2% -> 2% of each run, Pallas kernels for 20% -> 24%
where the time goes in v1:
time: 355 us; the launch traced here: 353 us
  waiting for transfers between devices  145 us (41%)
  Pallas kernels  96.7 us (27%)
  starting transfers between devices  92.8 us (26%)
  local copies, waits for them, and re-layouts  11.4 us (3%)
  other arithmetic  5.43 us (2%)
    ppermute x46, waiting for transfers between devices, ring_shift(): lax.ppermute(value, 'ctx', [(ring[i], ring[(i + step) % count]) for i in...  101 us
    ppermute x46, starting transfers between devices, ring_shift(): lax.ppermute(value, 'ctx', [(ring[i], ring[(i + step) % count]) for i in...  74.8 us
    pallas_call x22, Pallas kernels, call(): pl.pallas_call(kernel, out_shape=list(out), in_specs=[SM] + [VM] * (len(i...  54 us
    ppermute x9, waiting for transfers between devices, chip_shift(): lax.ppermute(value, 'fsdp', [(i, (i + 2 * step) % count) for i in range(c...  33.9 us
    pallas_call x1, Pallas kernels, attention_backward(): pl.pallas_call(functools.partial(bwd_kernel, meta), out_shape=jax.ShapeDt...  19.2 us
    pallas_call x1, Pallas kernels, attention_forward(): pl.pallas_call(functools.partial(fwd_kernel, meta), out_shape=[jax.ShapeD...  15.4 us
    ppermute x9, starting transfers between devices, chip_shift(): lax.ppermute(value, 'fsdp', [(i, (i + 2 * step) % count) for i in range(c...  9.61 us
    unnamed x68, local copies, waits for them, and re-layouts  9.27 us
  transfers between devices with their start and end apart: 80, of which 44 were waited for; matrix products, arithmetic and copies ran while one was open for 2% of the time, Pallas kernels for 24%

profile of v1, /device:TPU:0, one launch (start us, length us, event | category | flops | bytes accessed | tf_op | source)
XLA Modules:
  0.0 353.1 jit_solution(14481332220290277163)
XLA Ops:
  0.6 3.1 collective-permute-start.1
  7.7 2.0 collective-permute-start.2
  9.7 1.8 copy-done.2
  13.0 2.8 collective-permute-done.1.rows_ref
  25.7 4.1 %collective-permute-done.3.rows_ref = bf16[256,1024]{1,0:T(8,128)(2,1)S(1)} collective-permute-done((bf16[256,1024]{1,0:T(8,128)(2,1)S(1)}, bf16[256,1024]{1,0:T(8,128)(2,1)S(1)}, u32[]{:S(2)}, u32[]{:S(2)}) %collective-permute-start.3) | collective-permute-done | bytes 524320 | tf_op jit(solution)/shard_map/ppermute | solution.py:624
  35.8 9.2 %collective-permute-done.9.rows_ref = bf16[256,1024]{1,0:T(8,128)(2,1)S(1)} collective-permute-done((bf16[256,1024]{1,0:T(8,128)(2,1)S(1)}, bf16[256,1024]{1,0:T(8,128)(2,1)S(1)}, u32[]{:S(2)}, u32[]{:S(2)}) %collective-permute-start.9) | collective-permute-done | bytes 524320 | tf_op jit(solution)/shard_map/ppermute | solution.py:624
  50.6 2.3 collective-permute-done.12.rows_ref
  55.9 15.4 %attention_forward.1 = (bf16[256,128]{1,0:T(8,128)(2,1)S(1)}, bf16[256,128]{1,0:T(8,128)(2,1)S(1)}, bf16[256,128]{1,0:T(8,128)(2,1)S(1)}, bf16[256,128]{1,0:T(8,...) custom-call(s32[1,12]{1,0:T(1,128)S(1)} %constant_dynamic-slice_fusi, ...), custom_call_target="tpu_custom_call" | custom-call | bytes 57800000 | tf_op jit(solution)/shard_map/attention_forward/pallas_call | solution.py:205
  72.8 2.9 collective-permute-done.22.refs_7_
  77.3 2.5 collective-permute-start.17
  81.0 3.9 %collective-permute-start.19 = (bf16[256,128]{1,0:T(8,128)(2,1)S(1)}, bf16[256,128]{1,0:T(8,128)(2,1)S(1)}, u32[]{:S(2)}, u32[]{:S(2)}) collective-permute-start(bf16[256,128]{1,0:T(8,128)(2,1)S(1)} %get-tuple-element.336), channel_id=1, source_target_pairs={{4,24},{12,16},{20,8},{28,0},{24,4},{16,12},{8,20},{0,28},{5,25},{... | collective-permute-start | bytes 196616 | tf_op jit(solution)/shard_map/ppermute | solution.py:624
  86.5 2.7 collective-permute-done.18.refs_3_
  91.1 4.0 %collective-permute-done.21.refs_6_ = bf16[256,128]{1,0:T(8,128)(2,1)S(1)} collective-permute-done((bf16[256,128]{1,0:T(8,128)(2,1)S(1)}, bf16[256,128]{1,0:T(8,128)(2,1)S(1)}, u32[]{:S(2)}, u32[]{:S(2)}) %collective-permute-start.21) | collective-permute-done | bytes 65568 | tf_op jit(solution)/shard_map/ppermute | solution.py:624
  97.2 2.5 collective-permute-start.27
  99.8 7.5 %feed_forward.2 = (bf16[256,1024]{1,0:T(8,128)(2,1)S(1)}, bf16[256,1024]{1,0:T(8,128)(2,1)S(1)}, bf16[256,1024]{1,0:T(8,128)(2,1)S(1)}, bf16[256,1024]{1,0:T(8,1...) custom-call(s32[1,12]{1,0:T(1,128)S(1)} %constant_dynamic-slice_fusion.table, ...), custom_call_target="tpu_custom_call" | custom-call | bytes 32300000 | tf_op jit(solution)/shard_map/feed_forward/pallas_call | solution.py:259
  109.0 2.9 collective-permute-done.27.refs_0_.refs_2_
  113.8 7.3 %feed_forward.3 = (bf16[256,1024]{1,0:T(8,128)(2,1)S(1)}, bf16[256,1024]{1,0:T(8,128)(2,1)S(1)}, bf16[256,1024]{1,0:T(8,128)(2,1)S(1)}, bf16[256,1024]{1,0:T(8,1...) custom-call(s32[1,12]{1,0:T(1,128)S(1)} %constant_dynamic-slice_fusion.table, ...), custom_call_target="tpu_custom_call" | custom-call | bytes 32300000 | tf_op jit(solution)/shard_map/feed_forward/pallas_call | solution.py:259
  123.4 1.8 collective-permute-start.37
  125.2 7.1 %feed_forward_weights.1 = (bf16[192,1408]{1,0:T(8,128)(2,1)S(1)}, bf16[192,1408]{1,0:T(8,128)(2,1)S(1)}, bf16[192,1408]{1,0:T(8,128)(2,1)S(1)}, bf16[192,1408]{1...) custom-call(s32[1,12]{1,0:T(1,128)S(1)} %constant_dynamic-slice_fusi, ...), custom_call_target="tpu_custom_call" | custom-call | bytes 40800000 | tf_op jit(solution)/shard_map/feed_forward_weights/pallas_call | solution.py:259
  132.3 5.2 %collective-permute-done.37.refs_1_ = bf16[256,1024]{1,0:T(8,128)(2,1)S(1)} collective-permute-done((bf16[256,1024]{1,0:T(8,128)(2,1)S(1)}, bf16[256,1024]{1,0:T(8,128)(2,1)S(1)}, u32[]{:S(2)}, u32[]{:S(2)}) %collective-permute-start.37) | collective-permute-done | bytes 524320 | tf_op jit(solution)/shard_map/ppermute | solution.py:704
  137.5 2.4 branch.1
  143.6 1.8 collective-permute-start.47
  147.5 6.2 %collective-permute-done.35 = bf16[96,1408]{1,0:T(8,128)(2,1)S(1)} collective-permute-done((bf16[96,1408]{1,0:T(8,128)(2,1)S(1)}, bf16[96,1408]{1,0:T(8,128)(2,1)S(1)}, u32[]{:S(2)}, u32[]{:S(2)}) %collective-permute-start.35) | collective-permute-done | bytes 270368 | tf_op jit(solution)/shard_map/ppermute | solution.py:624
  156.4 2.4 collective-permute-start.41
  160.1 3.3 collective-permute-start.42
  163.4 3.2 collective-permute-start.43
  167.5 2.3 collective-permute-done.43.refs_15_
  173.8 19.2 %attention_backward.1.refs_9_ = bf16[8,256,512]{2,1,0:T(8,128)(2,1)} custom-call(s32[1,12]{1,0:T(1,128)S(1)} %constant_dynamic-slice_fusion.table, s32[1,4]{1,0:T(1,128)S(1)} %copy-done.26, s32[1,32]{1,0:T(1,128)S(1)} %copy-done.27, bf16[256,384]{1,0:T(8,128)(2,1)S(1)} %get-tuple-element.279.refs_0_, bf16[256,384]{1,0:T(8,128)(2,1)S(1)} %get-tuple-element.308.refs_1_, ...), custom_call_target="tpu_custom_call" | custom-call | bytes 61200000 | tf_op jit(solution)/shard_map/attention_backward/pallas_call | solution.py:218
  195.4 4.8 %qkv_weights.1 = (bf16[256,384]{1,0:T(8,128)(2,1)S(1)}, bf16[256,384]{1,0:T(8,128)(2,1)S(1)}, bf16[256,384]{1,0:T(8,128)(2,1)S(1)}, bf16[256,384]{1,0:T(8,128)(2,1)S(1)}) custom-call(s32[1,12]{1,0:T(1,128)S(1)} %constant_dynamic-slice_fusion.table, bf16[256,1024]{1,0:T(8,128)(2,1)S(1)} %get-tuple-element.437.refs_0_, ...), custom_call_target="tpu_custom_call" | custom-call | bytes 20400000 | tf_op jit(solution)/shard_map/qkv_weights/pallas_call | solution.py:259
  200.3 2.5 collective-permute-done.50
  204.6 3.8 %all-to-all-start = ((bf16[8,256,512]{2,1,0:T(8,128)(2,1)}), bf16[8,256,512]{2,1,0:T(8,128)(2,1)S(1)}, u32[]{:S(2)}, u32[]{:S(2)}) async-start(bf16[8,256,512]{2,1,0:T(8,128)(2,1)} %attention_backward.1.refs_9_), calls=%async_computation | async-start | bytes 4194304 | tf_op jit(solution)/shard_map/all_to_all | solution.py:696
  208.5 2.0 collective-permute-start.52
  212.3 25.8 %collective-permute-done.65.refs_2_ = bf16[256,3072]{1,0:T(8,128)(2,1)} collective-permute-done((bf16[256,3072]{1,0:T(8,128)(2,1)}, bf16[256,3072]{1,0:T(8,128)(2,1)}, u32[]{:S(2)}, u32[]{:S(2)}) %collective-permute-start.65) | collective-permute-done | bytes 1572896 | tf_op jit(solution)/shard_map/ppermute | solution.py:704
  239.1 5.6 %collective-permute-done.52.up_ref = bf16[192,1408]{1,0:T(8,128)(2,1)S(1)} collective-permute-done((bf16[192,1408]{1,0:T(8,128)(2,1)}, bf16[192,1408]{1,0:T(8,128)(2,1)S(1)}, u32[]{:S(2)}, u32[]{:S(2)}) %collective-permute-start.52) | collective-permute-done | bytes 540704 | tf_op jit(solution)/shard_map/ppermute | solution.py:624
  244.7 4.0 %collective-permute-done.53.down_ref = bf16[192,1408]{1,0:T(8,128)(2,1)S(1)} collective-permute-done((bf16[192,1408]{1,0:T(8,128)(2,1)}, bf16[192,1408]{1,0:T(8,128)(2,1)S(1)}, u32[]{:S(2)}, u32[]{:S(2)}) %collective-permute-start.53) | collective-permute-done | bytes 540704 | tf_op jit(solution)/shard_map/ppermute | solution.py:624
  252.8 1.8 collective-permute-start.56
  260.1 14.6 %collective-permute-start.61 = (bf16[192,1408]{1,0:T(8,128)(2,1)S(1)}, bf16[192,1408]{1,0:T(8,128)(2,1)S(1)}, u32[]{:S(2)}, u32[]{:S(2)}) collective-permute-start(bf16[192,1408]{1,0:T(8,128)(2,1)S(1)} %pack.1.refs_0_), channel_id=1, source_target_pairs={{4,0},{12,4},{20,12},{28,20},{24,28},{16,24},{8,16},{0,8},{5,1},{1... | collective-permute-start | bytes 1622024 | tf_op jit(solution)/shard_map/ppermute | solution.py:624
  274.7 2.0 collective-permute-start.72
  276.7 10.6 %collective-permute-done.61.refs_1_ = bf16[192,1408]{1,0:T(8,128)(2,1)S(1)} collective-permute-done((bf16[192,1408]{1,0:T(8,128)(2,1)S(1)}, bf16[192,1408]{1,0:T(8,128)(2,1)S(1)}, u32[]{:S(2)}, u32[]{:S(2)}) %collective-permute-start.61) | collective-permute-done | bytes 540704 | tf_op jit(solution)/shard_map/ppermute | solution.py:624
  290.2 1.9 collective-permute-done.72.refs_10_
  292.1 2.5 collective-permute-start.63
  294.6 2.4 collective-permute-done.71.refs_17_
  299.2 6.6 %tail.1 = bf16[256,1024]{1,0:T(8,128)(2,1)} custom-call(s32[1,12]{1,0:T(1,128)S(1)} %constant_dynamic-slice_fusion.table, bf16[256,1024]{1,0:T(8,128)(2,1)S(1)} %copy-done.5, f32[256,1024]{1,0:T(8,128)S(1)} %copy-done.11, bf16[8,256,512]{2,1,0:T(8,128)(2,1)S(1)} %all-to-all-done.refs_2_.parts_ref, bf16[256,3072]{1,0:T(8,128)(2,1)S(1)} %copy-done.1, ...), custom_call_target="tpu_custom_call" | custom-call | bytes 27200000 | tf_op jit(solution)/shard_map/tail/pallas_call | solution.py:259
  305.9 6.1 %collective-permute-done.73.refs_16_ = bf16[256,512]{1,0:T(8,128)(2,1)S(1)} collective-permute-done((bf16[256,512]{1,0:T(8,128)(2,1)S(1)}, bf16[256,512]{1,0:T(8,128)(2,1)S(1)}, u32[]{:S(2)}, u32[]{:S(2)}) %collective-permute-start.73) | collective-permute-done | bytes 262176 | tf_op jit(solution)/shard_map/ppermute | solution.py:624
  316.0 5.1 %collective-permute-done.75.refs_15_ = bf16[256,512]{1,0:T(8,128)(2,1)S(1)} collective-permute-done((bf16[256,512]{1,0:T(8,128)(2,1)S(1)}, bf16[256,512]{1,0:T(8,128)(2,1)S(1)}, u32[]{:S(2)}, u32[]{:S(2)}) %collective-permute-start.75) | collective-permute-done | bytes 262176 | tf_op jit(solution)/shard_map/ppermute | solution.py:624
  322.9 11.2 %collective-permute-done.76.refs_12_ = bf16[256,512]{1,0:T(8,128)(2,1)S(1)} collective-permute-done((bf16[256,512]{1,0:T(8,128)(2,1)S(1)}, bf16[256,512]{1,0:T(8,128)(2,1)S(1)}, u32[]{:S(2)}, u32[]{:S(2)}) %collective-permute-start.76) | collective-permute-done | bytes 262176 | tf_op jit(solution)/shard_map/ppermute | solution.py:624
  341.1 3.5 collective-permute-done.70.refs_5_
  344.9 8.1 %final.1 = (f32[256,5632]{1,0:T(8,128)}, f32[704,1024]{1,0:T(8,128)}, f32[256,3072]{1,0:T(8,128)}, f32[256,1024]{1,0:T(8,128)}, f32[1,256]{1,0:T(1,128)}, /*index=5*/f32[1,256]{1,0:T(1,128)}) custom-call(s32[1,12]{1,0:T(1,128)S(1)} %constant_dynamic-slice_fusion.table, bf16[256,5632]{1,0:T(8,128)(2,1)S(1)} %copy-done.3, ...), custom_call_target="tpu_custom_call" | custom-call | bytes 20400000 | tf_op jit(solution)/shard_map/final/pallas_call | solution.py:964
  (227 shorter events, 94.7 us)
Async XLA Ops:
  0.6 15.2 %collective-permute-start.1 = (bf16[256,1024]{1,0:T(8,128)(2,1)}, bf16[256,1024]{1,0:T(8,128)(2,1)S(1)}, u32[]{:S(2)}, u32[]{:S(2)}) collective-permute-start(bf16[256,1024]{1,0:T(8,128)(2,1)} %tokens_ref.3), channel_id=1, source_target_pairs={{4,0},{12,4},{20,12},{28,20},{24,28},{16,24},{8,16},{0,8},{5,1},{1... | collective-permute-start | bytes 1572872 | tf_op jit(solution)/shard_map/ppermute | solution.py:624
  3.7 13.6 %collective-permute-start = (bf16[256,1024]{1,0:T(8,128)(2,1)}, bf16[256,1024]{1,0:T(8,128)(2,1)S(1)}, u32[]{:S(2)}, u32[]{:S(2)}) collective-permute-start(bf16[256,1024]{1,0:T(8,128)(2,1)} %tokens_ref.3), channel_id=1, source_target_pairs={{4,12},{12,20},{20,28},{28,24},{24,16},{16,8},{8,0},{0,4},{5,13},{... | collective-permute-start | bytes 1572872 | tf_op jit(solution)/shard_map/ppermute | solution.py:624
  7.7 9.6 %collective-permute-start.2 = (bf16[264,384]{1,0:T(8,128)(2,1)S(1)}, bf16[264,384]{1,0:T(8,128)(2,1)S(1)}, u32[]{:S(2)}, u32[]{:S(2)}) collective-permute-start(bf16[264,384]{1,0:T(8,128)(2,1)S(1)} %slice.25.refs_0_.refs_12_.refs_6_.refs_4_), channel_id=1, source_target_pairs={{0,2},{1,3},{2,0},{3,1},{4,6},{5,7},{6,4},{7,5},{8,10},{9,11},{10,... | collective-permute-start | bytes 608264 | tf_op jit(solution)/shard_map/ppermute | solution.py:704
  12.8 17.4 %collective-permute-start.7 = (bf16[256,1408]{1,0:T(8,128)(2,1)S(1)}, bf16[256,1408]{1,0:T(8,128)(2,1)S(1)}, u32[]{:S(2)}, u32[]{:S(2)}) collective-permute-start(bf16[256,1408]{1,0:T(8,128)(2,1)S(1)} %get-tuple-element.264), channel_id=1, source_target_pairs={{0,1},{1,0},{2,3},{3,2},{4,5},{5,4},{6,7},{7,6},{8,9},{9,8},{10,11... | collective-permute-start | bytes 2162696 | tf_op jit(solution)/shard_map/ppermute | solution.py:734
  12.9 18.6 %collective-permute-start.8 = (bf16[256,1408]{1,0:T(8,128)(2,1)S(1)}, bf16[256,1408]{1,0:T(8,128)(2,1)S(1)}, u32[]{:S(2)}, u32[]{:S(2)}) collective-permute-start(bf16[256,1408]{1,0:T(8,128)(2,1)S(1)} %get-tuple-element.265), channel_id=1, source_target_pairs={{0,2},{1,3},{2,0},{3,1},{4,6},{5,7},{6,4},{7,5},{8,10},{9,11},{10,... | collective-permute-start | bytes 2162696 | tf_op jit(solution)/shard_map/ppermute | solution.py:734
  17.3 12.5 %collective-permute-start.3 = (bf16[256,1024]{1,0:T(8,128)(2,1)S(1)}, bf16[256,1024]{1,0:T(8,128)(2,1)S(1)}, u32[]{:S(2)}, u32[]{:S(2)}) collective-permute-start(bf16[256,1024]{1,0:T(8,128)(2,1)S(1)} %collective-permute-done.rows_ref), channel_id=1, source_target_pairs={{4,12},{12,20},{20,28},{28,24},{24,16},{16,8},{8,0},{0,4},{5,13},{... | collective-permute-start | bytes 1572872 | tf_op jit(solution)/shard_map/ppermute | solution.py:624
  17.6 12.5 %collective-permute-start.4 = (bf16[256,1024]{1,0:T(8,128)(2,1)S(1)}, bf16[256,1024]{1,0:T(8,128)(2,1)S(1)}, u32[]{:S(2)}, u32[]{:S(2)}) collective-permute-start(bf16[256,1024]{1,0:T(8,128)(2,1)S(1)} %collective-permute-done.1.rows_ref), channel_id=1, source_target_pairs={{4,0},{12,4},{20,12},{28,20},{24,28},{16,24},{8,16},{0,8},{5,1},{1... | collective-permute-start | bytes 1572872 | tf_op jit(solution)/shard_map/ppermute | solution.py:624
  31.4 13.5 %collective-permute-start.9 = (bf16[256,1024]{1,0:T(8,128)(2,1)S(1)}, bf16[256,1024]{1,0:T(8,128)(2,1)S(1)}, u32[]{:S(2)}, u32[]{:S(2)}) collective-permute-start(bf16[256,1024]{1,0:T(8,128)(2,1)S(1)} %collective-permute-done.3.rows_ref), channel_id=1, source_target_pairs={{4,12},{12,20},{20,28},{28,24},{24,16},{16,8},{8,0},{0,4},{5,13},{... | collective-permute-start | bytes 1572872 | tf_op jit(solution)/shard_map/ppermute | solution.py:624
  32.9 13.2 %collective-permute-start.10 = (bf16[256,1024]{1,0:T(8,128)(2,1)S(1)}, bf16[256,1024]{1,0:T(8,128)(2,1)S(1)}, u32[]{:S(2)}, u32[]{:S(2)}) collective-permute-start(bf16[256,1024]{1,0:T(8,128)(2,1)S(1)} %collective-permute-done.4.rows_ref), channel_id=1, source_target_pairs={{4,0},{12,4},{20,12},{28,20},{24,28},{16,24},{8,16},{0,8},{5,1},{1... | collective-permute-start | bytes 1572872 | tf_op jit(solution)/shard_map/ppermute | solution.py:624
  33.4 19.8 %collective-permute-start.13 = (bf16[256,1408]{1,0:T(8,128)(2,1)S(1)}, bf16[256,1408]{1,0:T(8,128)(2,1)S(1)}, u32[]{:S(2)}, u32[]{:S(2)}) collective-permute-start(bf16[256,1408]{1,0:T(8,128)(2,1)S(1)} %get-tuple-element.307), channel_id=1, source_target_pairs={{0,3},{1,2},{2,1},{3,0},{4,7},{5,6},{6,5},{7,4},{8,11},{9,10},{10,... | collective-permute-start | bytes 2162696 | tf_op jit(solution)/shard_map/ppermute | solution.py:734
  48.3 23.0 %collective-permute-start.15 = (bf16[256,1024]{1,0:T(8,128)(2,1)S(1)}, bf16[256,1024]{1,0:T(8,128)(2,1)S(1)}, u32[]{:S(2)}, u32[]{:S(2)}) collective-permute-start(bf16[256,1024]{1,0:T(8,128)(2,1)S(1)} %copy-done.9), channel_id=1, source_target_pairs={{0,1},{1,0},{2,3},{3,2},{4,5},{5,4},{6,7},{7,6},{8,9},{9,8},{10,11... | collective-permute-start | bytes 1572872 | tf_op jit(solution)/shard_map/ppermute | solution.py:700
  55.3 16.0 %collective-permute-start.14 = (bf16[256,1024]{1,0:T(8,128)(2,1)S(1)}, bf16[256,1024]{1,0:T(8,128)(2,1)S(1)}, u32[]{:S(2)}, u32[]{:S(2)}) collective-permute-start(bf16[256,1024]{1,0:T(8,128)(2,1)S(1)} %copy-done.9), channel_id=1, source_target_pairs={{0,2},{1,3},{2,0},{3,1},{4,6},{5,7},{6,4},{7,5},{8,10},{9,11},{10,... | collective-permute-start | bytes 1572872 | tf_op jit(solution)/shard_map/ppermute | solution.py:704
  75.6 19.5 %collective-permute-start.23 = (bf16[256,1024]{1,0:T(8,128)(2,1)S(1)}, bf16[256,1024]{1,0:T(8,128)(2,1)S(1)}, u32[]{:S(2)}, u32[]{:S(2)}) collective-permute-start(bf16[256,1024]{1,0:T(8,128)(2,1)S(1)} %collective-permute-done.14.refs_10_.refs_4_), channel_id=1, source_target_pairs={{0,1},{1,0},{2,3},{3,2},{4,5},{5,4},{6,7},{7,6},{8,9},{9,8},{10,11... | collective-permute-start | bytes 1572872 | tf_op jit(solution)/shard_map/ppermute | solution.py:700
  75.6 21.0 %collective-permute-start.24 = (bf16[256,1024]{1,0:T(8,128)(2,1)S(1)}, bf16[256,1024]{1,0:T(8,128)(2,1)S(1)}, u32[]{:S(2)}, u32[]{:S(2)}) collective-permute-start(bf16[256,1024]{1,0:T(8,128)(2,1)S(1)} %copy-done.6), channel_id=1, source_target_pairs={{0,2},{1,3},{2,0},{3,1},{4,6},{5,7},{6,4},{7,5},{8,10},{9,11},{10,... | collective-permute-start | bytes 1572872 | tf_op jit(solution)/shard_map/ppermute | solution.py:704
  79.8 9.4 %collective-permute-start.18 = (bf16[256,128]{1,0:T(8,128)(2,1)S(1)}, bf16[256,128]{1,0:T(8,128)(2,1)S(1)}, u32[]{:S(2)}, u32[]{:S(2)}) collective-permute-start(bf16[256,128]{1,0:T(8,128)(2,1)S(1)} %get-tuple-element.335), channel_id=1, source_target_pairs={{4,16},{12,8},{20,0},{28,4},{24,12},{16,20},{8,28},{0,24},{5,17},{... | collective-permute-start | bytes 196616 | tf_op jit(solution)/shard_map/ppermute | solution.py:624
  97.2 14.7 %collective-permute-start.27 = (bf16[256,1024]{1,0:T(8,128)(2,1)S(1)}, bf16[256,1024]{1,0:T(8,128)(2,1)S(1)}, u32[]{:S(2)}, u32[]{:S(2)}) collective-permute-start(bf16[256,1024]{1,0:T(8,128)(2,1)S(1)} %get-tuple-element.348.refs_0_), channel_id=1, source_target_pairs={{0,2},{1,3},{2,0},{3,1},{4,6},{5,7},{6,4},{7,5},{8,10},{9,11},{10,... | collective-permute-start | bytes 1572872 | tf_op jit(solution)/shard_map/ppermute | solution.py:704
  99.8 12.7 %collective-permute-start.30 = (bf16[256,1024]{1,0:T(8,128)(2,1)S(1)}, bf16[256,1024]{1,0:T(8,128)(2,1)S(1)}, u32[]{:S(2)}, u32[]{:S(2)}) collective-permute-start(bf16[256,1024]{1,0:T(8,128)(2,1)S(1)} %collective-permute-done.24.refs_2_.refs_6_), channel_id=1, source_target_pairs={{0,1},{1,0},{2,3},{3,2},{4,5},{5,4},{6,7},{7,6},{8,9},{9,8},{10,11... | collective-permute-start | bytes 1572872 | tf_op jit(solution)/shard_map/ppermute | solution.py:700
  111.9 9.5 %collective-permute-start.33 = (bf16[256,1024]{1,0:T(8,128)(2,1)S(1)}, bf16[256,1024]{1,0:T(8,128)(2,1)S(1)}, u32[]{:S(2)}, u32[]{:S(2)}) collective-permute-start(bf16[256,1024]{1,0:T(8,128)(2,1)S(1)} %get-tuple-element.369), channel_id=1, source_target_pairs={{0,1},{1,0},{2,3},{3,2},{4,5},{5,4},{6,7},{7,6},{8,9},{9,8},{10,11... | collective-permute-start | bytes 1572872 | tf_op jit(solution)/shard_map/ppermute | solution.py:700
  123.4 14.0 %collective-permute-start.37 = (bf16[256,1024]{1,0:T(8,128)(2,1)S(1)}, bf16[256,1024]{1,0:T(8,128)(2,1)S(1)}, u32[]{:S(2)}, u32[]{:S(2)}) collective-permute-start(bf16[256,1024]{1,0:T(8,128)(2,1)S(1)} %add_convert_fusion.9), channel_id=1, source_target_pairs={{0,2},{1,3},{2,0},{3,1},{4,6},{5,7},{6,4},{7,5},{8,10},{9,11},{10,... | collective-permute-start | bytes 1572872 | tf_op jit(solution)/shard_map/ppermute | solution.py:704
  141.5 21.9 %collective-permute-start.45 = (bf16[8,256,128]{2,1,0:T(8,128)(2,1)S(1)}, bf16[8,256,128]{2,1,0:T(8,128)(2,1)S(1)}, u32[]{:S(2)}, u32[]{:S(2)}) collective-permute-start(bf16[8,256,128]{2,1,0:T(8,128)(2,1)S(1)} %get-tuple-element.398), channel_id=1, source_target_pairs={{0,1},{1,0},{2,3},{3,2},{4,5},{5,4},{6,7},{7,6},{8,9},{9,8},{10,11... | collective-permute-start | bytes 1572872 | tf_op jit(solution)/shard_map/ppermute | solution.py:700
  143.6 23.0 %collective-permute-start.47 = (bf16[8,256,128]{2,1,0:T(8,128)(2,1)S(1)}, bf16[8,256,128]{2,1,0:T(8,128)(2,1)S(1)}, u32[]{:S(2)}, u32[]{:S(2)}) collective-permute-start(bf16[8,256,128]{2,1,0:T(8,128)(2,1)S(1)} %add_convert_fusion.7), channel_id=1, source_target_pairs={{0,2},{1,3},{2,0},{3,1},{4,6},{5,7},{6,4},{7,5},{8,10},{9,11},{10,... | collective-permute-start | bytes 1572872 | tf_op jit(solution)/shard_map/ppermute | solution.py:704
  154.7 12.2 %collective-permute-start.40 = (bf16[256,128]{1,0:T(8,128)(2,1)S(1)}, bf16[256,128]{1,0:T(8,128)(2,1)S(1)}, u32[]{:S(2)}, u32[]{:S(2)}) collective-permute-start(bf16[256,128]{1,0:T(8,128)(2,1)S(1)} %get-tuple-element.391), channel_id=1, source_target_pairs={{4,16},{12,8},{20,0},{28,4},{24,12},{16,20},{8,28},{0,24},{5,17},{... | collective-permute-start | bytes 196616 | tf_op jit(solution)/shard_map/ppermute | solution.py:624
  156.4 10.5 %collective-permute-start.41 = (bf16[256,128]{1,0:T(8,128)(2,1)S(1)}, bf16[256,128]{1,0:T(8,128)(2,1)S(1)}, u32[]{:S(2)}, u32[]{:S(2)}) collective-permute-start(bf16[256,128]{1,0:T(8,128)(2,1)S(1)} %get-tuple-element.392), channel_id=1, source_target_pairs={{4,24},{12,16},{20,8},{28,0},{24,4},{16,12},{8,20},{0,28},{5,25},{... | collective-permute-start | bytes 196616 | tf_op jit(solution)/shard_map/ppermute | solution.py:624
  171.8 21.3 %collective-permute-start.48 = (bf16[192,1408]{1,0:T(8,128)(2,1)S(1)}, bf16[192,1408]{1,0:T(8,128)(2,1)S(1)}, u32[]{:S(2)}, u32[]{:S(2)}) collective-permute-start(bf16[192,1408]{1,0:T(8,128)(2,1)S(1)} %add_convert_fusion.5), channel_id=1, source_target_pairs={{4,12},{12,20},{20,28},{28,24},{24,16},{16,8},{8,0},{0,4},{5,13},{... | collective-permute-start | bytes 1622024 | tf_op jit(solution)/shard_map/ppermute | solution.py:624
  172.4 20.7 %collective-permute-start.49 = (bf16[192,1408]{1,0:T(8,128)(2,1)S(1)}, bf16[192,1408]{1,0:T(8,128)(2,1)S(1)}, u32[]{:S(2)}, u32[]{:S(2)}) collective-permute-start(bf16[192,1408]{1,0:T(8,128)(2,1)S(1)} %add_convert_fusion.4), channel_id=1, source_target_pairs={{4,0},{12,4},{20,12},{28,20},{24,28},{16,24},{8,16},{0,8},{5,1},{1... | collective-permute-start | bytes 1622024 | tf_op jit(solution)/shard_map/ppermute | solution.py:624
  193.4 9.4 %collective-permute-start.50 = (bf16[192,1408]{1,0:T(8,128)(2,1)S(1)}, bf16[192,1408]{1,0:T(8,128)(2,1)S(1)}, u32[]{:S(2)}, u32[]{:S(2)}) collective-permute-start(bf16[192,1408]{1,0:T(8,128)(2,1)S(1)} %add_convert_fusion.3), channel_id=1, source_target_pairs={{4,12},{12,20},{20,28},{28,24},{24,16},{16,8},{8,0},{0,4},{5,13},{... | collective-permute-start | bytes 1622024 | tf_op jit(solution)/shard_map/ppermute | solution.py:624
  194.0 9.4 %collective-permute-start.51 = (bf16[192,1408]{1,0:T(8,128)(2,1)S(1)}, bf16[192,1408]{1,0:T(8,128)(2,1)S(1)}, u32[]{:S(2)}, u32[]{:S(2)}) collective-permute-start(bf16[192,1408]{1,0:T(8,128)(2,1)S(1)} %add_convert_fusion.2), channel_id=1, source_target_pairs={{4,0},{12,4},{20,12},{28,20},{24,28},{16,24},{8,16},{0,8},{5,1},{1... | collective-permute-start | bytes 1622024 | tf_op jit(solution)/shard_map/ppermute | solution.py:624
  204.6 50.8 %all-to-all-start = ((bf16[8,256,512]{2,1,0:T(8,128)(2,1)}), bf16[8,256,512]{2,1,0:T(8,128)(2,1)S(1)}, u32[]{:S(2)}, u32[]{:S(2)}) async-start(bf16[8,256,512]{2,1,0:T(8,128)(2,1)} %attention_backward.1.refs_9_), calls=%async_computation | async-start | bytes 4194304 | tf_op jit(solution)/shard_map/all_to_all | solution.py:696
  208.4 29.6 %collective-permute-start.65 = (bf16[256,3072]{1,0:T(8,128)(2,1)}, bf16[256,3072]{1,0:T(8,128)(2,1)}, u32[]{:S(2)}, u32[]{:S(2)}) collective-permute-start(bf16[256,3072]{1,0:T(8,128)(2,1)} %w_qkv_ref.1), channel_id=1, source_target_pairs={{0,2},{1,3},{2,0},{3,1},{4,6},{5,7},{6,4},{7,5},{8,10},{9,11},{10,... | collective-permute-start | bytes 4718600 | tf_op jit(solution)/shard_map/ppermute | solution.py:704
  208.5 36.2 %collective-permute-start.52 = (bf16[192,1408]{1,0:T(8,128)(2,1)}, bf16[192,1408]{1,0:T(8,128)(2,1)S(1)}, u32[]{:S(2)}, u32[]{:S(2)}) collective-permute-start(bf16[192,1408]{1,0:T(8,128)(2,1)} %get-tuple-element.458), channel_id=1, source_target_pairs={{4,12},{12,20},{20,28},{28,24},{24,16},{16,8},{8,0},{0,4},{5,13},{... | collective-permute-start | bytes 1622024 | tf_op jit(solution)/shard_map/ppermute | solution.py:624
  210.5 38.2 %collective-permute-start.53 = (bf16[192,1408]{1,0:T(8,128)(2,1)}, bf16[192,1408]{1,0:T(8,128)(2,1)S(1)}, u32[]{:S(2)}, u32[]{:S(2)}) collective-permute-start(bf16[192,1408]{1,0:T(8,128)(2,1)} %get-tuple-element.459), channel_id=1, source_target_pairs={{4,0},{12,4},{20,12},{28,20},{24,28},{16,24},{8,16},{0,8},{5,1},{1... | collective-permute-start | bytes 1622024 | tf_op jit(solution)/shard_map/ppermute | solution.py:624
  210.7 86.4 %collective-permute-start.64 = (bf16[256,3072]{1,0:T(8,128)(2,1)}, bf16[256,3072]{1,0:T(8,128)(2,1)}, u32[]{:S(2)}, u32[]{:S(2)}) collective-permute-start(bf16[256,3072]{1,0:T(8,128)(2,1)} %w_qkv_ref.1), channel_id=1, source_target_pairs={{0,1},{1,0},{2,3},{3,2},{4,5},{5,4},{6,7},{7,6},{8,9},{9,8},{10,11... | collective-permute-start | bytes 4718600 | tf_op jit(solution)/shard_map/ppermute | solution.py:700
  212.2 40.0 %collective-permute-start.57 = (bf16[256,384]{1,0:T(8,128)(2,1)}, bf16[256,384]{1,0:T(8,128)(2,1)S(1)}, u32[]{:S(2)}, u32[]{:S(2)}) collective-permute-start(bf16[256,384]{1,0:T(8,128)(2,1)} %copy-done.32), channel_id=1, source_target_pairs={{0,1},{1,0},{2,3},{3,2},{4,5},{5,4},{6,7},{7,6},{8,9},{9,8},{10,11... | collective-permute-start | bytes 589832 | tf_op jit(solution)/shard_map/ppermute | solution.py:700
  238.1 59.4 %collective-permute-start.66 = (bf16[256,3072]{1,0:T(8,128)(2,1)}, bf16[256,3072]{1,0:T(8,128)(2,1)}, u32[]{:S(2)}, u32[]{:S(2)}) collective-permute-start(bf16[256,3072]{1,0:T(8,128)(2,1)} %collective-permute-done.65.refs_2_), channel_id=1, source_target_pairs={{0,1},{1,0},{2,3},{3,2},{4,5},{5,4},{6,7},{7,6},{8,9},{9,8},{10,11... | collective-permute-start | bytes 4718600 | tf_op jit(solution)/shard_map/ppermute | solution.py:700
  260.1 27.3 %collective-permute-start.61 = (bf16[192,1408]{1,0:T(8,128)(2,1)S(1)}, bf16[192,1408]{1,0:T(8,128)(2,1)S(1)}, u32[]{:S(2)}, u32[]{:S(2)}) collective-permute-start(bf16[192,1408]{1,0:T(8,128)(2,1)S(1)} %pack.1.refs_0_), channel_id=1, source_target_pairs={{4,0},{12,4},{20,12},{28,20},{24,28},{16,24},{8,16},{0,8},{5,1},{1... | collective-permute-start | bytes 1622024 | tf_op jit(solution)/shard_map/ppermute | solution.py:624
  274.7 14.0 %collective-permute-start.60 = (bf16[192,1408]{1,0:T(8,128)(2,1)S(1)}, bf16[192,1408]{1,0:T(8,128)(2,1)S(1)}, u32[]{:S(2)}, u32[]{:S(2)}) collective-permute-start(bf16[192,1408]{1,0:T(8,128)(2,1)S(1)} %pack.1.refs_0_), channel_id=1, source_target_pairs={{4,12},{12,20},{20,28},{28,24},{24,16},{16,8},{8,0},{0,4},{5,13},{... | collective-permute-start | bytes 1622024 | tf_op jit(solution)/shard_map/ppermute | solution.py:624
  274.7 17.4 %collective-permute-start.72 = (bf16[256,512]{1,0:T(8,128)(2,1)S(1)}, bf16[256,512]{1,0:T(8,128)(2,1)S(1)}, u32[]{:S(2)}, u32[]{:S(2)}) collective-permute-start(bf16[256,512]{1,0:T(8,128)(2,1)S(1)} %join.1.refs_9_), channel_id=1, source_target_pairs={{4,0},{12,4},{20,12},{28,20},{24,28},{16,24},{8,16},{0,8},{5,1},{1... | collective-permute-start | bytes 786440 | tf_op jit(solution)/shard_map/ppermute | solution.py:624
  287.4 9.7 %collective-permute-start.71 = (bf16[256,512]{1,0:T(8,128)(2,1)S(1)}, bf16[256,512]{1,0:T(8,128)(2,1)S(1)}, u32[]{:S(2)}, u32[]{:S(2)}) collective-permute-start(bf16[256,512]{1,0:T(8,128)(2,1)S(1)} %join.1.refs_9_), channel_id=1, source_target_pairs={{4,12},{12,20},{20,28},{28,24},{24,16},{16,8},{8,0},{0,4},{5,13},{... | collective-permute-start | bytes 786440 | tf_op jit(solution)/shard_map/ppermute | solution.py:624
  288.7 24.2 %collective-permute-start.62 = (bf16[192,1408]{1,0:T(8,128)(2,1)S(1)}, bf16[192,1408]{1,0:T(8,128)(2,1)S(1)}, u32[]{:S(2)}, u32[]{:S(2)}) collective-permute-start(bf16[192,1408]{1,0:T(8,128)(2,1)S(1)} %collective-permute-done.60.refs_8_), channel_id=1, source_target_pairs={{4,12},{12,20},{20,28},{28,24},{24,16},{16,8},{8,0},{0,4},{5,13},{... | collective-permute-start | bytes 1622024 | tf_op jit(solution)/shard_map/ppermute | solution.py:624
  292.1 20.8 %collective-permute-start.63 = (bf16[192,1408]{1,0:T(8,128)(2,1)S(1)}, bf16[192,1408]{1,0:T(8,128)(2,1)S(1)}, u32[]{:S(2)}, u32[]{:S(2)}) collective-permute-start(bf16[192,1408]{1,0:T(8,128)(2,1)S(1)} %collective-permute-done.61.refs_1_), channel_id=1, source_target_pairs={{4,0},{12,4},{20,12},{28,20},{24,28},{16,24},{8,16},{0,8},{5,1},{1... | collective-permute-start | bytes 1622024 | tf_op jit(solution)/shard_map/ppermute | solution.py:624
  297.1 17.9 %collective-permute-start.31 = (bf16[256,1024]{1,0:T(8,128)(2,1)S(1)}, bf16[256,1024]{1,0:T(8,128)(2,1)S(1)}, u32[]{:S(2)}, u32[]{:S(2)}) collective-permute-start(bf16[256,1024]{1,0:T(8,128)(2,1)S(1)} %copy-done.31), channel_id=1, source_target_pairs={{0,1},{1,0},{2,3},{3,2},{4,5},{5,4},{6,7},{7,6},{8,9},{9,8},{10,11... | collective-permute-start | bytes 1572872 | tf_op jit(solution)/shard_map/ppermute | solution.py:700
  297.1 14.9 %collective-permute-start.73 = (bf16[256,512]{1,0:T(8,128)(2,1)S(1)}, bf16[256,512]{1,0:T(8,128)(2,1)S(1)}, u32[]{:S(2)}, u32[]{:S(2)}) collective-permute-start(bf16[256,512]{1,0:T(8,128)(2,1)S(1)} %collective-permute-done.71.refs_17_), channel_id=1, source_target_pairs={{4,12},{12,20},{20,28},{28,24},{24,16},{16,8},{8,0},{0,4},{5,13},{... | collective-permute-start | bytes 786440 | tf_op jit(solution)/shard_map/ppermute | solution.py:624
  297.5 14.5 %collective-permute-start.74 = (bf16[256,512]{1,0:T(8,128)(2,1)S(1)}, bf16[256,512]{1,0:T(8,128)(2,1)S(1)}, u32[]{:S(2)}, u32[]{:S(2)}) collective-permute-start(bf16[256,512]{1,0:T(8,128)(2,1)S(1)} %collective-permute-done.72.refs_10_), channel_id=1, source_target_pairs={{4,0},{12,4},{20,12},{28,20},{24,28},{16,24},{8,16},{0,8},{5,1},{1... | collective-permute-start | bytes 786440 | tf_op jit(solution)/shard_map/ppermute | solution.py:624
  312.0 24.9 %collective-permute-start.28 = (bf16[256,1024]{1,0:T(8,128)(2,1)S(1)}, bf16[256,1024]{1,0:T(8,128)(2,1)S(1)}, u32[]{:S(2)}, u32[]{:S(2)}) collective-permute-start(bf16[256,1024]{1,0:T(8,128)(2,1)S(1)} %copy-done.29), channel_id=1, source_target_pairs={{0,1},{1,0},{2,3},{3,2},{4,5},{5,4},{6,7},{7,6},{8,9},{9,8},{10,11... | collective-permute-start | bytes 1572872 | tf_op jit(solution)/shard_map/ppermute | solution.py:700
  312.9 21.8 %collective-permute-start.67 = (bf16[192,1408]{1,0:T(8,128)(2,1)S(1)}, bf16[192,1408]{1,0:T(8,128)(2,1)S(1)}, u32[]{:S(2)}, u32[]{:S(2)}) collective-permute-start(bf16[192,1408]{1,0:T(8,128)(2,1)S(1)} %collective-permute-done.62.refs_7_), channel_id=1, source_target_pairs={{4,12},{12,20},{20,28},{28,24},{24,16},{16,8},{8,0},{0,4},{5,13},{... | collective-permute-start | bytes 1622024 | tf_op jit(solution)/shard_map/ppermute | solution.py:624
  314.4 21.8 %collective-permute-start.68 = (bf16[192,1408]{1,0:T(8,128)(2,1)S(1)}, bf16[192,1408]{1,0:T(8,128)(2,1)S(1)}, u32[]{:S(2)}, u32[]{:S(2)}) collective-permute-start(bf16[192,1408]{1,0:T(8,128)(2,1)S(1)} %collective-permute-done.63.refs_2_), channel_id=1, source_target_pairs={{4,0},{12,4},{20,12},{28,20},{24,28},{16,24},{8,16},{0,8},{5,1},{1... | collective-permute-start | bytes 1622024 | tf_op jit(solution)/shard_map/ppermute | solution.py:624
  315.2 23.1 %collective-permute-start.32 = (bf16[256,1024]{1,0:T(8,128)(2,1)S(1)}, bf16[256,1024]{1,0:T(8,128)(2,1)S(1)}, u32[]{:S(2)}, u32[]{:S(2)}) collective-permute-start(bf16[256,1024]{1,0:T(8,128)(2,1)S(1)} %add_convert_fusion.12), channel_id=1, source_target_pairs={{0,2},{1,3},{2,0},{3,1},{4,6},{5,7},{6,4},{7,5},{8,10},{9,11},{10,... | collective-permute-start | bytes 1572872 | tf_op jit(solution)/shard_map/ppermute | solution.py:704
  321.1 12.9 %collective-permute-start.76 = (bf16[256,512]{1,0:T(8,128)(2,1)S(1)}, bf16[256,512]{1,0:T(8,128)(2,1)S(1)}, u32[]{:S(2)}, u32[]{:S(2)}) collective-permute-start(bf16[256,512]{1,0:T(8,128)(2,1)S(1)} %collective-permute-done.74.refs_11_), channel_id=1, source_target_pairs={{4,0},{12,4},{20,12},{28,20},{24,28},{16,24},{8,16},{0,8},{5,1},{1... | collective-permute-start | bytes 786440 | tf_op jit(solution)/shard_map/ppermute | solution.py:624
  (66 other events, 601.9 us)

commit v2 on v1

--- a/solution.py
+++ b/solution.py
@@ -302,11 +302,18 @@
     outs, parts_ref = refs[:-1], refs[-1]
     count = len(outs)
     hidden = w_ref.shape[1] // (2 * count)
-    for part in range(count):
-        parts_ref[part, :, 0:hidden] = w_ref[:, part * hidden : (part + 1) * hidden]
-        parts_ref[part, :, hidden:] = w_ref[:, (count + part) * hidden : (count + part + 1) * hidden]
-    for slot in range(count):
-        outs[slot][...] = parts_ref[table[0, n + slot]]
+    step = w_ref.shape[0] // 4
+
+    def one(i, unused):
+        lines = at(i * step, step)
+        for part in range(count):
+            parts_ref[part, lines, 0:hidden] = w_ref[lines, part * hidden : (part + 1) * hidden]
+            parts_ref[part, lines, hidden:] = w_ref[lines, (count + part) * hidden : (count + part + 1) * hidden]
+        for slot in range(count):
+            outs[slot][lines, :] = parts_ref[table[0, n + slot], lines, :]
+        return 0
+
+    lax.fori_loop(0, 4, one, 0)
 
 
 def project_kernel(n, table, rows_ref, *refs):
@@ -477,8 +484,8 @@
 
 
 def tail_kernel(n, count, table, tokens_ref, grad_ref, parts_ref, *refs):
-    weights, slices = refs[:count], refs[count : 2 * count]
-    out_ref, gain_ref, sum_ref, grads_ref = refs[2 * count :]
+    weights, slices = refs[: 2 * count], refs[2 * count : 3 * count]
+    out_ref, gain_ref, sum_ref, grads_ref = refs[3 * count :]
     own_width = parts_ref.shape[2] // 4
     width = tokens_ref.shape[1]
     shard = width // count
@@ -493,7 +500,8 @@
         lanes = at(part * width, width)
         for slot in range(count):
             place = at(table[0, n + slot] * shard, shard)
-            sum_ref[:, place] += nt(grads_ref[:, lanes], weights[slot][:, lanes])
+            both = jnp.concatenate([weights[2 * slot + piece][:, lanes] for piece in range(2)], axis=0)
+            sum_ref[:, place] += nt(grads_ref[:, lanes], both)
         return 0
 
     lax.fori_loop(0, 3, one, 0)
@@ -839,7 +847,7 @@
     near_out = partner(w_out, fsdp)
     out_slots, outs, near_out, gate_pieces = tie(out_slots, outs, near_out, gate_pieces)
     attn_parts = ring_exchange(out_slots, ring)
-    later_cot, outs, unused = tie(cotangent, outs, attn_parts[-1])
+    later_cot, unused = tie(cotangent, out_slots[0])
     cots = far_gather(later_cot, fsdp)
     outs = [outs[0], near_out] + near_gather(outs[1:], fsdp)
     resid, ffn_in = call(
@@ -907,7 +915,12 @@
     grad_qkv = attention_backward(
         table, lengths, block_order, qkv, grad_slots, part_out, out_t, log_total, own_heads, depth, TILE
     )
-    (grad_qkv,) = ffn_sums.advance(grad_qkv)
+    first_half, second_half = w_qkv[: shard // 2], w_qkv[shard // 2 :]
+    first_half, unused = tie(first_half, part_out)
+    first_half = far_gather(first_half, fsdp)
+    grad_qkv, first_half = ffn_sums.advance(grad_qkv, first_half)
+    second_half, unused = tie(second_half, grad_qkv)
+    second_half = far_gather(second_half, fsdp)
     qkv_sides = call(
         "qkv_weights", functools.partial(qkv_weight_kernel, len(attn_slots), ctx, fsdp),
         [shape((shard, 3 * own_width))] * fsdp, [table] + attn_slots + [grad_qkv],
@@ -916,13 +929,13 @@
     )
     if ffn_sums.step > 1:
         grad_qkv, qkv_sides = ffn_sums.advance(grad_qkv, qkv_sides)
-    grad_back = exchange(grad_qkv)
-    later_qkv, unused = tie(w_qkv, qkv_sides[0])
-    qkv_nears = far_gather(later_qkv, fsdp)
     qkv_sum = far_scatter(near_scatter(qkv_sides, fsdp), fsdp)
 
     qkv_sum = ffn_sums.advance(qkv_sum)[0] if ffn_sums.step > 1 else qkv_sum
     own_sum, ffn_up, ffn_down = ffn_sums.sums()
+    ffn_up, ffn_down, grad_qkv, qkv_sum, second_half = tie(ffn_up, ffn_down, grad_qkv, qkv_sum, second_half)
+    first_half, second_half = near_gather(first_half, fsdp), near_gather(second_half, fsdp)
+    grad_back = exchange(grad_qkv)
     *gate_sides, rest = call(
         "cut", functools.partial(cut_kernel, ctx),
         [shape((sub, 2 * hidden))] * fsdp + [shape((lines // 2, 2 * hidden))],
@@ -930,28 +943,27 @@
         scratch=[pltpu.VMEM((lines + lines // 2, 2 * hidden), jnp.bfloat16)],
         time=3,
     )
+    gate_sides = side_exchange(gate_sides, fsdp)
+    (packed,) = call(
+        "pack", functools.partial(pack_kernel, ctx),
+        [shape((lines + lines // 2, 2 * hidden))], [table, rest] + gate_sides,
+        time=2,
+    )
+    ffn_going = Gather(packed, ring)
     (joined,) = call(
         "join", functools.partial(join_kernel, len(qkv_sum)),
         [shape((shard, 4 * own_width))], [table] + qkv_sum + [grad_back],
         time=2.5,
     )
-    gate_sides = side_exchange(gate_sides, fsdp)
-    gate_sides, joined = tie(gate_sides, joined)
-    (packed,) = call(
-        "pack", functools.partial(pack_kernel, ctx),
-        [shape((lines + lines // 2, 2 * hidden))], [table, rest] + gate_sides,
-        time=2,
-    )
-    ffn_going = Gather(packed, ring)
+    (joined,) = ffn_going.advance(joined)
     attn_going = Gather(joined, ring)
-    weights = near_gather(qkv_nears, fsdp)
+    weights = [piece for pair in zip(first_half, second_half) for piece in pair]
     (grad_tokens,) = call(
         "tail", functools.partial(tail_kernel, ctx, fsdp),
         [shape((rows, width))], [table, tokens, grad_resid, grad_back] + weights + slices,
         scratch=[gain_scratch, pltpu.VMEM((rows, width), f32), pltpu.VMEM((rows, 3 * width), jnp.bfloat16)],
         time=8,
     )
-    ffn_going.advance()
     (grad_tokens,) = ffn_going.advance(grad_tokens)
     results = [
         shape((shard, 2 * hidden * fsdp), f32), shape((hidden, width), f32),

time: 355 us -> 350 us (0.986)
  starting transfers between devices: 92.8 us -> 85.4 us
  waiting for transfers between devices: 145 us -> 151 us
  local copies, waits for them, and re-layouts: 11.4 us -> 17.3 us
  Pallas kernels: 96.7 us -> 91.4 us
    ppermute x9 -> x10, waiting for transfers between devices: 33.9 us -> 13.1 us  [chip_shift(): lax.ppermute(value, 'fsdp', [(i, (i + 2 * step) % count) for i in range(c...]
    ppermute x46, waiting for transfers between devices: 101 us -> 119 us  [ring_shift(): lax.ppermute(value, 'ctx', [(ring[i], ring[(i + step) % count]) for i in...]
    ppermute x46, starting transfers between devices: 74.8 us -> 67.6 us  [ring_shift(): lax.ppermute(value, 'ctx', [(ring[i], ring[(i + step) % count]) for i in...]
    unnamed x68 -> x72, local copies, waits for them, and re-layouts: 9.27 us -> 13.9 us
    all_to_all x1, waiting for transfers between devices: 0.01 us -> 4.39 us  [exchange(): return lax.all_to_all(array, 'ctx', 0, 0, tiled=True)]
    ppermute x18 -> x20, waiting for transfers between devices: 8.3 us -> 9.03 us  [partner(): return lax.ppermute(value, 'fsdp', [(i, i ^ 1) for i in range(count)])]
    ppermute x9 -> x10, starting transfers between devices: 9.61 us -> 8.89 us  [chip_shift(): lax.ppermute(value, 'fsdp', [(i, (i + 2 * step) % count) for i in range(c...]
  transfers between devices with their start and end apart: 80 -> 83, of which waited for: 44 -> 44; matrix products, arithmetic and copies ran while one was open for 2% -> 2% of each run, Pallas kernels for 24% -> 22%
where the time goes in v2:
time: 350 us
  waiting for transfers between devices  151 us (43%)
  Pallas kernels  91.4 us (26%)
  starting transfers between devices  85.4 us (24%)
  local copies, waits for them, and re-layouts  17.3 us (5%)
  other arithmetic  3.57 us (1%)
    ppermute x46, waiting for transfers between devices, ring_shift(): lax.ppermute(value, 'ctx', [(ring[i], ring[(i + step) % count]) for i in...  119 us
    ppermute x46, starting transfers between devices, ring_shift(): lax.ppermute(value, 'ctx', [(ring[i], ring[(i + step) % count]) for i in...  67.6 us
    pallas_call x22, Pallas kernels, call(): pl.pallas_call(kernel, out_shape=list(out), in_specs=[SM] + [VM] * (len(i...  53.5 us
    pallas_call x1, Pallas kernels, attention_backward(): pl.pallas_call(functools.partial(bwd_kernel, meta), out_shape=jax.ShapeDt...  16.4 us
    unnamed x72, local copies, waits for them, and re-layouts  13.9 us
    ppermute x10, waiting for transfers between devices, chip_shift(): lax.ppermute(value, 'fsdp', [(i, (i + 2 * step) % count) for i in range(c...  13.1 us
    pallas_call x1, Pallas kernels, attention_forward(): pl.pallas_call(functools.partial(fwd_kernel, meta), out_shape=[jax.ShapeD...  12.8 us
    ppermute x20, waiting for transfers between devices, partner(): return lax.ppermute(value, 'fsdp', [(i, i ^ 1) for i in range(count)])  9.03 us
  transfers between devices with their start and end apart: 83, of which 44 were waited for; matrix products, arithmetic and copies ran while one was open for 2% of the time, Pallas kernels for 22%

profile of v2, /device:TPU:0, one launch (start us, length us, event | category | flops | bytes accessed | tf_op | source)
XLA Modules:
  0.0 350.3 jit_solution(9155285749708000467)
XLA Ops:
  0.6 3.0 collective-permute-start
  7.8 1.9 collective-permute-start.2
  9.7 1.8 copy-done.3
  13.3 2.6 collective-permute-done.rows_ref
  25.6 4.1 %collective-permute-done.3.rows_ref = bf16[256,1024]{1,0:T(8,128)(2,1)S(1)} collective-permute-done((bf16[256,1024]{1,0:T(8,128)(2,1)S(1)}, bf16[256,1024]{1,0:T(8,128)(2,1)S(1)}, u32[]{:S(2)}, u32[]{:S(2)}) %collective-permute-start.3) | collective-permute-done | bytes 524320 | tf_op jit(solution)/shard_map/ppermute | solution.py:632
  36.0 9.1 %collective-permute-done.9.rows_ref = bf16[256,1024]{1,0:T(8,128)(2,1)S(1)} collective-permute-done((bf16[256,1024]{1,0:T(8,128)(2,1)S(1)}, bf16[256,1024]{1,0:T(8,128)(2,1)S(1)}, u32[]{:S(2)}, u32[]{:S(2)}) %collective-permute-start.9) | collective-permute-done | bytes 524320 | tf_op jit(solution)/shard_map/ppermute | solution.py:632
  50.9 2.2 collective-permute-done.11.rows_ref
  57.0 12.8 %attention_forward.1 = (bf16[256,128]{1,0:T(8,128)(2,1)S(1)}, bf16[256,128]{1,0:T(8,128)(2,1)S(1)}, bf16[256,128]{1,0:T(8,128)(2,1)S(1)}, bf16[256,128]{1,0:T(8,...) custom-call(s32[1,12]{1,0:T(1,128)S(1)} %constant_dynamic-slice_fusi, ...), custom_call_target="tpu_custom_call" | custom-call | bytes 57800000 | tf_op jit(solution)/shard_map/attention_forward/pallas_call | solution.py:205
  70.0 2.4 collective-permute-start.24
  74.5 3.4 collective-permute-start.18
  79.5 5.7 %collective-permute-start.20 = (bf16[256,128]{1,0:T(8,128)(2,1)S(1)}, bf16[256,128]{1,0:T(8,128)(2,1)S(1)}, u32[]{:S(2)}, u32[]{:S(2)}) collective-permute-start(bf16[256,128]{1,0:T(8,128)(2,1)S(1)} %get-tuple-element.343), channel_id=1, source_target_pairs={{4,28},{12,24},{20,16},{28,8},{24,0},{16,4},{8,12},{0,20},{5,29},{... | collective-permute-start | bytes 196616 | tf_op jit(solution)/shard_map/ppermute | solution.py:632
  87.4 4.7 %collective-permute-done.21.refs_6_ = bf16[256,128]{1,0:T(8,128)(2,1)S(1)} collective-permute-done((bf16[256,128]{1,0:T(8,128)(2,1)S(1)}, bf16[256,128]{1,0:T(8,128)(2,1)S(1)}, u32[]{:S(2)}, u32[]{:S(2)}) %collective-permute-start.21) | collective-permute-done | bytes 65568 | tf_op jit(solution)/shard_map/ppermute | solution.py:632
  97.3 7.5 %feed_forward.2 = (bf16[256,1024]{1,0:T(8,128)(2,1)S(1)}, bf16[256,1024]{1,0:T(8,128)(2,1)S(1)}, bf16[256,1024]{1,0:T(8,128)(2,1)S(1)}, bf16[256,1024]{1,0:T(8,1...) custom-call(s32[1,12]{1,0:T(1,128)S(1)} %constant_dynamic-slice_fusion.table, ...), custom_call_target="tpu_custom_call" | custom-call | bytes 32300000 | tf_op jit(solution)/shard_map/feed_forward/pallas_call | solution.py:259
  106.4 2.6 collective-permute-done.27.refs_0_.refs_2_
  110.9 7.4 %feed_forward.3 = (bf16[256,1024]{1,0:T(8,128)(2,1)S(1)}, bf16[256,1024]{1,0:T(8,128)(2,1)S(1)}, bf16[256,1024]{1,0:T(8,128)(2,1)S(1)}, bf16[256,1024]{1,0:T(8,1...) custom-call(s32[1,12]{1,0:T(1,128)S(1)} %constant_dynamic-slice_fusion.table, ...), custom_call_target="tpu_custom_call" | custom-call | bytes 32300000 | tf_op jit(solution)/shard_map/feed_forward/pallas_call | solution.py:259
  120.9 7.1 %feed_forward_weights.1 = (bf16[192,1408]{1,0:T(8,128)(2,1)S(1)}, bf16[192,1408]{1,0:T(8,128)(2,1)S(1)}, bf16[192,1408]{1,0:T(8,128)(2,1)S(1)}, bf16[192,1408]{1...) custom-call(s32[1,12]{1,0:T(1,128)S(1)} %constant_dynamic-slice_fusi, ...), custom_call_target="tpu_custom_call" | custom-call | bytes 40800000 | tf_op jit(solution)/shard_map/feed_forward_weights/pallas_call | solution.py:259
  128.0 6.6 %collective-permute-done.37.refs_1_ = bf16[256,1024]{1,0:T(8,128)(2,1)S(1)} collective-permute-done((bf16[256,1024]{1,0:T(8,128)(2,1)S(1)}, bf16[256,1024]{1,0:T(8,128)(2,1)S(1)}, u32[]{:S(2)}, u32[]{:S(2)}) %collective-permute-start.37) | collective-permute-done | bytes 524320 | tf_op jit(solution)/shard_map/ppermute | solution.py:712
  134.6 2.4 branch.1
  142.3 5.2 %collective-permute-done.35 = bf16[96,1408]{1,0:T(8,128)(2,1)S(1)} collective-permute-done((bf16[96,1408]{1,0:T(8,128)(2,1)S(1)}, bf16[96,1408]{1,0:T(8,128)(2,1)S(1)}, u32[]{:S(2)}, u32[]{:S(2)}) %collective-permute-start.35) | collective-permute-done | bytes 270368 | tf_op jit(solution)/shard_map/ppermute | solution.py:632
  150.7 2.5 collective-permute-start.41
  154.4 2.8 collective-permute-start.43
  157.2 3.9 %collective-permute-done.47 = bf16[8,256,128]{2,1,0:T(8,128)(2,1)S(1)} collective-permute-done((bf16[8,256,128]{2,1,0:T(8,128)(2,1)S(1)}, bf16[8,256,128]{2,1,0:T(8,128)(2,1)S(1)}, u32[]{:S(2)}, u32[]{:S(2)}) %collective-permute-start.47) | collective-permute-done | bytes 524320 | tf_op jit(solution)/shard_map/ppermute | solution.py:712
  167.8 16.4 %attention_backward.1.refs_9_ = bf16[8,256,512]{2,1,0:T(8,128)(2,1)} custom-call(s32[1,12]{1,0:T(1,128)S(1)} %constant_dynamic-slice_fusion.table, s32[1,4]{1,0:T(1,128)S(1)} %copy-done.30, s32[1,32]{1,0:T(1,128)S(1)} %copy-done.31, bf16[256,384]{1,0:T(8,128)(2,1)S(1)} %get-tuple-element.285.refs_0_, bf16[256,384]{1,0:T(8,128)(2,1)S(1)} %get-tuple-element.314.refs_1_, ...), custom_call_target="tpu_custom_call" | custom-call | bytes 61200000 | tf_op jit(solution)/shard_map/attention_backward/pallas_call | solution.py:218
  186.6 2.6 collective-permute-start.58
  189.3 4.8 %qkv_weights.1 = (bf16[256,384]{1,0:T(8,128)(2,1)S(1)}, bf16[256,384]{1,0:T(8,128)(2,1)S(1)}, bf16[256,384]{1,0:T(8,128)(2,1)S(1)}, bf16[256,384]{1,0:T(8,128)(2,1)S(1)}) custom-call(s32[1,12]{1,0:T(1,128)S(1)} %constant_dynamic-slice_fusion.table, bf16[256,1024]{1,0:T(8,128)(2,1)S(1)} %get-tuple-element.444.refs_0_, ...), custom_call_target="tpu_custom_call" | custom-call | bytes 20400000 | tf_op jit(solution)/shard_map/qkv_weights/pallas_call | solution.py:259
  194.0 5.7 %collective-permute-done.51 = bf16[192,1408]{1,0:T(8,128)(2,1)S(1)} collective-permute-done((bf16[192,1408]{1,0:T(8,128)(2,1)S(1)}, bf16[192,1408]{1,0:T(8,128)(2,1)S(1)}, u32[]{:S(2)}, u32[]{:S(2)}) %collective-permute-start.51) | collective-permute-done | bytes 540704 | tf_op jit(solution)/shard_map/ppermute | solution.py:632
  204.5 10.3 %collective-permute-done.53.up_ref = bf16[192,1408]{1,0:T(8,128)(2,1)S(1)} collective-permute-done((bf16[192,1408]{1,0:T(8,128)(2,1)S(1)}, bf16[192,1408]{1,0:T(8,128)(2,1)S(1)}, u32[]{:S(2)}, u32[]{:S(2)}) %collective-permute-start.53) | collective-permute-done | bytes 540704 | tf_op jit(solution)/shard_map/ppermute | solution.py:632
  217.6 4.1 %all-to-all-start = ((bf16[8,256,512]{2,1,0:T(8,128)(2,1)}), bf16[8,256,512]{2,1,0:T(8,128)(2,1)S(1)}, u32[]{:S(2)}, u32[]{:S(2)}) async-start(bf16[8,256,512]{2,1,0:T(8,128)(2,1)} %attention_backward.1.refs_9_), calls=%async_computation | async-start | bytes 4194304 | tf_op jit(solution)/shard_map/all_to_all | solution.py:704
  226.0 1.8 collective-permute-start.61
  227.8 3.6 %collective-permute-done.60.refs_2_ = bf16[32,1408]{1,0:T(8,128)(2,1)S(1)} collective-permute-done((bf16[32,1408]{1,0:T(8,128)(2,1)S(1)}, bf16[32,1408]{1,0:T(8,128)(2,1)S(1)}, u32[]{:S(2)}, u32[]{:S(2)}) %collective-permute-start.60) | collective-permute-done | bytes 90144 | tf_op jit(solution)/shard_map/ppermute | solution.py:742
  233.0 2.1 collective-permute-start.62
  237.1 23.0 %collective-permute-done.62.refs_8_ = bf16[192,1408]{1,0:T(8,128)(2,1)S(1)} collective-permute-done((bf16[192,1408]{1,0:T(8,128)(2,1)S(1)}, bf16[192,1408]{1,0:T(8,128)(2,1)S(1)}, u32[]{:S(2)}, u32[]{:S(2)}) %collective-permute-start.62) | collective-permute-done | bytes 540704 | tf_op jit(solution)/shard_map/ppermute | solution.py:632
  261.0 6.1 %collective-permute-done.63.refs_1_ = bf16[192,1408]{1,0:T(8,128)(2,1)} collective-permute-done((bf16[192,1408]{1,0:T(8,128)(2,1)S(1)}, bf16[192,1408]{1,0:T(8,128)(2,1)}, u32[]{:S(2)}, u32[]{:S(2)}) %collective-permute-start.63) | collective-permute-done | bytes 540704 | tf_op jit(solution)/shard_map/ppermute | solution.py:632
  267.0 4.4 %all-to-all-done.refs_2_.parts_ref = bf16[8,256,512]{2,1,0:T(8,128)(2,1)S(1)} async-done(((bf16[8,256,512]{2,1,0:T(8,128)(2,1)}), bf16[8,256,512]{2,1,0:T(8,128)(2,1)S(1)}, u32[]{:S(2)}, u32[]{:S(2)}) %all-to-all-start) | async-done | bytes 2097184 | tf_op jit(solution)/shard_map/all_to_all | solution.py:704
  274.5 10.6 %collective-permute-start.75 = (bf16[256,512]{1,0:T(8,128)(2,1)S(1)}, bf16[256,512]{1,0:T(8,128)(2,1)S(1)}, u32[]{:S(2)}, u32[]{:S(2)}) collective-permute-start(bf16[256,512]{1,0:T(8,128)(2,1)S(1)} %join.1.refs_9_), channel_id=1, source_target_pairs={{4,0},{12,4},{20,12},{28,20},{24,28},{16,24},{8,16},{0,8},{5,1},{1... | collective-permute-start | bytes 786440 | tf_op jit(solution)/shard_map/ppermute | solution.py:632
  285.8 6.4 %collective-permute-done.74.refs_17_ = bf16[256,512]{1,0:T(8,128)(2,1)S(1)} collective-permute-done((bf16[256,512]{1,0:T(8,128)(2,1)S(1)}, bf16[256,512]{1,0:T(8,128)(2,1)S(1)}, u32[]{:S(2)}, u32[]{:S(2)}) %collective-permute-start.74) | collective-permute-done | bytes 262176 | tf_op jit(solution)/shard_map/ppermute | solution.py:632
  292.2 2.1 collective-permute-start.65
  294.3 2.0 collective-permute-start.77
  296.3 7.1 %tail.1 = bf16[256,1024]{1,0:T(8,128)(2,1)} custom-call(s32[1,12]{1,0:T(1,128)S(1)} %constant_dynamic-slice_fusion.table, bf16[256,1024]{1,0:T(8,128)(2,1)S(1)} %copy-done.6, f32[256,1024]{1,0:T(8,128)S(1)} %copy-done.14, bf16[8,256,512]{2,1,0:T(8,128)(2,1)S(1)} %all-to-all-done.refs_2_.parts_ref, bf16[128,3072]{1,0:T(8,128)(2,1)} %get-tuple-element.492.refs_0_, ...), custom_call_target="tpu_custom_call" | custom-call | bytes 27200000 | tf_op jit(solution)/shard_map/tail/pallas_call | solution.py:259
  303.5 4.9 %collective-permute-done.76.refs_16_ = bf16[256,512]{1,0:T(8,128)(2,1)S(1)} collective-permute-done((bf16[256,512]{1,0:T(8,128)(2,1)S(1)}, bf16[256,512]{1,0:T(8,128)(2,1)S(1)}, u32[]{:S(2)}, u32[]{:S(2)}) %collective-permute-start.76) | collective-permute-done | bytes 262176 | tf_op jit(solution)/shard_map/ppermute | solution.py:632
  308.3 1.9 collective-permute-done.77.refs_11_
  310.5 2.3 collective-permute-start.70
  313.1 6.3 %collective-permute-done.78.refs_15_ = bf16[256,512]{1,0:T(8,128)(2,1)S(1)} collective-permute-done((bf16[256,512]{1,0:T(8,128)(2,1)S(1)}, bf16[256,512]{1,0:T(8,128)(2,1)S(1)}, u32[]{:S(2)}, u32[]{:S(2)}) %collective-permute-start.78) | collective-permute-done | bytes 262176 | tf_op jit(solution)/shard_map/ppermute | solution.py:632
  320.9 9.7 %collective-permute-done.79.refs_12_ = bf16[256,512]{1,0:T(8,128)(2,1)S(1)} collective-permute-done((bf16[256,512]{1,0:T(8,128)(2,1)S(1)}, bf16[256,512]{1,0:T(8,128)(2,1)S(1)}, u32[]{:S(2)}, u32[]{:S(2)}) %collective-permute-start.79) | collective-permute-done | bytes 262176 | tf_op jit(solution)/shard_map/ppermute | solution.py:632
  330.6 1.9 collective-permute-start.80
  332.8 1.9 collective-permute-start.72
  339.3 2.2 collective-permute-done.73.refs_5_
  341.5 8.6 %final.1 = (f32[256,5632]{1,0:T(8,128)}, f32[704,1024]{1,0:T(8,128)}, f32[256,3072]{1,0:T(8,128)}, f32[256,1024]{1,0:T(8,128)}, f32[1,256]{1,0:T(1,128)}, /*index=5*/f32[1,256]{1,0:T(1,128)}) custom-call(s32[1,12]{1,0:T(1,128)S(1)} %constant_dynamic-slice_fusion.table, bf16[256,5632]{1,0:T(8,128)(2,1)S(1)} %copy-done.4, ...), custom_call_target="tpu_custom_call" | custom-call | bytes 20400000 | tf_op jit(solution)/shard_map/final/pallas_call | solution.py:976
  (238 shorter events, 94.3 us)
Async XLA Ops:
  0.6 15.2 %collective-permute-start = (bf16[256,1024]{1,0:T(8,128)(2,1)}, bf16[256,1024]{1,0:T(8,128)(2,1)S(1)}, u32[]{:S(2)}, u32[]{:S(2)}) collective-permute-start(bf16[256,1024]{1,0:T(8,128)(2,1)} %tokens_ref.3), channel_id=1, source_target_pairs={{4,12},{12,20},{20,28},{28,24},{24,16},{16,8},{8,0},{0,4},{5,13},{... | collective-permute-start | bytes 1572872 | tf_op jit(solution)/shard_map/ppermute | solution.py:632
  3.7 13.6 %collective-permute-start.1 = (bf16[256,1024]{1,0:T(8,128)(2,1)}, bf16[256,1024]{1,0:T(8,128)(2,1)S(1)}, u32[]{:S(2)}, u32[]{:S(2)}) collective-permute-start(bf16[256,1024]{1,0:T(8,128)(2,1)} %tokens_ref.3), channel_id=1, source_target_pairs={{4,0},{12,4},{20,12},{28,20},{24,28},{16,24},{8,16},{0,8},{5,1},{1... | collective-permute-start | bytes 1572872 | tf_op jit(solution)/shard_map/ppermute | solution.py:632
  13.0 18.0 %collective-permute-start.7 = (bf16[256,1408]{1,0:T(8,128)(2,1)S(1)}, bf16[256,1408]{1,0:T(8,128)(2,1)S(1)}, u32[]{:S(2)}, u32[]{:S(2)}) collective-permute-start(bf16[256,1408]{1,0:T(8,128)(2,1)S(1)} %get-tuple-element.270), channel_id=1, source_target_pairs={{0,1},{1,0},{2,3},{3,2},{4,5},{5,4},{6,7},{7,6},{8,9},{9,8},{10,11... | collective-permute-start | bytes 2162696 | tf_op jit(solution)/shard_map/ppermute | solution.py:742
  13.1 18.6 %collective-permute-start.8 = (bf16[256,1408]{1,0:T(8,128)(2,1)S(1)}, bf16[256,1408]{1,0:T(8,128)(2,1)S(1)}, u32[]{:S(2)}, u32[]{:S(2)}) collective-permute-start(bf16[256,1408]{1,0:T(8,128)(2,1)S(1)} %get-tuple-element.271), channel_id=1, source_target_pairs={{0,2},{1,3},{2,0},{3,1},{4,6},{5,7},{6,4},{7,5},{8,10},{9,11},{10,... | collective-permute-start | bytes 2162696 | tf_op jit(solution)/shard_map/ppermute | solution.py:742
  17.3 12.5 %collective-permute-start.3 = (bf16[256,1024]{1,0:T(8,128)(2,1)S(1)}, bf16[256,1024]{1,0:T(8,128)(2,1)S(1)}, u32[]{:S(2)}, u32[]{:S(2)}) collective-permute-start(bf16[256,1024]{1,0:T(8,128)(2,1)S(1)} %collective-permute-done.rows_ref), channel_id=1, source_target_pairs={{4,12},{12,20},{20,28},{28,24},{24,16},{16,8},{8,0},{0,4},{5,13},{... | collective-permute-start | bytes 1572872 | tf_op jit(solution)/shard_map/ppermute | solution.py:632
  18.8 12.2 %collective-permute-start.4 = (bf16[256,1024]{1,0:T(8,128)(2,1)S(1)}, bf16[256,1024]{1,0:T(8,128)(2,1)S(1)}, u32[]{:S(2)}, u32[]{:S(2)}) collective-permute-start(bf16[256,1024]{1,0:T(8,128)(2,1)S(1)} %collective-permute-done.1.rows_ref), channel_id=1, source_target_pairs={{4,0},{12,4},{20,12},{28,20},{24,28},{16,24},{8,16},{0,8},{5,1},{1... | collective-permute-start | bytes 1572872 | tf_op jit(solution)/shard_map/ppermute | solution.py:632
  31.6 13.5 %collective-permute-start.9 = (bf16[256,1024]{1,0:T(8,128)(2,1)S(1)}, bf16[256,1024]{1,0:T(8,128)(2,1)S(1)}, u32[]{:S(2)}, u32[]{:S(2)}) collective-permute-start(bf16[256,1024]{1,0:T(8,128)(2,1)S(1)} %collective-permute-done.3.rows_ref), channel_id=1, source_target_pairs={{4,12},{12,20},{20,28},{28,24},{24,16},{16,8},{8,0},{0,4},{5,13},{... | collective-permute-start | bytes 1572872 | tf_op jit(solution)/shard_map/ppermute | solution.py:632
  33.1 13.2 %collective-permute-start.10 = (bf16[256,1024]{1,0:T(8,128)(2,1)S(1)}, bf16[256,1024]{1,0:T(8,128)(2,1)S(1)}, u32[]{:S(2)}, u32[]{:S(2)}) collective-permute-start(bf16[256,1024]{1,0:T(8,128)(2,1)S(1)} %collective-permute-done.4.rows_ref), channel_id=1, source_target_pairs={{4,0},{12,4},{20,12},{28,20},{24,28},{16,24},{8,16},{0,8},{5,1},{1... | collective-permute-start | bytes 1572872 | tf_op jit(solution)/shard_map/ppermute | solution.py:632
  33.7 20.8 %collective-permute-start.13 = (bf16[256,1408]{1,0:T(8,128)(2,1)S(1)}, bf16[256,1408]{1,0:T(8,128)(2,1)S(1)}, u32[]{:S(2)}, u32[]{:S(2)}) collective-permute-start(bf16[256,1408]{1,0:T(8,128)(2,1)S(1)} %get-tuple-element.313), channel_id=1, source_target_pairs={{0,3},{1,2},{2,1},{3,0},{4,7},{5,6},{6,5},{7,4},{8,11},{9,10},{10,... | collective-permute-start | bytes 2162696 | tf_op jit(solution)/shard_map/ppermute | solution.py:742
  48.5 21.3 %collective-permute-start.15 = (bf16[256,1024]{1,0:T(8,128)(2,1)S(1)}, bf16[256,1024]{1,0:T(8,128)(2,1)S(1)}, u32[]{:S(2)}, u32[]{:S(2)}) collective-permute-start(bf16[256,1024]{1,0:T(8,128)(2,1)S(1)} %copy-done.12), channel_id=1, source_target_pairs={{0,1},{1,0},{2,3},{3,2},{4,5},{5,4},{6,7},{7,6},{8,9},{9,8},{10,11... | collective-permute-start | bytes 1572872 | tf_op jit(solution)/shard_map/ppermute | solution.py:708
  56.4 13.4 %collective-permute-start.14 = (bf16[256,1024]{1,0:T(8,128)(2,1)S(1)}, bf16[256,1024]{1,0:T(8,128)(2,1)S(1)}, u32[]{:S(2)}, u32[]{:S(2)}) collective-permute-start(bf16[256,1024]{1,0:T(8,128)(2,1)S(1)} %copy-done.12), channel_id=1, source_target_pairs={{0,2},{1,3},{2,0},{3,1},{4,6},{5,7},{6,4},{7,5},{8,10},{9,11},{10,... | collective-permute-start | bytes 1572872 | tf_op jit(solution)/shard_map/ppermute | solution.py:712
  69.9 23.1 %collective-permute-start.23 = (bf16[256,1024]{1,0:T(8,128)(2,1)S(1)}, bf16[256,1024]{1,0:T(8,128)(2,1)S(1)}, u32[]{:S(2)}, u32[]{:S(2)}) collective-permute-start(bf16[256,1024]{1,0:T(8,128)(2,1)S(1)} %collective-permute-done.14.refs_10_.refs_4_), channel_id=1, source_target_pairs={{0,1},{1,0},{2,3},{3,2},{4,5},{5,4},{6,7},{7,6},{8,9},{9,8},{10,11... | collective-permute-start | bytes 1572872 | tf_op jit(solution)/shard_map/ppermute | solution.py:708
  70.0 24.6 %collective-permute-start.24 = (bf16[256,1024]{1,0:T(8,128)(2,1)S(1)}, bf16[256,1024]{1,0:T(8,128)(2,1)S(1)}, u32[]{:S(2)}, u32[]{:S(2)}) collective-permute-start(bf16[256,1024]{1,0:T(8,128)(2,1)S(1)} %copy-done.7), channel_id=1, source_target_pairs={{0,2},{1,3},{2,0},{3,1},{4,6},{5,7},{6,4},{7,5},{8,10},{9,11},{10,... | collective-permute-start | bytes 1572872 | tf_op jit(solution)/shard_map/ppermute | solution.py:712
  74.5 12.5 %collective-permute-start.18 = (bf16[256,128]{1,0:T(8,128)(2,1)S(1)}, bf16[256,128]{1,0:T(8,128)(2,1)S(1)}, u32[]{:S(2)}, u32[]{:S(2)}) collective-permute-start(bf16[256,128]{1,0:T(8,128)(2,1)S(1)} %get-tuple-element.341), channel_id=1, source_target_pairs={{4,16},{12,8},{20,0},{28,4},{24,12},{16,20},{8,28},{0,24},{5,17},{... | collective-permute-start | bytes 196616 | tf_op jit(solution)/shard_map/ppermute | solution.py:632
  95.1 13.9 %collective-permute-start.27 = (bf16[256,1024]{1,0:T(8,128)(2,1)S(1)}, bf16[256,1024]{1,0:T(8,128)(2,1)S(1)}, u32[]{:S(2)}, u32[]{:S(2)}) collective-permute-start(bf16[256,1024]{1,0:T(8,128)(2,1)S(1)} %get-tuple-element.352.refs_0_), channel_id=1, source_target_pairs={{0,2},{1,3},{2,0},{3,1},{4,6},{5,7},{6,4},{7,5},{8,10},{9,11},{10,... | collective-permute-start | bytes 1572872 | tf_op jit(solution)/shard_map/ppermute | solution.py:712
  95.3 14.2 %collective-permute-start.30 = (bf16[256,1024]{1,0:T(8,128)(2,1)S(1)}, bf16[256,1024]{1,0:T(8,128)(2,1)S(1)}, u32[]{:S(2)}, u32[]{:S(2)}) collective-permute-start(bf16[256,1024]{1,0:T(8,128)(2,1)S(1)} %collective-permute-done.24.refs_2_.refs_6_), channel_id=1, source_target_pairs={{0,1},{1,0},{2,3},{3,2},{4,5},{5,4},{6,7},{7,6},{8,9},{9,8},{10,11... | collective-permute-start | bytes 1572872 | tf_op jit(solution)/shard_map/ppermute | solution.py:708
  120.5 14.0 %collective-permute-start.37 = (bf16[256,1024]{1,0:T(8,128)(2,1)S(1)}, bf16[256,1024]{1,0:T(8,128)(2,1)S(1)}, u32[]{:S(2)}, u32[]{:S(2)}) collective-permute-start(bf16[256,1024]{1,0:T(8,128)(2,1)S(1)} %add_convert_fusion.9), channel_id=1, source_target_pairs={{0,2},{1,3},{2,0},{3,1},{4,6},{5,7},{6,4},{7,5},{8,10},{9,11},{10,... | collective-permute-start | bytes 1572872 | tf_op jit(solution)/shard_map/ppermute | solution.py:712
  141.2 12.0 %collective-permute-start.39 = (bf16[256,128]{1,0:T(8,128)(2,1)S(1)}, bf16[256,128]{1,0:T(8,128)(2,1)S(1)}, u32[]{:S(2)}, u32[]{:S(2)}) collective-permute-start(bf16[256,128]{1,0:T(8,128)(2,1)S(1)} %get-tuple-element.394), channel_id=1, source_target_pairs={{4,8},{12,0},{20,4},{28,12},{24,20},{16,28},{8,24},{0,16},{5,9},{1... | collective-permute-start | bytes 196616 | tf_op jit(solution)/shard_map/ppermute | solution.py:632
  142.2 12.2 %collective-permute-start.45 = (bf16[8,256,128]{2,1,0:T(8,128)(2,1)S(1)}, bf16[8,256,128]{2,1,0:T(8,128)(2,1)S(1)}, u32[]{:S(2)}, u32[]{:S(2)}) collective-permute-start(bf16[8,256,128]{2,1,0:T(8,128)(2,1)S(1)} %get-tuple-element.402), channel_id=1, source_target_pairs={{0,1},{1,0},{2,3},{3,2},{4,5},{5,4},{6,7},{7,6},{8,9},{9,8},{10,11... | collective-permute-start | bytes 1572872 | tf_op jit(solution)/shard_map/ppermute | solution.py:708
  147.5 13.5 %collective-permute-start.47 = (bf16[8,256,128]{2,1,0:T(8,128)(2,1)S(1)}, bf16[8,256,128]{2,1,0:T(8,128)(2,1)S(1)}, u32[]{:S(2)}, u32[]{:S(2)}) collective-permute-start(bf16[8,256,128]{2,1,0:T(8,128)(2,1)S(1)} %add_convert_fusion.7), channel_id=1, source_target_pairs={{0,2},{1,3},{2,0},{3,1},{4,6},{5,7},{6,4},{7,5},{8,10},{9,11},{10,... | collective-permute-start | bytes 1572872 | tf_op jit(solution)/shard_map/ppermute | solution.py:712
  149.1 12.9 %collective-permute-start.40 = (bf16[256,128]{1,0:T(8,128)(2,1)S(1)}, bf16[256,128]{1,0:T(8,128)(2,1)S(1)}, u32[]{:S(2)}, u32[]{:S(2)}) collective-permute-start(bf16[256,128]{1,0:T(8,128)(2,1)S(1)} %get-tuple-element.395), channel_id=1, source_target_pairs={{4,16},{12,8},{20,0},{28,4},{24,12},{16,20},{8,28},{0,24},{5,17},{... | collective-permute-start | bytes 196616 | tf_op jit(solution)/shard_map/ppermute | solution.py:632
  165.5 18.8 %collective-permute-start.50 = (bf16[128,3072]{1,0:T(8,128)(2,1)}, bf16[128,3072]{1,0:T(8,128)(2,1)}, u32[]{:S(2)}, u32[]{:S(2)}) collective-permute-start(bf16[128,3072]{1,0:T(8,128)(2,1)} %get-tuple-element.492.refs_0_), channel_id=1, source_target_pairs={{0,2},{1,3},{2,0},{3,1},{4,6},{5,7},{6,4},{7,5},{8,10},{9,11},{10,... | collective-permute-start | bytes 2359304 | tf_op jit(solution)/shard_map/ppermute | solution.py:712
  165.8 18.5 %collective-permute-start.48 = (bf16[192,1408]{1,0:T(8,128)(2,1)S(1)}, bf16[192,1408]{1,0:T(8,128)(2,1)S(1)}, u32[]{:S(2)}, u32[]{:S(2)}) collective-permute-start(bf16[192,1408]{1,0:T(8,128)(2,1)S(1)} %add_convert_fusion.5), channel_id=1, source_target_pairs={{4,12},{12,20},{20,28},{28,24},{24,16},{16,8},{8,0},{0,4},{5,13},{... | collective-permute-start | bytes 1622024 | tf_op jit(solution)/shard_map/ppermute | solution.py:632
  166.6 17.7 %collective-permute-start.49 = (bf16[192,1408]{1,0:T(8,128)(2,1)S(1)}, bf16[192,1408]{1,0:T(8,128)(2,1)S(1)}, u32[]{:S(2)}, u32[]{:S(2)}) collective-permute-start(bf16[192,1408]{1,0:T(8,128)(2,1)S(1)} %add_convert_fusion.4), channel_id=1, source_target_pairs={{4,0},{12,4},{20,12},{28,20},{24,28},{16,24},{8,16},{0,8},{5,1},{1... | collective-permute-start | bytes 1622024 | tf_op jit(solution)/shard_map/ppermute | solution.py:632
  184.5 15.2 %collective-permute-start.51 = (bf16[192,1408]{1,0:T(8,128)(2,1)S(1)}, bf16[192,1408]{1,0:T(8,128)(2,1)S(1)}, u32[]{:S(2)}, u32[]{:S(2)}) collective-permute-start(bf16[192,1408]{1,0:T(8,128)(2,1)S(1)} %add_convert_fusion.3), channel_id=1, source_target_pairs={{4,12},{12,20},{20,28},{28,24},{24,16},{16,8},{8,0},{0,4},{5,13},{... | collective-permute-start | bytes 1622024 | tf_op jit(solution)/shard_map/ppermute | solution.py:632
  185.4 14.4 %collective-permute-start.52 = (bf16[192,1408]{1,0:T(8,128)(2,1)S(1)}, bf16[192,1408]{1,0:T(8,128)(2,1)S(1)}, u32[]{:S(2)}, u32[]{:S(2)}) collective-permute-start(bf16[192,1408]{1,0:T(8,128)(2,1)S(1)} %add_convert_fusion.2), channel_id=1, source_target_pairs={{4,0},{12,4},{20,12},{28,20},{24,28},{16,24},{8,16},{0,8},{5,1},{1... | collective-permute-start | bytes 1622024 | tf_op jit(solution)/shard_map/ppermute | solution.py:632
  186.6 30.3 %collective-permute-start.58 = (bf16[128,3072]{1,0:T(8,128)(2,1)}, bf16[128,3072]{1,0:T(8,128)(2,1)}, u32[]{:S(2)}, u32[]{:S(2)}) collective-permute-start(bf16[128,3072]{1,0:T(8,128)(2,1)} %get-tuple-element.493.refs_1_), channel_id=1, source_target_pairs={{0,2},{1,3},{2,0},{3,1},{4,6},{5,7},{6,4},{7,5},{8,10},{9,11},{10,... | collective-permute-start | bytes 2359304 | tf_op jit(solution)/shard_map/ppermute | solution.py:712
  200.3 14.6 %collective-permute-start.53 = (bf16[192,1408]{1,0:T(8,128)(2,1)S(1)}, bf16[192,1408]{1,0:T(8,128)(2,1)S(1)}, u32[]{:S(2)}, u32[]{:S(2)}) collective-permute-start(bf16[192,1408]{1,0:T(8,128)(2,1)S(1)} %get-tuple-element.465), channel_id=1, source_target_pairs={{4,12},{12,20},{20,28},{28,24},{24,16},{16,8},{8,0},{0,4},{5,13},{... | collective-permute-start | bytes 1622024 | tf_op jit(solution)/shard_map/ppermute | solution.py:632
  201.8 14.3 %collective-permute-start.54 = (bf16[192,1408]{1,0:T(8,128)(2,1)S(1)}, bf16[192,1408]{1,0:T(8,128)(2,1)S(1)}, u32[]{:S(2)}, u32[]{:S(2)}) collective-permute-start(bf16[192,1408]{1,0:T(8,128)(2,1)S(1)} %get-tuple-element.466), channel_id=1, source_target_pairs={{4,0},{12,4},{20,12},{28,20},{24,28},{16,24},{8,16},{0,8},{5,1},{1... | collective-permute-start | bytes 1622024 | tf_op jit(solution)/shard_map/ppermute | solution.py:632
  202.4 14.5 %collective-permute-start.57 = (bf16[256,384]{1,0:T(8,128)(2,1)S(1)}, bf16[256,384]{1,0:T(8,128)(2,1)S(1)}, u32[]{:S(2)}, u32[]{:S(2)}) collective-permute-start(bf16[256,384]{1,0:T(8,128)(2,1)S(1)} %add_convert_fusion.14), channel_id=1, source_target_pairs={{0,2},{1,3},{2,0},{3,1},{4,6},{5,7},{6,4},{7,5},{8,10},{9,11},{10,... | collective-permute-start | bytes 589832 | tf_op jit(solution)/shard_map/ppermute | solution.py:712
  217.6 53.8 %all-to-all-start = ((bf16[8,256,512]{2,1,0:T(8,128)(2,1)}), bf16[8,256,512]{2,1,0:T(8,128)(2,1)S(1)}, u32[]{:S(2)}, u32[]{:S(2)}) async-start(bf16[8,256,512]{2,1,0:T(8,128)(2,1)} %attention_backward.1.refs_9_), calls=%async_computation | async-start | bytes 4194304 | tf_op jit(solution)/shard_map/all_to_all | solution.py:704
  233.0 27.0 %collective-permute-start.62 = (bf16[192,1408]{1,0:T(8,128)(2,1)S(1)}, bf16[192,1408]{1,0:T(8,128)(2,1)S(1)}, u32[]{:S(2)}, u32[]{:S(2)}) collective-permute-start(bf16[192,1408]{1,0:T(8,128)(2,1)S(1)} %pack.1.refs_0_), channel_id=1, source_target_pairs={{4,12},{12,20},{20,28},{28,24},{24,16},{16,8},{8,0},{0,4},{5,13},{... | collective-permute-start | bytes 1622024 | tf_op jit(solution)/shard_map/ppermute | solution.py:632
  235.1 39.4 %collective-permute-start.66 = (bf16[128,3072]{1,0:T(8,128)(2,1)}, bf16[128,3072]{1,0:T(8,128)(2,1)}, u32[]{:S(2)}, u32[]{:S(2)}) collective-permute-start(bf16[128,3072]{1,0:T(8,128)(2,1)} %get-tuple-element.492.refs_0_), channel_id=1, source_target_pairs={{0,1},{1,0},{2,3},{3,2},{4,5},{5,4},{6,7},{7,6},{8,9},{9,8},{10,11... | collective-permute-start | bytes 2359304 | tf_op jit(solution)/shard_map/ppermute | solution.py:708
  235.4 31.6 %collective-permute-start.63 = (bf16[192,1408]{1,0:T(8,128)(2,1)S(1)}, bf16[192,1408]{1,0:T(8,128)(2,1)}, u32[]{:S(2)}, u32[]{:S(2)}) collective-permute-start(bf16[192,1408]{1,0:T(8,128)(2,1)S(1)} %pack.1.refs_0_), channel_id=1, source_target_pairs={{4,0},{12,4},{20,12},{28,20},{24,28},{16,24},{8,16},{0,8},{5,1},{1... | collective-permute-start | bytes 1622024 | tf_op jit(solution)/shard_map/ppermute | solution.py:632
  236.6 48.4 %collective-permute-start.68 = (bf16[128,3072]{1,0:T(8,128)(2,1)}, bf16[128,3072]{1,0:T(8,128)(2,1)}, u32[]{:S(2)}, u32[]{:S(2)}) collective-permute-start(bf16[128,3072]{1,0:T(8,128)(2,1)} %collective-permute-done.50.refs_4_), channel_id=1, source_target_pairs={{0,1},{1,0},{2,3},{3,2},{4,5},{5,4},{6,7},{7,6},{8,9},{9,8},{10,11... | collective-permute-start | bytes 2359304 | tf_op jit(solution)/shard_map/ppermute | solution.py:708
  236.6 57.6 %collective-permute-start.67 = (bf16[128,3072]{1,0:T(8,128)(2,1)}, bf16[128,3072]{1,0:T(8,128)(2,1)}, u32[]{:S(2)}, u32[]{:S(2)}) collective-permute-start(bf16[128,3072]{1,0:T(8,128)(2,1)} %get-tuple-element.493.refs_1_), channel_id=1, source_target_pairs={{0,1},{1,0},{2,3},{3,2},{4,5},{5,4},{6,7},{7,6},{8,9},{9,8},{10,11... | collective-permute-start | bytes 2359304 | tf_op jit(solution)/shard_map/ppermute | solution.py:708
  260.1 34.2 %collective-permute-start.69 = (bf16[128,3072]{1,0:T(8,128)(2,1)}, bf16[128,3072]{1,0:T(8,128)(2,1)}, u32[]{:S(2)}, u32[]{:S(2)}) collective-permute-start(bf16[128,3072]{1,0:T(8,128)(2,1)} %collective-permute-done.58.refs_5_), channel_id=1, source_target_pairs={{0,1},{1,0},{2,3},{3,2},{4,5},{5,4},{6,7},{7,6},{8,9},{9,8},{10,11... | collective-permute-start | bytes 2359304 | tf_op jit(solution)/shard_map/ppermute | solution.py:708
  274.0 18.2 %collective-permute-start.74 = (bf16[256,512]{1,0:T(8,128)(2,1)S(1)}, bf16[256,512]{1,0:T(8,128)(2,1)S(1)}, u32[]{:S(2)}, u32[]{:S(2)}) collective-permute-start(bf16[256,512]{1,0:T(8,128)(2,1)S(1)} %join.1.refs_9_), channel_id=1, source_target_pairs={{4,12},{12,20},{20,28},{28,24},{24,16},{16,8},{8,0},{0,4},{5,13},{... | collective-permute-start | bytes 786440 | tf_op jit(solution)/shard_map/ppermute | solution.py:632
  274.5 19.7 %collective-permute-start.75 = (bf16[256,512]{1,0:T(8,128)(2,1)S(1)}, bf16[256,512]{1,0:T(8,128)(2,1)S(1)}, u32[]{:S(2)}, u32[]{:S(2)}) collective-permute-start(bf16[256,512]{1,0:T(8,128)(2,1)S(1)} %join.1.refs_9_), channel_id=1, source_target_pairs={{4,0},{12,4},{20,12},{28,20},{24,28},{16,24},{8,16},{0,8},{5,1},{1... | collective-permute-start | bytes 786440 | tf_op jit(solution)/shard_map/ppermute | solution.py:632
  285.1 25.4 %collective-permute-start.64 = (bf16[192,1408]{1,0:T(8,128)(2,1)S(1)}, bf16[192,1408]{1,0:T(8,128)(2,1)S(1)}, u32[]{:S(2)}, u32[]{:S(2)}) collective-permute-start(bf16[192,1408]{1,0:T(8,128)(2,1)S(1)} %copy-done.17), channel_id=1, source_target_pairs={{4,12},{12,20},{20,28},{28,24},{24,16},{16,8},{8,0},{0,4},{5,13},{... | collective-permute-start | bytes 1622024 | tf_op jit(solution)/shard_map/ppermute | solution.py:632
  292.2 18.4 %collective-permute-start.65 = (bf16[192,1408]{1,0:T(8,128)(2,1)}, bf16[192,1408]{1,0:T(8,128)(2,1)S(1)}, u32[]{:S(2)}, u32[]{:S(2)}) collective-permute-start(bf16[192,1408]{1,0:T(8,128)(2,1)} %collective-permute-done.63.refs_1_), channel_id=1, source_target_pairs={{4,0},{12,4},{20,12},{28,20},{24,28},{16,24},{8,16},{0,8},{5,1},{1... | collective-permute-start | bytes 1622024 | tf_op jit(solution)/shard_map/ppermute | solution.py:632
  294.2 18.6 %collective-permute-start.31 = (bf16[256,1024]{1,0:T(8,128)(2,1)S(1)}, bf16[256,1024]{1,0:T(8,128)(2,1)S(1)}, u32[]{:S(2)}, u32[]{:S(2)}) collective-permute-start(bf16[256,1024]{1,0:T(8,128)(2,1)S(1)} %copy-done.35), channel_id=1, source_target_pairs={{0,1},{1,0},{2,3},{3,2},{4,5},{5,4},{6,7},{7,6},{8,9},{9,8},{10,11... | collective-permute-start | bytes 1572872 | tf_op jit(solution)/shard_map/ppermute | solution.py:708
  294.2 14.1 %collective-permute-start.76 = (bf16[256,512]{1,0:T(8,128)(2,1)S(1)}, bf16[256,512]{1,0:T(8,128)(2,1)S(1)}, u32[]{:S(2)}, u32[]{:S(2)}) collective-permute-start(bf16[256,512]{1,0:T(8,128)(2,1)S(1)} %collective-permute-done.74.refs_17_), channel_id=1, source_target_pairs={{4,12},{12,20},{20,28},{28,24},{24,16},{16,8},{8,0},{0,4},{5,13},{... | collective-permute-start | bytes 786440 | tf_op jit(solution)/shard_map/ppermute | solution.py:632
  294.3 15.9 %collective-permute-start.77 = (bf16[256,512]{1,0:T(8,128)(2,1)S(1)}, bf16[256,512]{1,0:T(8,128)(2,1)S(1)}, u32[]{:S(2)}, u32[]{:S(2)}) collective-permute-start(bf16[256,512]{1,0:T(8,128)(2,1)S(1)} %collective-permute-done.75.refs_10_), channel_id=1, source_target_pairs={{4,0},{12,4},{20,12},{28,20},{24,28},{16,24},{8,16},{0,8},{5,1},{1... | collective-permute-start | bytes 786440 | tf_op jit(solution)/shard_map/ppermute | solution.py:632
  308.3 26.4 %collective-permute-start.28 = (bf16[256,1024]{1,0:T(8,128)(2,1)S(1)}, bf16[256,1024]{1,0:T(8,128)(2,1)S(1)}, u32[]{:S(2)}, u32[]{:S(2)}) collective-permute-start(bf16[256,1024]{1,0:T(8,128)(2,1)S(1)} %copy-done.33), channel_id=1, source_target_pairs={{0,1},{1,0},{2,3},{3,2},{4,5},{5,4},{6,7},{7,6},{8,9},{9,8},{10,11... | collective-permute-start | bytes 1572872 | tf_op jit(solution)/shard_map/ppermute | solution.py:708
  310.5 22.0 %collective-permute-start.70 = (bf16[192,1408]{1,0:T(8,128)(2,1)S(1)}, bf16[192,1408]{1,0:T(8,128)(2,1)S(1)}, u32[]{:S(2)}, u32[]{:S(2)}) collective-permute-start(bf16[192,1408]{1,0:T(8,128)(2,1)S(1)} %collective-permute-done.64.refs_7_), channel_id=1, source_target_pairs={{4,12},{12,20},{20,28},{28,24},{24,16},{16,8},{8,0},{0,4},{5,13},{... | collective-permute-start | bytes 1622024 | tf_op jit(solution)/shard_map/ppermute | solution.py:632
  312.8 20.0 %collective-permute-start.71 = (bf16[192,1408]{1,0:T(8,128)(2,1)S(1)}, bf16[192,1408]{1,0:T(8,128)(2,1)S(1)}, u32[]{:S(2)}, u32[]{:S(2)}) collective-permute-start(bf16[192,1408]{1,0:T(8,128)(2,1)S(1)} %collective-permute-done.65.refs_2_), channel_id=1, source_target_pairs={{4,0},{12,4},{20,12},{28,20},{24,28},{16,24},{8,16},{0,8},{5,1},{1... | collective-permute-start | bytes 1622024 | tf_op jit(solution)/shard_map/ppermute | solution.py:632
  313.0 22.2 %collective-permute-start.32 = (bf16[256,1024]{1,0:T(8,128)(2,1)S(1)}, bf16[256,1024]{1,0:T(8,128)(2,1)S(1)}, u32[]{:S(2)}, u32[]{:S(2)}) collective-permute-start(bf16[256,1024]{1,0:T(8,128)(2,1)S(1)} %add_convert_fusion.12), channel_id=1, source_target_pairs={{0,2},{1,3},{2,0},{3,1},{4,6},{5,7},{6,4},{7,5},{8,10},{9,11},{10,... | collective-permute-start | bytes 1572872 | tf_op jit(solution)/shard_map/ppermute | solution.py:712
  (71 other events, 564.3 us)
